TPU v7x, 32 devices: a whole 2x2x4 slice. The times are simulated.
32 devices in a mesh: fsdp: 8 (over y, x, core), tensor: 4 (over z).
Axes of the slice: x: 2, y: 2, z: 4, core: 2. Of those that a mesh axis runs over, the one named last changes fastest.
Arguments:
- layer_input: bfloat16 [1, 4096, 1024], P(None, ('fsdp', 'tensor')), may hold values from -6 to 6
- out_grad: bfloat16 [1, 4096, 1024], P(None, ('fsdp', 'tensor')), may hold values from -6 to 6
- segments: int32 [1, 32, 128], P(None, 'fsdp'), may hold values from 0 to 3, as said below
- positions: int32 [1, 32, 128], P(None, 'fsdp'), may hold values from 0 to 2047, as said below
- qkv_weight: bfloat16 [1024, 3072], P('fsdp', 'tensor')
- qkv_bias: bfloat16 [16, 192], P('tensor', 'fsdp'), may hold values from -3 to 3
- dense_weight: bfloat16 [1024, 1024], P('tensor', 'fsdp'), may hold values from -1 to 1
- dense_bias: float32 [1024], P(('fsdp', 'tensor')), may hold values from -3 to 3
- inner_weight: bfloat16 [1024, 4096], P('fsdp', 'tensor'), may hold values from -0.1875 to 0.1875
- inner_bias: bfloat16 [16, 256], P('tensor', 'fsdp'), may hold values from -3 to 3
- outer_weight: bfloat16 [4096, 1024], P('tensor', 'fsdp'), may hold values from -0.09375 to 0.09375
- outer_bias: float32 [1024], P(('fsdp', 'tensor')), may hold values from -3 to 3
- attention_norm_gain: float32 [1024], P(('fsdp', 'tensor')), may hold values from 0.1 to 1.9
- attention_norm_bias: float32 [1024], P(('fsdp', 'tensor')), may hold values from -3 to 3
- feedforward_norm_gain: float32 [1024], P(('fsdp', 'tensor')), may hold values from 0.1 to 1.9
- feedforward_norm_bias: float32 [1024], P(('fsdp', 'tensor')), may hold values from -3 to 3
Outputs:
- layer_out: bfloat16 [1, 4096, 1024], P(None, ('fsdp', 'tensor'))
- in_grad: bfloat16 [1, 4096, 1024], P(None, ('fsdp', 'tensor'))
- qkv_weight_grad: float32 [1024, 3072], P('fsdp', 'tensor')
- qkv_bias_grad: float32 [16, 192], P('tensor', 'fsdp')
- dense_weight_grad: float32 [1024, 1024], P('tensor', 'fsdp')
- dense_bias_grad: float32 [1024], P(('fsdp', 'tensor'))
- inner_weight_grad: float32 [1024, 4096], P('fsdp', 'tensor')
- inner_bias_grad: float32 [16, 256], P('tensor', 'fsdp')
- outer_weight_grad: float32 [4096, 1024], P('tensor', 'fsdp')
- outer_bias_grad: float32 [1024], P(('fsdp', 'tensor'))
- norm1_gain_grad: float32 [1024], P(('fsdp', 'tensor'))
- norm1_shift_grad: float32 [1024], P(('fsdp', 'tensor'))
- norm2_gain_grad: float32 [1024], P(('fsdp', 'tensor'))
- norm2_shift_grad: float32 [1024], P(('fsdp', 'tensor'))
Inputs may be any that keep to these rules, and one draw needn't show every extreme that they name: `segments`: each sequence of 128 tokens holds exactly 4 documents, numbered from 0 in order and never falling, each of one token or more. Within a document positions rise by one or two from token to token; every document but the first of a sequence starts at 0.
All inputs are finite; a program needn't handle non-finite values.
Results may differ from a plain program's by a relative error of at most 0.015.
Values may be sent and summed in bfloat16 or wider, within the bound.
No kernel may reach another device: no remote copies, remote signals or barrier semaphores. Data moves between devices by JAX's collectives and lax.ppermute only.
A program may use at most 128 MiB of HBM per device.

v0:
```python
import jax
import jax.numpy as jnp
from jax import lax
from jax.sharding import PartitionSpec as P

H = 16
HD = 64
ROT = 16
FF = 4096


EPS = 1e-05
ROOT_HALF = 0.7071067811865476
INV_ROOT_TAU = 0.3989422804014327
MASKED = -1e30


def normalize_rows(token_row_block):
    values = token_row_block.astype(jnp.float32)
    centre = values - jnp.mean(values, -1, keepdims=True)
    scale = lax.rsqrt(jnp.mean(centre * centre, -1, keepdims=True) + EPS)
    return (centre * scale, scale)


def gelu_value(pre):
    return 0.5 * pre * (1.0 + lax.erf(pre * ROOT_HALF))


def gelu_slope(pre):
    return 0.5 * (1.0 + lax.erf(pre * ROOT_HALF)) + pre * jnp.exp(-0.5 * pre * pre) * INV_ROOT_TAU


def angle_tables(positions):
    half = ROT // 2
    freq = jnp.power(10000.0, -jnp.arange(half, dtype=jnp.float32) * (2.0 / ROT))
    angle = positions.astype(jnp.float32)[..., None] * freq
    cosine = jnp.cos(angle)
    sine = jnp.sin(angle)
    return (
        jnp.concatenate([cosine, cosine], -1)[:, :, None, :],
        jnp.concatenate([sine, sine], -1)[:, :, None, :],
    )


def turn(vec, cosine, sine):
    half = ROT // 2
    head = vec[..., :ROT]
    swapped = jnp.concatenate([-head[..., half:], head[..., :half]], -1)
    return jnp.concatenate([head * cosine + swapped * sine, vec[..., ROT:]], -1)


def turn_back(grad, cosine, sine):
    half = ROT // 2
    head = grad[..., :ROT]
    scaled = head * sine
    back = jnp.concatenate([scaled[..., half:], -scaled[..., :half]], -1)
    return jnp.concatenate([head * cosine + back, grad[..., ROT:]], -1)


def attention_mask(segs):
    index = jnp.arange(segs.shape[-1])
    causal = index[None, :, None] >= index[None, None, :]
    return (segs[:, :, None] == segs[:, None, :]) & causal


def matmul(left, right, left_dim, right_dim):
    return lax.dot_general(
        left, right, (((left_dim,), (right_dim,)), ((), ())), preferred_element_type=jnp.float32
    )


def unpack(gathered):
    qkv_w, qkv_b, dense_w, inner_w, inner_b, outer_w = gathered
    return (
        qkv_w,
        qkv_b.reshape(-1).astype(jnp.float32),
        dense_w,
        inner_w,
        inner_b.reshape(-1).astype(jnp.float32),
        outer_w,
    )


def raw_scores(query, keyed, mask, scale):
    product = jnp.einsum("sqhd,skhd->shqk", query, keyed, preferred_element_type=jnp.float32)
    return jnp.where(mask, product * scale, MASKED)


def shards(
    layer_input,
    out_grad,
    segments,
    positions,
    qkv_weight,
    qkv_bias,
    dense_weight,
    dense_bias,
    inner_weight,
    inner_bias,
    outer_weight,
    outer_bias,
    attention_norm_gain,
    attention_norm_bias,
    feedforward_norm_gain,
    feedforward_norm_bias,
):
    attention_gain, attention_bias, feedforward_gain, feedforward_bias, bias_dense, bias_outer = (
        lax.all_gather(attention_norm_gain, ("fsdp", "tensor"), axis=0, tiled=True),
        lax.all_gather(attention_norm_bias, ("fsdp", "tensor"), axis=0, tiled=True),
        lax.all_gather(feedforward_norm_gain, ("fsdp", "tensor"), axis=0, tiled=True),
        lax.all_gather(feedforward_norm_bias, ("fsdp", "tensor"), axis=0, tiled=True),
        lax.all_gather(dense_bias, ("fsdp", "tensor"), axis=0, tiled=True),
        lax.all_gather(outer_bias, ("fsdp", "tensor"), axis=0, tiled=True),
    )
    scale = HD ** (-0.5)
    microbatch = 0
    weights = unpack(
        (
            lax.all_gather(qkv_weight, "fsdp", axis=0, tiled=True),
            lax.all_gather(qkv_bias, "fsdp", axis=1, tiled=True),
            lax.all_gather(dense_weight, "fsdp", axis=1, tiled=True),
            lax.all_gather(inner_weight, "fsdp", axis=0, tiled=True),
            lax.all_gather(inner_bias, "fsdp", axis=1, tiled=True),
            lax.all_gather(outer_weight, "fsdp", axis=1, tiled=True),
        )
    )
    qkv_w, qkv_b, dense_w, inner_w, inner_b, outer_w = weights
    token_row_block = lax.all_gather(layer_input[microbatch], "tensor", axis=0, tiled=True)
    segs = segments[microbatch]
    seqs, length = segs.shape
    heads = qkv_w.shape[1] // (3 * HD)
    normalized_input, unused_result = normalize_rows(token_row_block)
    first_branch = (normalized_input * attention_gain + attention_bias).astype(jnp.bfloat16)
    second_branch = (normalized_input * feedforward_gain + feedforward_bias).astype(jnp.bfloat16)
    packed = (jnp.dot(first_branch, qkv_w, preferred_element_type=jnp.float32) + qkv_b).reshape(
        seqs, length, heads, 3, HD
    )
    cosine, sine = angle_tables(positions[microbatch])
    query = turn(packed[:, :, :, 0], cosine, sine).astype(jnp.bfloat16)
    keyed = turn(packed[:, :, :, 1], cosine, sine).astype(jnp.bfloat16)
    value = packed[:, :, :, 2].astype(jnp.bfloat16)
    mask = attention_mask(segs)[:, None]
    scores = raw_scores(query, keyed, mask, scale)
    peak = jnp.max(scores, -1, keepdims=True)
    log_total = peak + jnp.log(jnp.sum(jnp.exp(scores - peak), -1, keepdims=True))
    probs_b = jnp.exp(scores - log_total).astype(jnp.bfloat16)
    context = jnp.einsum(
        "shqk,skhd->sqhd", probs_b, value, preferred_element_type=jnp.float32
    ).astype(jnp.bfloat16)
    flat_ctx = context.reshape(seqs * length, heads * HD)
    pre = jnp.dot(second_branch, inner_w, preferred_element_type=jnp.float32) + inner_b
    act = gelu_value(pre).astype(jnp.bfloat16)
    ctx_rows = flat_ctx
    act_rows = act
    mixed = lax.psum_scatter(
        (
            jnp.dot(ctx_rows, dense_w, preferred_element_type=jnp.float32)
            + jnp.dot(act_rows, outer_w, preferred_element_type=jnp.float32)
        ).astype(jnp.bfloat16),
        "tensor",
        scatter_dimension=0,
        tiled=True,
    ).astype(jnp.float32)
    outputs = [
        (layer_input[microbatch].astype(jnp.float32) + mixed + bias_dense + bias_outer).astype(
            jnp.bfloat16
        )
    ]
    saved = [
        (
            token_row_block,
            first_branch,
            second_branch,
            query,
            keyed,
            value,
            log_total,
            context,
            flat_ctx,
            pre,
            act,
        )
    ]
    g_qkv_b = jnp.zeros((qkv_bias.shape[0], 3 * HD), jnp.float32)
    g_inner_b = jnp.zeros((inner_bias.shape[0], FF // H), jnp.float32)
    microbatch = 0
    weights = unpack(
        (
            lax.all_gather(qkv_weight, "fsdp", axis=0, tiled=True),
            lax.all_gather(qkv_bias, "fsdp", axis=1, tiled=True),
            lax.all_gather(dense_weight, "fsdp", axis=1, tiled=True),
            lax.all_gather(inner_weight, "fsdp", axis=0, tiled=True),
            lax.all_gather(inner_bias, "fsdp", axis=1, tiled=True),
            lax.all_gather(outer_weight, "fsdp", axis=1, tiled=True),
        )
    )
    qkv_w, qkv_b, dense_w, inner_w, inner_b, outer_w = weights
    (
        token_row_block,
        first_branch,
        second_branch,
        query,
        keyed,
        value,
        log_total,
        context,
        flat_ctx,
        pre,
        act,
    ) = saved[microbatch]
    segs = segments[microbatch]
    seqs, length = segs.shape
    heads = qkv_w.shape[1] // (3 * HD)
    cot_rows = lax.all_gather(out_grad[microbatch], "tensor", axis=0, tiled=True)
    own_cot = out_grad[microbatch].astype(jnp.float32)
    g_bias = jnp.sum(own_cot, 0)
    d_act = matmul(cot_rows, outer_w, 1, 1)
    g_outer = matmul(act, cot_rows, 0, 0)
    d_pre = d_act * gelu_slope(pre)
    g_inner_b = jnp.sum(d_pre, 0).reshape(g_inner_b.shape)
    d_pre_b = d_pre.astype(jnp.bfloat16)
    g_inner = matmul(second_branch, d_pre_b, 0, 0)
    second_branch_gradient = matmul(d_pre_b, inner_w, 1, 1)
    d_ctx = matmul(cot_rows, dense_w, 1, 1).astype(jnp.bfloat16)
    g_dense = matmul(flat_ctx, cot_rows, 0, 0)
    d_ctx4 = d_ctx.reshape(context.shape)
    delta = jnp.sum(d_ctx4.astype(jnp.float32) * context.astype(jnp.float32), -1)
    mask = attention_mask(segs)[:, None]
    probs = jnp.exp(raw_scores(query, keyed, mask, scale) - log_total)
    d_probs = jnp.einsum("sqhd,skhd->shqk", d_ctx4, value, preferred_element_type=jnp.float32)
    d_scores = probs * (d_probs - jnp.transpose(delta, (0, 2, 1))[..., None])
    d_value = jnp.einsum(
        "shqk,sqhd->skhd", probs.astype(jnp.bfloat16), d_ctx4, preferred_element_type=jnp.float32
    )
    d_scores_b = d_scores.astype(jnp.bfloat16)
    d_query = (
        jnp.einsum("shqk,skhd->sqhd", d_scores_b, keyed, preferred_element_type=jnp.float32) * scale
    )
    d_key = (
        jnp.einsum("shqk,sqhd->skhd", d_scores_b, query, preferred_element_type=jnp.float32) * scale
    )
    cosine, sine = angle_tables(positions[microbatch])
    d_packed = jnp.stack(
        [turn_back(d_query, cosine, sine), turn_back(d_key, cosine, sine), d_value], 3
    )
    d_packed = d_packed.reshape(seqs * length, heads * 3 * HD)
    g_qkv_b = jnp.sum(d_packed, 0).reshape(g_qkv_b.shape)
    d_packed_b = d_packed.astype(jnp.bfloat16)
    g_qkv = matmul(first_branch, d_packed_b, 0, 0)
    first_branch_gradient = matmul(d_packed_b, qkv_w, 1, 1)
    local_normalized_input, local_inverse_deviation = normalize_rows(layer_input[microbatch])
    local_first_branch = lax.psum_scatter(
        first_branch_gradient.astype(jnp.bfloat16), "tensor", scatter_dimension=0, tiled=True
    ).astype(jnp.float32)
    local_second_branch = lax.psum_scatter(
        second_branch_gradient.astype(jnp.bfloat16), "tensor", scatter_dimension=0, tiled=True
    ).astype(jnp.float32)
    attention_gain_gradient = jnp.sum(local_first_branch * local_normalized_input, 0)
    g_shift1 = jnp.sum(local_first_branch, 0)
    feedforward_gain_gradient = jnp.sum(local_second_branch * local_normalized_input, 0)
    g_shift2 = jnp.sum(local_second_branch, 0)
    normalized_gradient = (
        local_first_branch * attention_gain + local_second_branch * feedforward_gain
    )
    input_gradient = own_cot + local_inverse_deviation * (
        normalized_gradient
        - jnp.mean(normalized_gradient, -1, keepdims=True)
        - local_normalized_input
        * jnp.mean(normalized_gradient * local_normalized_input, -1, keepdims=True)
    )
    in_grads = [input_gradient.astype(jnp.bfloat16)]
    s_qkv, s_qkv_b, s_dense, s_inner, s_inner_b, s_outer = (
        lax.psum_scatter(
            g_qkv.astype(jnp.bfloat16), "fsdp", scatter_dimension=0, tiled=True
        ).astype(jnp.float32),
        lax.psum_scatter(
            g_qkv_b.astype(jnp.bfloat16), "fsdp", scatter_dimension=1, tiled=True
        ).astype(jnp.float32),
        lax.psum_scatter(
            g_dense.astype(jnp.bfloat16), "fsdp", scatter_dimension=1, tiled=True
        ).astype(jnp.float32),
        lax.psum_scatter(
            g_inner.astype(jnp.bfloat16), "fsdp", scatter_dimension=0, tiled=True
        ).astype(jnp.float32),
        lax.psum_scatter(
            g_inner_b.astype(jnp.bfloat16), "fsdp", scatter_dimension=1, tiled=True
        ).astype(jnp.float32),
        lax.psum_scatter(
            g_outer.astype(jnp.bfloat16), "fsdp", scatter_dimension=1, tiled=True
        ).astype(jnp.float32),
    )
    s_bias, s_gain1, s_shift1, s_gain2, s_shift2 = (
        lax.psum_scatter(g_bias, ("fsdp", "tensor"), scatter_dimension=0, tiled=True),
        lax.psum_scatter(
            attention_gain_gradient, ("fsdp", "tensor"), scatter_dimension=0, tiled=True
        ),
        lax.psum_scatter(g_shift1, ("fsdp", "tensor"), scatter_dimension=0, tiled=True),
        lax.psum_scatter(
            feedforward_gain_gradient, ("fsdp", "tensor"), scatter_dimension=0, tiled=True
        ),
        lax.psum_scatter(g_shift2, ("fsdp", "tensor"), scatter_dimension=0, tiled=True),
    )
    return (
        jnp.stack(outputs),
        jnp.stack(in_grads),
        s_qkv,
        s_qkv_b,
        s_dense,
        s_bias,
        s_inner,
        s_inner_b,
        s_outer,
        s_bias,
        s_gain1,
        s_shift1,
        s_gain2,
        s_shift2,
    )


def solution(mesh):
    placed = (
        P(None, ("fsdp", "tensor"), None),
        P(None, ("fsdp", "tensor"), None),
        P(None, "fsdp", None),
        P(None, "fsdp", None),
        P("fsdp", "tensor"),
        P("tensor", "fsdp"),
        P("tensor", "fsdp"),
        P(("fsdp", "tensor")),
        P("fsdp", "tensor"),
        P("tensor", "fsdp"),
        P("tensor", "fsdp"),
        P(("fsdp", "tensor")),
        P(("fsdp", "tensor")),
        P(("fsdp", "tensor")),
        P(("fsdp", "tensor")),
        P(("fsdp", "tensor")),
    )
    return jax.shard_map(
        shards,
        mesh=mesh,
        in_specs=placed,
        out_specs=(
            P(None, ("fsdp", "tensor"), None),
            P(None, ("fsdp", "tensor"), None),
            P("fsdp", "tensor"),
            P("tensor", "fsdp"),
            P("tensor", "fsdp"),
            P(("fsdp", "tensor")),
            P("fsdp", "tensor"),
            P("tensor", "fsdp"),
            P("tensor", "fsdp"),
            P(("fsdp", "tensor")),
            P(("fsdp", "tensor")),
            P(("fsdp", "tensor")),
            P(("fsdp", "tensor")),
            P(("fsdp", "tensor")),
        ),
        check_vma=False,
    )
```

profile of v0, /device:TPU:0, one launch (start us, length us, event | category | flops | bytes accessed | tf_op | source)
XLA Modules:
  0.0 455.6 jit_solution(6523221713986140903)
XLA Ops:
  7.2 0.7 all-gather.16.cloned.1.call-update
  8.0 0.7 all-gather.18.cloned.1.call-update
  8.7 0.7 all-gather.10.cloned.1.call-update
  9.5 0.5 all-gather.12.cloned.1.call-update
  10.0 0.5 all-gather.14.cloned.1.call-update
  10.7 0.7 convert_bitcast_fusion.3
  11.4 10.5 %all-gather.2 = bf16[8,24,4]{1,2,0:T(4,128)(2,1)S(1)} all-gather(bf16[1,24,4]{1,2,0:T(4,128)(2,1)} %bitcast.204), channel_id=1, replica_groups=mesh['fsdp'=8,'tensor'=4] {'fsdp'}, dimensions={0}, use_global_device_ids=true | all-gather | bytes 1728 | tf_op jit(solution)/shard_map/all_gather | solution.py:120
  22.1 8.8 %all-gather.3 = bf16[8,32,4]{1,2,0:T(4,128)(2,1)S(1)} all-gather(bf16[1,32,4]{1,2,0:T(4,128)(2,1)} %bitcast.205), channel_id=1, replica_groups=mesh['fsdp'=8,'tensor'=4] {'fsdp'}, dimensions={0}, use_global_device_ids=true | all-gather | bytes 2304 | tf_op jit(solution)/shard_map/all_gather | solution.py:123
  30.9 9.3 %all_gather.51 = bf16[256,1024]{1,0:T(8,128)(2,1)S(1)} all-gather(bf16[256,128]{1,0:T(8,128)(2,1)} %param.22), channel_id=1, replica_groups=mesh['fsdp'=8,'tensor'=4] {'fsdp'}, dimensions={1}, use_global_device_ids=true | all-gather | bytes 589824 | tf_op jit(solution)/shard_map/all_gather | solution.py:121
  40.2 0.8 dynamic-update-slice
  41.1 0.8 dynamic-update-slice.1
  41.9 0.8 dynamic-update-slice.2
  42.7 0.8 dynamic-update-slice.3
  43.9 40.9 %all-reduce.13 = (f32[1024]{0:T(1024)}, f32[1024]{0:T(1024)S(1)}, f32[1024]{0:T(1024)S(1)}, f32[1024]{0:T(1024)S(1)}) all-reduce(f32[1024]{0:T(1024)S(1)} %dynamic-update-slice.3, f32[1024]{0:T(1024)S(1)} %dynamic-update-slice.2, f32[1024]{0:T(1024)S(1)} %dynamic-update-slice.1, ...), channel_id=1, replica_groups=mesh['fsdp'=8,'tensor'=4] {'fsdp','tensor'}, use_global_device_ids=true, to_apply=%add.3 | all-reduce | flops 4096 | bytes 32768
  84.8 1.4 convert_reduce_fusion
  86.2 1.7 fusion.9
  88.0 1.7 convolution_convert_fusion.6
  90.2 7.0 %all-gather.10.cloned.1.call-done = bf16[1024,768]{1,0:T(8,128)(2,1)} async-done(((bf16[128,768]{1,0:T(8,128)(2,1)}), bf16[1024,768]{1,0:T(8,128)(2,1)}) %all-gather.10.cloned.1.call-update) | async-done | bytes 1572880 | tf_op jit(solution)/shard_map/all_gather | solution.py:119
  97.2 3.7 convolution_add_fusion
  100.9 1.9 copy.74
  102.8 0.5 reshape.143
  105.1 0.5 fusion.18
  106.1 0.5 convolution_bitcast_fusion
  106.8 1.5 copy.89
  108.9 1.0 copy.98
  110.2 16.6 %all-gather.12.cloned.1.call-done = bf16[1024,1024]{1,0:T(8,128)(2,1)} async-done(((bf16[128,1024]{1,0:T(8,128)(2,1)}), bf16[1024,1024]{1,0:T(8,128)(2,1)}) %all-gather.12.cloned.1.call-update) | async-done | bytes 2097168 | tf_op jit(solution)/shard_map/all_gather | solution.py:122
  126.8 4.6 %multiply_convert_fusion = (bf16[512,1024]{1,0:T(8,128)(2,1)}, f32[512,1024]{1,0:T(8,128)}) fusion(f32[1024]{0:T(1024)S(1)} %bitcast.202, bf16[1024,1024]{1,0:T(8,128)(2,1)} %all-gather.12.cloned.1.call-done, bf16[1,512,1024]{2,1,0:T(8,128)(2,1)S(1)} %copy-done.2, f32[1024]{0:T(1024)S(1)} %copy-done.10, f32[1024]{0:T(1024)S(1)} %get-tuple-element.28, ...), kind=kOutput, calls=%fused_computation.19 | convolution fusion | flops 1080033280 | bytes 6307840 | tf_op jit(solution)/shard_map/dot_general | solution.py:151
  131.3 25.3 %all-gather.14.cloned.1.call-done = bf16[1024,1024]{1,0:T(8,128)(2,1)} async-done(((bf16[1024,128]{1,0:T(8,128)(2,1)}), bf16[1024,1024]{1,0:T(8,128)(2,1)}) %all-gather.14.cloned.1.call-update) | async-done | bytes 2097168 | tf_op jit(solution)/shard_map/all_gather | solution.py:124
  156.6 5.5 %fusion.80 = (bf16[1024]{0:T(1024)(128)(2,1)S(1)}, bf16[512,1024]{1,0:T(8,128)(2,1)}) fusion(f32[512,1024]{1,0:T(8,128)} %get-tuple-element.56, f32[1024]{0:T(1024)S(1)} %bitcast.203, bf16[1024,1024]{1,0:T(8,128)(2,1)} %all-gather.14.cloned.1.call-done, bf16[1,512,1024]{2,1,0:T(8,128)(2,1)} %all-gather.18.cloned.1.call-done), kind=kOutput, calls=%fused_computation.145 | convolution fusion | flops 1080032256 | bytes 6297600 | tf_op jit(solution)/shard_map/dot_general | solution.py:67
  162.1 0.8 copy.100
  162.9 3.6 convolution_convert_fusion.2
  166.6 3.8 convolution_convert_fusion.3
  170.5 4.2 convolution_convert_fusion.4
  174.8 3.2 fusion.81
  178.0 1.4 add_convert_fusion
  179.5 4.1 convolution_convert_fusion
  183.7 4.0 copy.102
  187.7 4.0 convolution_convert_fusion.1
  191.7 0.6 copy-done.15
  192.3 0.6 dynamic-slice
  194.8 13.3 %all-reduce.6 = bf16[4,192]{1,0:T(4,128)(2,1)S(1)} all-reduce(bf16[4,192]{1,0:T(4,128)(2,1)S(1)} %convert_element_type.187), channel_id=8, replica_groups=mesh['fsdp'=8,'tensor'=4] {'fsdp'}, use_global_device_ids=true, to_apply=%region_14.15.clone | all-reduce | flops 768 | bytes 3072
  208.1 0.7 dynamic-slice_convert_fusion
  208.7 0.9 copy.99
  209.7 0.7 convert_element_type.190
  210.3 21.1 %reduce-scatter.28.cloned.1.call-done = bf16[32,4]{1,0:T(8,128)(2,1)} async-done(((bf16[256,4]{1,0:T(8,128)(2,1)}), bf16[32,4]{1,0:T(8,128)(2,1)}) %reduce-scatter.28.cloned.1.call-update) | async-done | bytes 272
  231.5 0.8 copy.101
  232.2 0.6 convert_element_type.195
  232.8 40.3 %reduce-scatter.22.cloned.1.call-done = bf16[128,768]{1,0:T(8,128)(2,1)} async-done(((bf16[1024,768]{1,0:T(8,128)(2,1)}), bf16[128,768]{1,0:T(8,128)(2,1)}) %reduce-scatter.22.cloned.1.call-update) | async-done | bytes 196624 | tf_op jit(solution)/shard_map/reduce_scatter | solution.py:273
  273.1 1.7 convert_element_type.185
  274.8 27.9 %reduce-scatter.18.cloned.1.call-done = bf16[128,1024]{1,0:T(8,128)(2,1)} async-done(((bf16[512,1024]{1,0:T(8,128)(2,1)}), bf16[128,1024]{1,0:T(8,128)(2,1)}) %reduce-scatter.18.cloned.1.call-update) | async-done | bytes 262160 | tf_op jit(solution)/shard_map/reduce_scatter | solution.py:252
  302.7 28.0 %reduce-scatter.20.cloned.1.call-done = bf16[128,1024]{1,0:T(8,128)(2,1)} async-done(((bf16[512,1024]{1,0:T(8,128)(2,1)}), bf16[128,1024]{1,0:T(8,128)(2,1)}) %reduce-scatter.20.cloned.1.call-update) | async-done | bytes 262160 | tf_op jit(solution)/shard_map/reduce_scatter | solution.py:255
  330.7 1.4 fusion.52
  332.2 40.2 %all-reduce.12 = (f32[1024]{0:T(1024)S(1)}, f32[1024]{0:T(1024)S(1)}, f32[1024]{0:T(1024)S(1)}, f32[1024]{0:T(1024)S(1)}, f32[1024]{0:T(1024)S(1)}, /*index=5*/f32[1024]{0:T(1024)S(1)}, f32[1024]{0:T(1024)S(1)}) all-reduce(f32[1024]{0:T(1024)S(1)} %dynamic-update-slice.5, ...), channel_id=1, replica_groups=mesh['fsdp'=8,'tensor'=4] {'fsdp','tensor'}, use_global_device_ids=true, to_apply=%add.5 | all-reduce | flops 7168 | bytes 57344
  372.5 0.6 dynamic-slice.3
  373.0 0.6 dynamic-slice.4
  373.6 0.6 dynamic-slice.5
  374.2 0.6 dynamic-slice.6
  374.8 2.2 fusion.57
  377.0 25.4 %reduce-scatter.30.cloned.1.call-done = bf16[128,1024]{1,0:T(8,128)(2,1)} async-done(((bf16[1024,1024]{1,0:T(8,128)(2,1)}), bf16[128,1024]{1,0:T(8,128)(2,1)}) %reduce-scatter.30.cloned.1.call-update) | async-done | bytes 262160
  402.4 1.1 copy.103
  403.5 0.8 convert_element_type.197
  404.3 42.5 %reduce-scatter.24.cloned.1.call-done = bf16[128,1024]{1,0:T(8,128)(2,1)} async-done(((bf16[1024,1024]{1,0:T(8,128)(2,1)}), bf16[128,1024]{1,0:T(8,128)(2,1)}) %reduce-scatter.24.cloned.1.call-update) | async-done | bytes 262160 | tf_op jit(solution)/shard_map/reduce_scatter | solution.py:282
  446.8 1.8 convert_element_type.192
  448.6 0.5 copy.146
  (118 shorter events, 6.3 us)
Async XLA Ops:
  7.2 36.5 %copy-start.7 = (s32[1,4,128]{2,1,0:T(4,128)S(1)}, s32[1,4,128]{2,1,0:T(4,128)}, u32[]{:S(2)}) copy-start(s32[1,4,128]{2,1,0:T(4,128)} %param.18) | copy-start | bytes 6148
  7.2 77.6 %all-gather.16.cloned.1.call-start = ((), (), s32[]{:S(2)}) async-start(), calls=%async_computation.16 | async-start | bytes 1310720 | tf_op jit(solution)/shard_map/all_gather | solution.py:128
  7.9 80.1 %all-gather.18.cloned.1.call-start = ((), (), s32[]{:S(2)}) async-start(), calls=%async_computation.17 | async-start | bytes 1310720 | tf_op jit(solution)/shard_map/all_gather | solution.py:214
  8.7 88.5 %all-gather.10.cloned.1.call-start = ((), (), s32[]{:S(2)}) async-start(), calls=%async_computation.8 | async-start | bytes 1769472 | tf_op jit(solution)/shard_map/all_gather | solution.py:119
  9.4 117.3 %all-gather.12.cloned.1.call-start = ((), (), s32[]{:S(2)}) async-start(), calls=%async_computation.9 | async-start | bytes 2359296 | tf_op jit(solution)/shard_map/all_gather | solution.py:122
  10.0 146.6 %all-gather.14.cloned.1.call-start = ((), (), s32[]{:S(2)}) async-start(), calls=%async_computation.10 | async-start | bytes 2359296 | tf_op jit(solution)/shard_map/all_gather | solution.py:124
  10.6 198.1 %reduce-scatter.26.cloned.1.call-start = ((), (), s32[]{:S(2)}) async-start(), calls=%async_computation.18 | async-start | bytes 589824
  40.2 49.5 %copy-start.4 = (bf16[256,1024]{1,0:T(8,128)(2,1)}, bf16[256,1024]{1,0:T(8,128)(2,1)S(1)}, u32[]{:S(2)}) copy-start(bf16[256,1024]{1,0:T(8,128)(2,1)S(1)} %all_gather.51) | copy-start | bytes 1572868
  84.8 12.4 %copy-start.11 = (f32[1024]{0:T(1024)}, f32[1024]{0:T(1024)S(1)}, u32[]{:S(2)}) copy-start(f32[1024]{0:T(1024)S(1)} %get-tuple-element.29) | copy-start | bytes 12292
  86.2 11.0 %copy-start.1 = (bf16[1,512,1024]{2,1,0:T(8,128)(2,1)S(1)}, bf16[1,512,1024]{2,1,0:T(8,128)(2,1)}, u32[]{:S(2)}) copy-start(bf16[1,512,1024]{2,1,0:T(8,128)(2,1)} %all-gather.16.cloned.1.call-done) | copy-start | bytes 3145732
  88.0 9.2 %copy-start.8 = (f32[512]{0:T(512)}, f32[512]{0:T(512)S(1)}, u32[]{:S(2)}) copy-start(f32[512]{0:T(512)S(1)} %add_rsqrt_fusion) | copy-start | bytes 6148
  106.6 1.9 copy-start.6
  108.3 18.5 %copy-start.2 = (bf16[1,512,1024]{2,1,0:T(8,128)(2,1)S(1)}, bf16[1,512,1024]{2,1,0:T(8,128)(2,1)}, u32[]{:S(2)}) copy-start(bf16[1,512,1024]{2,1,0:T(8,128)(2,1)} %all-gather.16.cloned.1.call-done) | copy-start | bytes 3145732
  108.3 18.5 %copy-start.9 = (f32[512]{0:T(512)S(1)}, f32[512]{0:T(512)}, u32[]{:S(2)}) copy-start(f32[512]{0:T(512)} %copy-done.8) | copy-start | bytes 6148
  108.3 18.5 %copy-start.10 = (f32[1024]{0:T(1024)S(1)}, f32[1024]{0:T(1024)}, u32[]{:S(2)}) copy-start(f32[1024]{0:T(1024)} %get-tuple-element.27) | copy-start | bytes 12292
  110.0 121.5 %reduce-scatter.28.cloned.1.call-start = ((), (), s32[]{:S(2)}) async-start(), calls=%async_computation.19 | async-start | bytes 73728
  156.6 6.3 %copy-start.12 = (f32[1024]{0:T(1024)S(1)}, f32[1024]{0:T(1024)}, u32[]{:S(2)}) copy-start(f32[1024]{0:T(1024)} %copy-done.11) | copy-start | bytes 12292
  162.9 110.3 %reduce-scatter.22.cloned.1.call-start = ((), (), s32[]{:S(2)}) async-start(), calls=%async_computation.14 | async-start | bytes 1769472 | tf_op jit(solution)/shard_map/reduce_scatter | solution.py:273
  166.6 136.2 %reduce-scatter.18.cloned.1.call-start = ((), (), s32[]{:S(2)}) async-start(), calls=%async_computation.12 | async-start | bytes 1310720 | tf_op jit(solution)/shard_map/reduce_scatter | solution.py:252
  170.4 160.3 %reduce-scatter.20.cloned.1.call-start = ((), (), s32[]{:S(2)}) async-start(), calls=%async_computation.13 | async-start | bytes 1310720 | tf_op jit(solution)/shard_map/reduce_scatter | solution.py:255
  174.7 200.1 %reduce-scatter.16.cloned.1.call-start = ((), (), s32[]{:S(2)}) async-start(), calls=%async_computation.11 | async-start | bytes 1310720 | tf_op jit(solution)/shard_map/reduce_scatter | solution.py:155
  174.8 3.2 copy-start.5
  179.5 222.9 %reduce-scatter.30.cloned.1.call-start = ((), (), s32[]{:S(2)}) async-start(), calls=%async_computation.20 | async-start | bytes 2359296
  187.7 259.1 %reduce-scatter.24.cloned.1.call-start = ((), (), s32[]{:S(2)}) async-start(), calls=%async_computation.15 | async-start | bytes 2359296 | tf_op jit(solution)/shard_map/reduce_scatter | solution.py:282
  191.7 0.7 copy-start.15
  191.7 1.9 copy-start.13
  191.7 2.2 copy-start.14
  191.7 2.4 copy-start
  191.7 2.5 copy-start.3
  372.5 76.6 %copy-start.16 = (f32[32]{0:T(128)}, f32[32]{0:T(128)S(1)}, u32[]{:S(2)}) copy-start(f32[32]{0:T(128)S(1)} %dynamic-slice.2) | copy-start | bytes 388
Sparse Core Ops, SparseCore 0:
  9.6 30.6 all-gather.15
  41.9 28.0 all-gather.17
  71.9 25.2 all-gather.9
  98.9 27.7 all-gather.11
  128.5 28.0 all-gather.13
  160.1 34.1 reduce-scatter.25
  197.8 33.5 reduce-scatter.27
  234.7 38.3 reduce-scatter.21
  275.4 27.2 reduce-scatter.17
  304.9 25.7 reduce-scatter.19
  333.0 26.4 reduce-scatter.15
  362.7 39.6 reduce-scatter.29
  405.6 41.0 reduce-scatter.23
where the time goes:
time: 457 us; the launch traced here: 456 us
  waiting for transfers between devices  237 us (52%)
  blocking collectives  123 us (27%)
  matrix products  42.6 us (9%)
  local copies, waits for them, and re-layouts  21.9 us (5%)
  other arithmetic  15.2 us (3%)
  between operations  15 us (3%)
    unnamed x3, blocking collectives  94.4 us
    unnamed x16, waiting for transfers between devices  49.7 us
    reduce_scatter x1, waiting for transfers between devices, shards(): lax.psum_scatter(g_inner.astype(jnp.bfloat16), 'fsdp', scatter_dimension=...  42.5 us
    reduce_scatter x1, waiting for transfers between devices, shards(): lax.psum_scatter(g_qkv.astype(jnp.bfloat16), 'fsdp', scatter_dimension=0,...  40.3 us
    reduce_scatter x1, waiting for transfers between devices, shards(): lax.psum_scatter(second_branch_gradient.astype(jnp.bfloat16), 'tensor', s...  28 us
    reduce_scatter x1, waiting for transfers between devices, shards(): lax.psum_scatter(first_branch_gradient.astype(jnp.bfloat16), 'tensor', sc...  27.9 us
    dot_general x8, matrix products, matmul(): lax.dot_general(left, right, (((left_dim,), (right_dim,)), ((), ())), pre...  27.3 us
    all_gather x1, waiting for transfers between devices, shards(): lax.all_gather(outer_weight, 'fsdp', axis=1, tiled=True)  25.3 us
  transfers between devices with their start and end apart: 13, of which 9 were waited for; matrix products, arithmetic and copies ran while one was open for 17% of the time, Pallas kernels for 0%

commit v1 on v0

--- a/solution.py
+++ b/solution.py
@@ -86,7 +86,7 @@
     return jnp.where(mask, product * scale, MASKED)
 
 
-def shards(
+def plain_shards(
     layer_input,
     out_grad,
     segments,
@@ -318,7 +318,317 @@
     )
 
 
+def core_swap(value):
+    count = lax.axis_size("fsdp")
+    return lax.ppermute(value, "fsdp", [(i, i ^ 1) for i in range(count)])
+
+
+def near_swap(value):
+    count = lax.axis_size("fsdp")
+    return lax.ppermute(value, "fsdp", [(i, i ^ (4 if i & 1 else 2)) for i in range(count)])
+
+
+def far_swap(value):
+    count = lax.axis_size("fsdp")
+    return lax.ppermute(value, "fsdp", [(i, i ^ (2 if i & 1 else 4)) for i in range(count)])
+
+
+def depth_swap(value, mask):
+    count = lax.axis_size("tensor")
+    return lax.ppermute(value, "tensor", [(i, i ^ mask) for i in range(count)])
+
+
+def slot_masks():
+    core = lax.axis_index("fsdp") & 1
+    near = jnp.where(core == 0, 2, 4)
+    far = 6 - near
+    return [0, 1, near, near + 1, far, far + 1, 6, 7]
+
+
+def gather_blocks(shard):
+    partner = core_swap(shard)
+    near = near_swap(jnp.stack([shard, partner]))
+    across = far_swap(near[0])
+    far = core_swap(near)
+    across_partner = core_swap(across)
+    return [shard, partner, near[0], near[1], far[1], far[0], across, across_partner]
+
+
+def in_order(slots):
+    me = lax.axis_index("fsdp")
+    core = me & 1
+    stacked = jnp.stack(slots)
+    ordered = []
+    for k in range(len(slots)):
+        mask = me ^ k
+        middle = (mask >= 2) & (mask < 6)
+        slot = jnp.where((core == 1) & middle, mask ^ 6, mask)
+        ordered.append(lax.dynamic_index_in_dim(stacked, slot, 0, keepdims=False))
+    return ordered
+
+
+def scatter_sum(keep, send):
+    kept = keep.astype(jnp.float32) + core_swap(send).astype(jnp.float32)
+    across = far_swap(kept[3].astype(jnp.bfloat16))
+    pair = jnp.stack([kept[1] + across.astype(jnp.float32), kept[2]]).astype(jnp.bfloat16)
+    near = near_swap(pair)
+    far = core_swap(near[1])
+    return kept[0] + near[0].astype(jnp.float32) + far.astype(jnp.float32)
+
+
+def split_blocks(blocks):
+    me = lax.axis_index("fsdp")
+    masks = slot_masks()
+    pick = lambda s: lax.dynamic_index_in_dim(blocks, me ^ masks[s], 0, keepdims=False)
+    return jnp.stack([pick(s) for s in (0, 2, 3, 6)]), jnp.stack([pick(s) for s in (1, 5, 4, 7)])
+
+
+def in_three(value):
+    high = lax.reduce_precision(value, 8, 7)
+    rest = value - high
+    middle = lax.reduce_precision(rest, 8, 7)
+    return jnp.concatenate([high, middle, rest - middle]).astype(jnp.bfloat16)
+
+
+def pair_shards(
+    layer_input,
+    out_grad,
+    segments,
+    positions,
+    qkv_weight,
+    qkv_bias,
+    dense_weight,
+    dense_bias,
+    inner_weight,
+    inner_bias,
+    outer_weight,
+    outer_bias,
+    attention_norm_gain,
+    attention_norm_bias,
+    feedforward_norm_gain,
+    feedforward_norm_bias,
+):
+    n = lax.axis_size("fsdp")
+    m = lax.axis_size("tensor")
+    f = lax.axis_index("fsdp")
+    t = lax.axis_index("tensor")
+    x = layer_input[0]
+    g = out_grad[0]
+    rows, width = x.shape
+    strip = width // n
+    heads = qkv_bias.shape[0]
+    qkv_cols = qkv_weight.shape[1]
+    units = inner_weight.shape[1]
+    lanes = attention_norm_gain.shape[0]
+    scale = HD ** (-0.5)
+
+    vectors = in_three(
+        jnp.stack(
+            [
+                attention_norm_gain,
+                attention_norm_bias,
+                feedforward_norm_gain,
+                feedforward_norm_bias,
+                dense_bias + outer_bias,
+            ]
+        )
+    )
+    spread = lax.dynamic_update_slice(jnp.zeros((15, strip), jnp.bfloat16), vectors, (0, lanes * t))
+    for bit in range(m.bit_length() - 1):
+        spread = spread + depth_swap(spread, 1 << bit)
+    qkv_row = lax.dynamic_update_slice(
+        jnp.zeros((heads, 3 * HD), jnp.bfloat16), qkv_bias, (0, qkv_bias.shape[1] * f)
+    ).reshape(-1, strip)
+    inner_row = lax.dynamic_update_slice(
+        jnp.zeros((heads, units // heads), jnp.bfloat16), inner_bias, (0, inner_bias.shape[1] * f)
+    ).reshape(-1, strip)
+    qkv_rows, inner_rows = qkv_row.shape[0], inner_row.shape[0]
+    used = 15 + qkv_rows + inner_rows
+    small = jnp.concatenate(
+        [spread, qkv_row, inner_row, jnp.zeros((strip - used, strip), jnp.bfloat16)]
+    )
+
+    x_slots = [x] + [depth_swap(x, k) for k in range(1, m)]
+    outer_parts = [outer_weight[strip * i : strip * (i + 1)] for i in range(units // strip)]
+    dense_parts = [dense_weight[strip * i : strip * (i + 1)] for i in range(heads * HD // strip)]
+    second_msg = jnp.concatenate([inner_weight] + outer_parts + dense_parts, axis=1)
+    first_msg = jnp.concatenate([qkv_weight, small], axis=1)
+    second_blocks = in_order(gather_blocks(second_msg))
+    first_blocks = in_order(gather_blocks(first_msg))
+    g_slots = [g] + [depth_swap(g, k) for k in range(1, m)]
+
+    qkv_w = jnp.concatenate([b[:, :qkv_cols] for b in first_blocks])
+    smalls = jnp.stack([b[:, qkv_cols:] for b in first_blocks]).astype(jnp.float32)
+    vec = smalls[:, 0:5] + smalls[:, 5:10] + smalls[:, 10:15]
+    vec = jnp.transpose(vec, (1, 0, 2)).reshape(5, width)
+    biases = jnp.sum(smalls[:, 15:used], 0)
+    qkv_b = biases[:qkv_rows].reshape(-1)
+    inner_b = biases[qkv_rows:].reshape(-1)
+    inner_w = jnp.concatenate([b[:, :units] for b in second_blocks])
+
+    def columns(start, count):
+        return jnp.concatenate(
+            [
+                jnp.concatenate([b[:, start + strip * i : start + strip * (i + 1)] for b in second_blocks], axis=1)
+                for i in range(count)
+            ]
+        )
+
+    outer_w = columns(units, units // strip)
+    dense_w = columns(2 * units, heads * HD // strip)
+
+    pick = lambda a: jnp.concatenate([lax.dynamic_slice_in_dim(a, t ^ k, 1, 0) for k in range(m)])
+    segs = pick(segments[0])
+    poss = pick(positions[0])
+    tokens = jnp.concatenate(x_slots)
+    cot = jnp.concatenate(g_slots)
+    xhat, rstd = normalize_rows(tokens)
+    first = (xhat * vec[0] + vec[1]).astype(jnp.bfloat16)
+    second = (xhat * vec[2] + vec[3]).astype(jnp.bfloat16)
+    packed = (matmul(first, qkv_w, 1, 0) + qkv_b).reshape(m, rows, heads, 3, HD)
+    cosine, sine = angle_tables(poss)
+    query = turn(packed[:, :, :, 0], cosine, sine).astype(jnp.bfloat16)
+    keyed = turn(packed[:, :, :, 1], cosine, sine).astype(jnp.bfloat16)
+    value = packed[:, :, :, 2].astype(jnp.bfloat16)
+    mask = attention_mask(segs)[:, None]
+    scores = raw_scores(query, keyed, mask, scale)
+    peak = jnp.max(scores, -1, keepdims=True)
+    log_total = peak + jnp.log(jnp.sum(jnp.exp(scores - peak), -1, keepdims=True))
+    probs = jnp.exp(scores - log_total)
+    context = jnp.einsum(
+        "shqk,skhd->sqhd", probs.astype(jnp.bfloat16), value, preferred_element_type=jnp.float32
+    ).astype(jnp.bfloat16)
+    flat_ctx = context.reshape(m * rows, heads * HD)
+    pre = matmul(second, inner_w, 1, 0) + inner_b
+    act = gelu_value(pre).astype(jnp.bfloat16)
+    partial = matmul(flat_ctx, dense_w, 1, 0) + matmul(act, outer_w, 1, 0)
+    result = x.astype(jnp.float32) + vec[4] + partial[:rows]
+    for k in range(1, m):
+        result = result + depth_swap(partial[rows * k : rows * (k + 1)].astype(jnp.bfloat16), k).astype(jnp.float32)
+
+    d_act = matmul(cot, outer_w, 1, 1)
+    g_outer = matmul(act, cot, 0, 0)
+    d_pre = d_act * gelu_slope(pre)
+    g_inner_b = jnp.sum(d_pre, 0)
+    d_pre_b = d_pre.astype(jnp.bfloat16)
+    g_inner = matmul(second, d_pre_b, 0, 0)
+    d_second = matmul(d_pre_b, inner_w, 1, 1)
+    big = jnp.stack(
+        [
+            jnp.concatenate(
+                [g_inner[strip * k : strip * (k + 1)]]
+                + [g_outer[strip * i : strip * (i + 1), strip * k : strip * (k + 1)] for i in range(units // strip)],
+                axis=1,
+            )
+            for k in range(n)
+        ]
+    ).astype(jnp.bfloat16)
+    big_sum = scatter_sum(*split_blocks(big))
+
+    d_ctx = matmul(cot, dense_w, 1, 1).astype(jnp.bfloat16)
+    g_dense = matmul(flat_ctx, cot, 0, 0)
+    d_ctx4 = d_ctx.reshape(context.shape)
+    delta = jnp.sum(d_ctx4.astype(jnp.float32) * context.astype(jnp.float32), -1)
+    d_probs = jnp.einsum("sqhd,skhd->shqk", d_ctx4, value, preferred_element_type=jnp.float32)
+    d_scores = probs * (d_probs - jnp.transpose(delta, (0, 2, 1))[..., None])
+    d_value = jnp.einsum(
+        "shqk,sqhd->skhd", probs.astype(jnp.bfloat16), d_ctx4, preferred_element_type=jnp.float32
+    )
+    d_scores_b = d_scores.astype(jnp.bfloat16)
+    d_query = (
+        jnp.einsum("shqk,skhd->sqhd", d_scores_b, keyed, preferred_element_type=jnp.float32) * scale
+    )
+    d_key = (
+        jnp.einsum("shqk,sqhd->skhd", d_scores_b, query, preferred_element_type=jnp.float32) * scale
+    )
+    d_packed = jnp.stack(
+        [turn_back(d_query, cosine, sine), turn_back(d_key, cosine, sine), d_value], 3
+    ).reshape(m * rows, qkv_cols)
+    g_qkv_b = jnp.sum(d_packed, 0)
+    d_packed_b = d_packed.astype(jnp.bfloat16)
+    g_qkv = matmul(first, d_packed_b, 0, 0)
+    d_first = matmul(d_packed_b, qkv_w, 1, 1)
+
+    own = g.astype(jnp.float32)
+    sums = jnp.stack(
+        [
+            jnp.sum(own, 0),
+            jnp.sum(d_first * xhat, 0),
+            jnp.sum(d_first, 0),
+            jnp.sum(d_second * xhat, 0),
+            jnp.sum(d_second, 0),
+        ]
+    )
+    for bit in range(m.bit_length() - 1):
+        sums = sums + depth_swap(sums, 1 << bit)
+    d_norm = d_first * vec[0] + d_second * vec[2]
+    local_norm = d_norm[:rows]
+    for k in range(1, m):
+        local_norm = local_norm + depth_swap(d_norm[rows * k : rows * (k + 1)].astype(jnp.bfloat16), k).astype(jnp.float32)
+    local_xhat, local_rstd = xhat[:rows], rstd[:rows]
+    input_gradient = own + local_rstd * (
+        local_norm
+        - jnp.mean(local_norm, -1, keepdims=True)
+        - local_xhat * jnp.mean(local_norm * local_xhat, -1, keepdims=True)
+    )
+    rest = jnp.stack(
+        [
+            jnp.concatenate(
+                [g_qkv[strip * k : strip * (k + 1)]]
+                + [g_dense[strip * i : strip * (i + 1), strip * k : strip * (k + 1)] for i in range(heads * HD // strip)]
+                + [
+                    jnp.concatenate(
+                        [
+                            sums[:, strip * k : strip * (k + 1)],
+                            g_qkv_b.reshape(-1, strip),
+                            g_inner_b.reshape(-1, strip),
+                            jnp.zeros((strip - 5 - qkv_rows - inner_rows, strip), jnp.float32),
+                        ]
+                    )
+                ],
+                axis=1,
+            )
+            for k in range(n)
+        ]
+    ).astype(jnp.bfloat16)
+    rest_sum = scatter_sum(*split_blocks(rest))
+    s_inner = big_sum[:, :units]
+    s_outer = jnp.concatenate([big_sum[:, units + strip * i : units + strip * (i + 1)] for i in range(units // strip)])
+    s_qkv = rest_sum[:, :qkv_cols]
+    at = qkv_cols
+    s_dense = jnp.concatenate([rest_sum[:, at + strip * i : at + strip * (i + 1)] for i in range(heads * HD // strip)])
+    tiny = rest_sum[:, qkv_cols + heads * HD :]
+    five = lax.dynamic_slice(tiny, (0, lanes * t), (5, lanes))
+    s_qkv_b = lax.dynamic_slice_in_dim(
+        tiny[5 : 5 + qkv_rows].reshape(heads, 3 * HD), qkv_bias.shape[1] * f, qkv_bias.shape[1], 1
+    )
+    s_inner_b = lax.dynamic_slice_in_dim(
+        tiny[5 + qkv_rows : 5 + qkv_rows + inner_rows].reshape(heads, units // heads),
+        inner_bias.shape[1] * f,
+        inner_bias.shape[1],
+        1,
+    )
+    return (
+        result.astype(jnp.bfloat16)[None],
+        input_gradient.astype(jnp.bfloat16)[None],
+        s_qkv,
+        s_qkv_b,
+        s_dense,
+        five[0],
+        s_inner,
+        s_inner_b,
+        s_outer,
+        five[0],
+        five[1],
+        five[2],
+        five[3],
+        five[4],
+    )
+
+
 def solution(mesh):
+    n, m = mesh.shape["fsdp"], mesh.shape["tensor"]
+    shards = pair_shards if n == 8 and m & (m - 1) == 0 else plain_shards
     placed = (
         P(None, ("fsdp", "tensor"), None),
         P(None, ("fsdp", "tensor"), None),

time: 457 us -> 237 us (0.52)
  waiting for transfers between devices: 237 us -> 87.6 us
  blocking collectives: 123 us -> 0 us
  local copies, waits for them, and re-layouts: 21.9 us -> 63.6 us
  starting transfers between devices: 0.7 us -> 34.8 us
  matrix products: 42.6 us -> 25.2 us
  between operations: 15 us -> 2.92 us
  other arithmetic: 15.2 us -> 20.2 us
    reduce_scatter x5 -> x0, waiting for transfers between devices: 139 us -> none  [the longest x1 42.5 us: shards(): lax.psum_scatter(g_inner.astype(jnp.bfloat16), 'fsdp', scatter_dimension=...]
    unnamed x3 -> x0, blocking collectives: 94.4 us -> none
    ppermute x0 -> x34, waiting for transfers between devices: none -> 87.6 us  [the longest x16 43.7 us: depth_swap(): return lax.ppermute(value, 'tensor', [(i, i ^ mask) for i in range(count)])]
    unnamed x16 -> x0, waiting for transfers between devices: 49.7 us -> none
    all_gather x5 -> x0, waiting for transfers between devices: 48.8 us -> none  [the longest x1 25.3 us: shards(): lax.all_gather(outer_weight, 'fsdp', axis=1, tiled=True)]
    ppermute x0 -> x34, starting transfers between devices: none -> 34.8 us  [the longest x16 22.6 us: depth_swap(): return lax.ppermute(value, 'tensor', [(i, i ^ mask) for i in range(count)])]
    all_gather x3 -> x0, blocking collectives: 28.6 us -> none  [the longest x1 10.5 us: shards(): lax.all_gather(qkv_bias, 'fsdp', axis=1, tiled=True)]
    unnamed x60 -> x290, local copies, waits for them, and re-layouts: 16.6 us -> 41.1 us
  transfers between devices with their start and end apart: 13 -> 34, of which waited for: 9 -> 14; matrix products, arithmetic and copies ran while one was open for 17% -> 29% of each run, Pallas kernels for 0% -> 0%
where the time goes in v1:
time: 237 us; the launch traced here: 234 us
  waiting for transfers between devices  87.6 us (37%)
  local copies, waits for them, and re-layouts  63.6 us (27%)
  starting transfers between devices  34.8 us (15%)
  matrix products  25.2 us (11%)
  other arithmetic  20.2 us (9%)
  between operations  2.92 us (1%)
    ppermute x16, waiting for transfers between devices, depth_swap(): return lax.ppermute(value, 'tensor', [(i, i ^ mask) for i in range(count)])  43.7 us
    unnamed x290, local copies, waits for them, and re-layouts  41.1 us
    dot_general x12, matrix products, matmul(): lax.dot_general(left, right, (((left_dim,), (right_dim,)), ((), ())), pre...  22.9 us
    ppermute x16, starting transfers between devices, depth_swap(): return lax.ppermute(value, 'tensor', [(i, i ^ mask) for i in range(count)])  22.6 us
    ppermute x4, waiting for transfers between devices, near_swap(): lax.ppermute(value, 'fsdp', [(i, i ^ (4 if i & 1 else 2)) for i in range(...  21.1 us
    ppermute x4, waiting for transfers between devices, far_swap(): lax.ppermute(value, 'fsdp', [(i, i ^ (2 if i & 1 else 4)) for i in range(...  20.6 us
    ppermute x4, starting transfers between devices, near_swap(): lax.ppermute(value, 'fsdp', [(i, i ^ (4 if i & 1 else 2)) for i in range(...  6.02 us
    ppermute x4, starting transfers between devices, far_swap(): lax.ppermute(value, 'fsdp', [(i, i ^ (2 if i & 1 else 4)) for i in range(...  5.67 us
  transfers between devices with their start and end apart: 34, of which 14 were waited for; matrix products, arithmetic and copies ran while one was open for 29% of the time, Pallas kernels for 0%

profile of v1, /device:TPU:0, one launch (start us, length us, event | category | flops | bytes accessed | tf_op | source)
XLA Modules:
  0.0 234.2 jit_solution(11318683365397691259)
XLA Ops:
  0.7 5.1 %collective-permute-start.9 = (bf16[128,1024]{1,0:T(8,128)(2,1)}, bf16[128,1024]{1,0:T(8,128)(2,1)S(1)}, u32[]{:S(2)}, u32[]{:S(2)}) collective-permute-start(bf16[128,1024]{1,0:T(8,128)(2,1)} %bitcast.285), channel_id=1, source_target_pairs={{0,3},{1,2},{2,1},{3,0},{4,7},{5,6},{6,5},{7,4},{8,11},{9,10},{10,... | collective-permute-start | bytes 786440 | tf_op jit(solution)/shard_map/ppermute | solution.py:338
  8.1 1.5 collective-permute-start
  20.9 2.2 collective-permute-done
  23.3 1.4 collective-permute-start.1
  25.3 3.2 %collective-permute-done.1 = bf16[15,128]{1,0:T(8,128)(2,1)S(1)} collective-permute-done((bf16[15,128]{1,0:T(8,128)(2,1)S(1)}, bf16[15,128]{1,0:T(8,128)(2,1)S(1)}, u32[]{:S(2)}, u32[]{:S(2)}) %collective-permute-start.1) | collective-permute-done | bytes 3872 | tf_op jit(solution)/shard_map/ppermute | solution.py:338
  30.1 2.5 %collective-permute-start.20 = (bf16[128,1024]{1,0:T(8,128)(2,1)}, bf16[128,1024]{1,0:T(8,128)(2,1)}, u32[]{:S(2)}, u32[]{:S(2)}) collective-permute-start(bf16[128,1024]{1,0:T(8,128)(2,1)} %bitcast.61), channel_id=1, source_target_pairs={{0,3},{1,2},{2,1},{3,0},{4,7},{5,6},{6,5},{7,4},{8,11},{9,10},{10,... | collective-permute-start | bytes 786440 | tf_op jit(solution)/shard_map/ppermute | solution.py:338
  33.6 1.1 collective-permute-start.18
  34.7 1.5 collective-permute-start.3
  37.7 5.5 %collective-permute-done.3 = bf16[2,128,896]{2,1,0:T(8,128)(2,1)S(1)} collective-permute-done((bf16[2,128,896]{2,1,0:T(8,128)(2,1)S(1)}, bf16[2,128,896]{2,1,0:T(8,128)(2,1)S(1)}, u32[]{:S(2)}, u32[]{:S(2)}) %collective-permute-start.3) | collective-permute-done | bytes 458784 | tf_op jit(solution)/shard_map/ppermute | solution.py:328
  43.2 1.6 collective-permute-start.5
  44.8 1.1 pad_maximum_fusion.2
  46.0 3.3 %collective-permute-done.5 = bf16[128,896]{1,0:T(8,128)(2,1)S(1)} collective-permute-done((bf16[128,896]{1,0:T(8,128)(2,1)S(1)}, bf16[128,896]{1,0:T(8,128)(2,1)S(1)}, u32[]{:S(2)}, u32[]{:S(2)}) %collective-permute-start.5) | collective-permute-done | bytes 229408 | tf_op jit(solution)/shard_map/ppermute | solution.py:333
  49.3 1.5 collective-permute-start.11
  50.9 1.4 collective-permute-done.6
  54.6 1.1 convolution_add_fusion.1
  58.3 7.5 %collective-permute-done.11 = bf16[2,128,2304]{2,1,0:T(8,128)(2,1)} collective-permute-done((bf16[2,128,2304]{2,1,0:T(8,128)(2,1)}, bf16[2,128,2304]{2,1,0:T(8,128)(2,1)}, u32[]{:S(2)}, u32[]{:S(2)}) %collective-permute-start.11) | collective-permute-done | bytes 1179680 | tf_op jit(solution)/shard_map/ppermute | solution.py:328
  65.8 1.1 slice_bitcast_fusion.2
  66.9 1.6 collective-permute-start.13
  69.1 2.4 %constant_dynamic-update-slice_fusion.34 = bf16[8,128,2304]{2,1,0:T(8,128)(2,1)} fusion(bf16[8,128,2304]{2,1,0:T(8,128)(2,1)} %constant_dynamic-update-slice_fusion.35, bf16[2,128,2304]{2,1,0:T(8,128)(2,1)} %collective-permute-done.11), kind=kLoop, calls=%fused_computation.177 | loop fusion | bytes 2359296
  71.5 5.4 %collective-permute-done.13 = bf16[128,2304]{1,0:T(8,128)(2,1)S(1)} collective-permute-done((bf16[128,2304]{1,0:T(8,128)(2,1)S(1)}, bf16[128,2304]{1,0:T(8,128)(2,1)S(1)}, u32[]{:S(2)}, u32[]{:S(2)}) %collective-permute-start.13) | collective-permute-done | bytes 589856 | tf_op jit(solution)/shard_map/ppermute | solution.py:333
  80.4 2.6 %dynamic-slice_bitcast_fusion = (bf16[128,2304]{1,0:T(8,128)(2,1)S(1)}, bf16[128,2304]{1,0:T(8,128)(2,1)S(1)}, bf16[128,2304]{1,0:T(8,128)(2,1)S(1)}, bf16[128,2...) fusion(bf16[8,128,2304]{2,1,0:T(8,128)(2,1)} %bitcast_dynamic-u, ...), kind=kLoop, calls=%fused_computation.100 | loop fusion | bytes 9437216 | tf_op jit(solution)/shard_map/jit(dynamic_index_in_dim)/squeeze | solution.py:366
  86.3 2.4 %convolution_convert_fusion.4 = bf16[512,256]{1,0:T(8,128)(2,1)} fusion(bf16[128,1024]{1,0:T(8,128)(2,1)S(1)} %get-tuple-element.208, bf16[128,1024]{1,0:T(8,128)(2,1)S(1)} %get-tuple-element.206, bf16[128,1024]{1,0:T(8,128)(2,1)} %collective-permute-done.20, bf16[128,1024]{1,0:T(8,128)(2,1)} %collective-permute-done.19, ...), kind=kOutput, calls=%fused_computation.38 | convolution fusion | flops 273809408 | bytes 1835008 | tf_op jit(solution)/shard_map/dot_general | solution.py:67
  88.7 1.2 reshape.217
  93.2 1.0 constant_dynamic-update-slice_fusion.59
  94.2 1.0 constant_dynamic-update-slice_fusion.58
  95.2 1.0 constant_dynamic-update-slice_fusion.57
  96.2 1.0 constant_dynamic-update-slice_fusion.56
  97.1 1.0 constant_dynamic-update-slice_fusion.55
  100.1 1.3 fusion.22
  101.5 1.5 multiply_convert_fusion
  103.1 3.4 %fusion.110 = (bf16[1024]{0:T(1024)(128)(2,1)S(1)}, bf16[512,1024]{1,0:T(8,128)(2,1)S(1)}) fusion(f32[512,1024]{1,0:T(8,128)S(1)} %get-tuple-element.291, f32[1024]{0:T(1024)S(1)} %copy-done.66, bf16[1024,1024]{1,0:T(8,128)(2,1)S(1)} %copy-done.75, bf16[128,1024]{1,0:T(8,128)(2,1)} %collective-permute-done.20, ...), kind=kOutput, calls=%fused_computation.513 | convolution fusion | flops 1084226560 | bytes 6297600 | tf_op jit(solution)/shard_map/dot_general | solution.py:67
  106.5 1.9 fusion.93
  108.4 2.6 %collective-permute-start.23 = (bf16[128,1024]{1,0:T(8,128)(2,1)S(1)}, bf16[128,1024]{1,0:T(8,128)(2,1)S(1)}, u32[]{:S(2)}, u32[]{:S(2)}) collective-permute-start(bf16[128,1024]{1,0:T(8,128)(2,1)S(1)} %get-tuple-element.198), channel_id=1, source_target_pairs={{0,3},{1,2},{2,1},{3,0},{4,7},{5,6},{6,5},{7,4},{8,11},{9,10},{10,... | collective-permute-start | bytes 786440 | tf_op jit(solution)/shard_map/ppermute | solution.py:338
  111.0 1.9 collective-permute-start.21
  112.9 1.5 convolution_convert_fusion.1
  114.8 3.9 %convolution_convert_fusion = bf16[1024,1024]{0,1:T(8,128)(2,1)} fusion(bf16[512,1024]{1,0:T(8,128)(2,1)S(1)} %get-tuple-element.290, bf16[128,1024]{1,0:T(8,128)(2,1)} %collective-permute-done.20, bf16[128,1024]{1,0:T(8,128)(2,1)} %collective-permute-done.19, bf16[128,1024]{1,0:T(8,128)(2,1)} %collective-permute-done.18, bf16[128,1024]{1,0:T(8,128)(2,1)} %bitcast.61), kind=kOutput, calls=%fused_computation.21 | convolution fusion | flops 1078984704 | bytes 4194304 | tf_op jit(solution)/shard_map/dot_general | solution.py:67
  126.6 1.9 constant_dynamic-slice_fusion.8
  128.5 1.2 convolution_convert_fusion.2
  129.7 1.7 convolution_convert_fusion.3
  131.5 1.2 fusion.98
  132.7 1.7 collective-permute-done.22
  134.7 2.1 convert_reduce_fusion.1
  137.9 12.7 %collective-permute-done.24 = f32[5,1024]{0,1:T(8,128)S(1)} collective-permute-done((f32[5,1024]{0,1:T(8,128)S(1)}, f32[5,1024]{0,1:T(8,128)S(1)}, u32[]{:S(2)}, u32[]{:S(2)}) %collective-permute-start.24) | collective-permute-done | bytes 20512 | tf_op jit(solution)/shard_map/ppermute | solution.py:338
  151.9 23.8 %collective-permute-done.25 = f32[5,1024]{0,1:T(8,128)} collective-permute-done((f32[5,1024]{0,1:T(8,128)S(1)}, f32[5,1024]{0,1:T(8,128)}, u32[]{:S(2)}, u32[]{:S(2)}) %collective-permute-start.25) | collective-permute-done | bytes 20512 | tf_op jit(solution)/shard_map/ppermute | solution.py:338
  175.7 1.1 add_convert_fusion.2
  176.9 1.2 constant_dynamic-update-slice_fusion.83
  182.7 1.2 copy-done.76
  184.1 1.3 fusion.111
  185.4 1.8 fusion.109
  188.1 1.7 collective-permute-start.17
  189.8 2.7 %collective-permute-start.15 = (bf16[128,1024]{1,0:T(8,128)(2,1)}, bf16[128,1024]{1,0:T(8,128)(2,1)}, u32[]{:S(2)}, u32[]{:S(2)}) collective-permute-start(bf16[128,1024]{1,0:T(8,128)(2,1)} %get-tuple-element.200), channel_id=1, source_target_pairs={{0,1},{1,0},{2,3},{3,2},{4,5},{5,4},{6,7},{7,6},{8,9},{9,8},{10,11... | collective-permute-start | bytes 786440 | tf_op jit(solution)/shard_map/ppermute | solution.py:338
  192.9 1.6 collective-permute-start.27
  196.1 3.6 %collective-permute-done.27 = bf16[128,1152]{0,1:T(8,128)(2,1)S(1)} collective-permute-done((bf16[128,1152]{0,1:T(8,128)(2,1)S(1)}, bf16[128,1152]{0,1:T(8,128)(2,1)S(1)}, u32[]{:S(2)}, u32[]{:S(2)}) %collective-permute-start.27) | collective-permute-done | bytes 294944 | tf_op jit(solution)/shard_map/ppermute | solution.py:333
  199.8 1.6 collective-permute-start.28
  201.4 8.3 %collective-permute-done.31 = bf16[128,2048]{0,1:T(8,128)(2,1)S(1)} collective-permute-done((bf16[128,2048]{0,1:T(8,128)(2,1)S(1)}, bf16[128,2048]{0,1:T(8,128)(2,1)S(1)}, u32[]{:S(2)}, u32[]{:S(2)}) %collective-permute-start.31) | collective-permute-done | bytes 524320 | tf_op jit(solution)/shard_map/ppermute | solution.py:333
  209.8 1.1 pad_maximum_fusion.14
  210.9 1.5 collective-permute-start.32
  213.3 2.2 fusion.58
  215.5 1.0 fusion.29
  217.8 8.2 %collective-permute-done.32 = bf16[2,128,2048]{1,2,0:T(8,128)(2,1)} collective-permute-done((bf16[2,128,2048]{1,2,0:T(8,128)(2,1)}, bf16[2,128,2048]{1,2,0:T(8,128)(2,1)}, u32[]{:S(2)}, u32[]{:S(2)}) %collective-permute-start.32) | collective-permute-done | bytes 1048608 | tf_op jit(solution)/shard_map/ppermute | solution.py:328
  226.0 1.1 slice_bitcast_fusion.3
  230.1 1.5 fusion.19
  231.6 1.0 copy.125
  232.7 1.0 copy.126
  (449 shorter events, 59.6 us)
Async XLA Ops:
  0.6 18.6 %copy-start.67 = (s32[1,4,128]{2,1,0:T(4,128)S(1)}, s32[1,4,128]{2,1,0:T(4,128)}, u32[]{:S(2)}) copy-start(s32[1,4,128]{2,1,0:T(4,128)} %param.18) | copy-start | bytes 6148
  0.7 18.7 %copy-start.68 = (s32[1,4,128]{2,1,0:T(4,128)S(1)}, s32[1,4,128]{2,1,0:T(4,128)}, u32[]{:S(2)}) copy-start(s32[1,4,128]{2,1,0:T(4,128)} %param.19) | copy-start | bytes 6148
  0.7 24.0 %copy-start.71 = (bf16[4,32]{1,0:T(4,128)(2,1)S(1)}, bf16[4,32]{1,0:T(4,128)(2,1)}, u32[]{:S(2)}) copy-start(bf16[4,32]{1,0:T(4,128)(2,1)} %param.25) | copy-start | bytes 772
  0.7 24.1 %copy-start.72 = (bf16[4,24]{1,0:T(4,128)(2,1)S(1)}, bf16[4,24]{1,0:T(4,128)(2,1)}, u32[]{:S(2)}) copy-start(bf16[4,24]{1,0:T(4,128)(2,1)} %param.21) | copy-start | bytes 580
  0.7 27.8 %copy-start.26 = (bf16[128,768]{1,0:T(8,128)(2,1)S(1)}, bf16[128,768]{1,0:T(8,128)(2,1)}, u32[]{:S(2)}) copy-start(bf16[128,768]{1,0:T(8,128)(2,1)} %param.20) | copy-start | bytes 589828
  0.7 32.0 %collective-permute-start.9 = (bf16[128,1024]{1,0:T(8,128)(2,1)}, bf16[128,1024]{1,0:T(8,128)(2,1)S(1)}, u32[]{:S(2)}, u32[]{:S(2)}) collective-permute-start(bf16[128,1024]{1,0:T(8,128)(2,1)} %bitcast.285), channel_id=1, source_target_pairs={{0,3},{1,2},{2,1},{3,0},{4,7},{5,6},{6,5},{7,4},{8,11},{9,10},{10,... | collective-permute-start | bytes 786440 | tf_op jit(solution)/shard_map/ppermute | solution.py:338
  5.8 27.7 %collective-permute-start.8 = (bf16[128,1024]{1,0:T(8,128)(2,1)}, bf16[128,1024]{1,0:T(8,128)(2,1)S(1)}, u32[]{:S(2)}, u32[]{:S(2)}) collective-permute-start(bf16[128,1024]{1,0:T(8,128)(2,1)} %bitcast.286), channel_id=1, source_target_pairs={{0,2},{1,3},{2,0},{3,1},{4,6},{5,7},{6,4},{7,5},{8,10},{9,11},{10,... | collective-permute-start | bytes 786440 | tf_op jit(solution)/shard_map/ppermute | solution.py:338
  5.8 28.8 %collective-permute-start.7 = (bf16[128,1024]{1,0:T(8,128)(2,1)}, bf16[128,1024]{1,0:T(8,128)(2,1)S(1)}, u32[]{:S(2)}, u32[]{:S(2)}) collective-permute-start(bf16[128,1024]{1,0:T(8,128)(2,1)} %bitcast.287), channel_id=1, source_target_pairs={{0,1},{1,0},{2,3},{3,2},{4,5},{5,4},{6,7},{7,6},{8,9},{9,8},{10,11... | collective-permute-start | bytes 786440 | tf_op jit(solution)/shard_map/ppermute | solution.py:338
  8.1 15.0 %collective-permute-start = (bf16[15,128]{1,0:T(8,128)(2,1)S(1)}, bf16[15,128]{1,0:T(8,128)(2,1)S(1)}, u32[]{:S(2)}, u32[]{:S(2)}) collective-permute-start(bf16[15,128]{1,0:T(8,128)(2,1)S(1)} %dynamic_update_slice.11), channel_id=1, source_target_pairs={{0,1},{1,0},{2,3},{3,2},{4,5},{5,4},{6,7},{7,6},{8,9},{9,8},{10,11... | collective-permute-start | bytes 11528 | tf_op jit(solution)/shard_map/ppermute | solution.py:338
  18.3 17.9 %copy-start.6 = (bf16[1,128,1024]{2,1,0:T(8,128)(2,1)S(1)}, bf16[1,128,1024]{2,1,0:T(8,128)(2,1)}, u32[]{:S(2)}) copy-start(bf16[1,128,1024]{2,1,0:T(8,128)(2,1)} %param.16) | copy-start | bytes 786436
  18.3 18.6 %collective-permute-start.10 = (bf16[128,2304]{1,0:T(8,128)(2,1)S(1)}, bf16[128,2304]{1,0:T(8,128)(2,1)S(1)}, u32[]{:S(2)}, u32[]{:S(2)}) collective-permute-start(bf16[128,2304]{1,0:T(8,128)(2,1)S(1)} %constant_dynamic-update-slice_fusion.23), channel_id=1, source_target_pairs={{0,4},{4,0},{8,12},{12,8},{16,20},{20,16},{24,28},{28,24},{1,5},{5... | collective-permute-start | bytes 1769480 | tf_op jit(solution)/shard_map/ppermute | solution.py:323
  23.3 5.2 %collective-permute-start.1 = (bf16[15,128]{1,0:T(8,128)(2,1)S(1)}, bf16[15,128]{1,0:T(8,128)(2,1)S(1)}, u32[]{:S(2)}, u32[]{:S(2)}) collective-permute-start(bf16[15,128]{1,0:T(8,128)(2,1)S(1)} %add.282), channel_id=1, source_target_pairs={{0,2},{1,3},{2,0},{3,1},{4,6},{5,7},{6,4},{7,5},{8,10},{9,11},{10,... | collective-permute-start | bytes 11528 | tf_op jit(solution)/shard_map/ppermute | solution.py:338
  28.6 1.6 collective-permute-start.2
  30.1 56.1 %collective-permute-start.20 = (bf16[128,1024]{1,0:T(8,128)(2,1)}, bf16[128,1024]{1,0:T(8,128)(2,1)}, u32[]{:S(2)}, u32[]{:S(2)}) collective-permute-start(bf16[128,1024]{1,0:T(8,128)(2,1)} %bitcast.61), channel_id=1, source_target_pairs={{0,3},{1,2},{2,1},{3,0},{4,7},{5,6},{6,5},{7,4},{8,11},{9,10},{10,... | collective-permute-start | bytes 786440 | tf_op jit(solution)/shard_map/ppermute | solution.py:338
  32.7 20.8 %copy-start.16 = (bf16[128,1024]{1,0:T(8,128)(2,1)}, bf16[128,1024]{1,0:T(8,128)(2,1)S(1)}, u32[]{:S(2)}) copy-start(bf16[128,1024]{1,0:T(8,128)(2,1)S(1)} %collective-permute-done.9) | copy-start | bytes 786436
  32.7 53.5 %collective-permute-start.19 = (bf16[128,1024]{1,0:T(8,128)(2,1)}, bf16[128,1024]{1,0:T(8,128)(2,1)}, u32[]{:S(2)}, u32[]{:S(2)}) collective-permute-start(bf16[128,1024]{1,0:T(8,128)(2,1)} %bitcast.61), channel_id=1, source_target_pairs={{0,2},{1,3},{2,0},{3,1},{4,6},{5,7},{6,4},{7,5},{8,10},{9,11},{10,... | collective-permute-start | bytes 786440 | tf_op jit(solution)/shard_map/ppermute | solution.py:338
  33.6 19.9 %copy-start.18 = (bf16[128,1024]{1,0:T(8,128)(2,1)}, bf16[128,1024]{1,0:T(8,128)(2,1)S(1)}, u32[]{:S(2)}) copy-start(bf16[128,1024]{1,0:T(8,128)(2,1)S(1)} %collective-permute-done.8) | copy-start | bytes 786436
  33.6 52.6 %collective-permute-start.18 = (bf16[128,1024]{1,0:T(8,128)(2,1)}, bf16[128,1024]{1,0:T(8,128)(2,1)}, u32[]{:S(2)}, u32[]{:S(2)}) collective-permute-start(bf16[128,1024]{1,0:T(8,128)(2,1)} %bitcast.61), channel_id=1, source_target_pairs={{0,1},{1,0},{2,3},{3,2},{4,5},{5,4},{6,7},{7,6},{8,9},{9,8},{10,11... | collective-permute-start | bytes 786440 | tf_op jit(solution)/shard_map/ppermute | solution.py:338
  34.7 18.8 %copy-start.20 = (bf16[128,1024]{1,0:T(8,128)(2,1)}, bf16[128,1024]{1,0:T(8,128)(2,1)S(1)}, u32[]{:S(2)}) copy-start(bf16[128,1024]{1,0:T(8,128)(2,1)S(1)} %collective-permute-done.7) | copy-start | bytes 786436
  34.7 8.5 %collective-permute-start.3 = (bf16[2,128,896]{2,1,0:T(8,128)(2,1)S(1)}, bf16[2,128,896]{2,1,0:T(8,128)(2,1)S(1)}, u32[]{:S(2)}, u32[]{:S(2)}) collective-permute-start(bf16[2,128,896]{2,1,0:T(8,128)(2,1)S(1)} %pad_maximum_fusion.33), channel_id=1, source_target_pairs={{0,8},{4,20},{8,0},{12,28},{16,24},{20,4},{24,16},{28,12},{1,9},{5... | collective-permute-start | bytes 1376264 | tf_op jit(solution)/shard_map/ppermute | solution.py:328
  36.4 17.1 %copy-start.58 = (f32[512]{0:T(512)}, f32[512]{0:T(512)S(1)}, u32[]{:S(2)}) copy-start(f32[512]{0:T(512)S(1)} %broadcast_multiply_fusion) | copy-start | bytes 6148
  36.8 16.7 %copy-start.69 = (f32[512]{0:T(512)}, f32[512]{0:T(512)S(1)}, u32[]{:S(2)}) copy-start(f32[512]{0:T(512)S(1)} %add_rsqrt_fusion) | copy-start | bytes 6148
  43.2 6.1 %collective-permute-start.5 = (bf16[128,896]{1,0:T(8,128)(2,1)S(1)}, bf16[128,896]{1,0:T(8,128)(2,1)S(1)}, u32[]{:S(2)}, u32[]{:S(2)}) collective-permute-start(bf16[128,896]{1,0:T(8,128)(2,1)S(1)} %slice_bitcast_fusion.7), channel_id=1, source_target_pairs={{0,16},{4,12},{8,24},{12,4},{16,0},{20,28},{24,8},{28,20},{1,17},{... | collective-permute-start | bytes 688136 | tf_op jit(solution)/shard_map/ppermute | solution.py:333
  44.8 6.0 %collective-permute-start.4 = (bf16[2,128,896]{2,1,0:T(8,128)(2,1)S(1)}, bf16[2,128,896]{2,1,0:T(8,128)(2,1)S(1)}, u32[]{:S(2)}, u32[]{:S(2)}) collective-permute-start(bf16[2,128,896]{2,1,0:T(8,128)(2,1)S(1)} %collective-permute-done.3), channel_id=1, source_target_pairs={{0,4},{4,0},{8,12},{12,8},{16,20},{20,16},{24,28},{28,24},{1,5},{5... | collective-permute-start | bytes 1376264 | tf_op jit(solution)/shard_map/ppermute | solution.py:323
  49.3 16.5 %collective-permute-start.11 = (bf16[2,128,2304]{2,1,0:T(8,128)(2,1)}, bf16[2,128,2304]{2,1,0:T(8,128)(2,1)}, u32[]{:S(2)}, u32[]{:S(2)}) collective-permute-start(bf16[2,128,2304]{2,1,0:T(8,128)(2,1)} %pad_maximum_fusion.2), channel_id=1, source_target_pairs={{0,8},{4,20},{8,0},{12,28},{16,24},{20,4},{24,16},{28,12},{1,9},{5... | collective-permute-start | bytes 3538952 | tf_op jit(solution)/shard_map/ppermute | solution.py:328
  50.8 1.5 collective-permute-start.6
  57.3 9.7 %copy-start.24 = (bf16[4,128,4,48]{1,3,2,0:T(8,128)(2,1)}, bf16[4,128,4,48]{1,3,2,0:T(8,128)(2,1)S(1)}, u32[]{:S(2)}) copy-start(bf16[4,128,4,48]{1,3,2,0:T(8,128)(2,1)S(1)} %slice.1898) | copy-start | bytes 589828
  57.7 9.2 %copy-start.43 = (bf16[4,128,4,16]{1,3,2,0:T(8,128)(2,1)}, bf16[4,128,4,16]{1,3,2,0:T(8,128)(2,1)S(1)}, u32[]{:S(2)}) copy-start(bf16[4,128,4,16]{1,3,2,0:T(8,128)(2,1)S(1)} %get-tuple-element.267) | copy-start | bytes 196612
  57.7 9.2 %copy-start.45 = (bf16[4,128,4,16]{1,3,2,0:T(8,128)(2,1)}, bf16[4,128,4,16]{1,3,2,0:T(8,128)(2,1)S(1)}, u32[]{:S(2)}) copy-start(bf16[4,128,4,16]{1,3,2,0:T(8,128)(2,1)S(1)} %get-tuple-element.266) | copy-start | bytes 196612
  65.8 11.1 %collective-permute-start.12 = (bf16[2,128,2304]{2,1,0:T(8,128)(2,1)}, bf16[2,128,2304]{2,1,0:T(8,128)(2,1)S(1)}, u32[]{:S(2)}, u32[]{:S(2)}) collective-permute-start(bf16[2,128,2304]{2,1,0:T(8,128)(2,1)} %collective-permute-done.11), channel_id=1, source_target_pairs={{0,4},{4,0},{8,12},{12,8},{16,20},{20,16},{24,28},{28,24},{1,5},{5... | collective-permute-start | bytes 3538952 | tf_op jit(solution)/shard_map/ppermute | solution.py:323
  66.9 9.9 %collective-permute-start.13 = (bf16[128,2304]{1,0:T(8,128)(2,1)S(1)}, bf16[128,2304]{1,0:T(8,128)(2,1)S(1)}, u32[]{:S(2)}, u32[]{:S(2)}) collective-permute-start(bf16[128,2304]{1,0:T(8,128)(2,1)S(1)} %slice_bitcast_fusion.2), channel_id=1, source_target_pairs={{0,16},{4,12},{8,24},{12,4},{16,0},{20,28},{24,8},{28,20},{1,17},{... | collective-permute-start | bytes 1769480 | tf_op jit(solution)/shard_map/ppermute | solution.py:333
  76.9 2.6 %collective-permute-start.14 = (bf16[128,2304]{1,0:T(8,128)(2,1)S(1)}, bf16[128,2304]{1,0:T(8,128)(2,1)S(1)}, u32[]{:S(2)}, u32[]{:S(2)}) collective-permute-start(bf16[128,2304]{1,0:T(8,128)(2,1)S(1)} %collective-permute-done.13), channel_id=1, source_target_pairs={{0,4},{4,0},{8,12},{12,8},{16,20},{20,16},{24,28},{28,24},{1,5},{5... | collective-permute-start | bytes 1769480 | tf_op jit(solution)/shard_map/ppermute | solution.py:323
  84.8 3.8 %copy-start.35 = (bf16[128,1024]{1,0:T(8,128)(2,1)}, bf16[128,1024]{1,0:T(8,128)(2,1)S(1)}, u32[]{:S(2)}) copy-start(bf16[128,1024]{1,0:T(8,128)(2,1)S(1)} %get-tuple-element.206) | copy-start | bytes 786436
  94.2 4.2 %copy-start.42 = (f32[4,128,16]{1,2,0:T(8,128)S(1)}, f32[4,128,16]{1,2,0:T(8,128)}, u32[]{:S(2)}) copy-start(f32[4,128,16]{1,2,0:T(8,128)} %pad_maximum_fusion.43) | copy-start | bytes 98308
  98.4 31.3 %copy-start.14 = (bf16[4,128,4,64]{1,0,3,2:T(4,128)(2,1)}, bf16[4,128,4,64]{1,0,3,2:T(4,128)(2,1)S(1)}, u32[]{:S(2)}) copy-start(bf16[4,128,4,64]{1,0,3,2:T(4,128)(2,1)S(1)} %copy.91) | copy-start | bytes 786436
  103.0 11.8 %copy-start.77 = (bf16[512,1024]{1,0:T(8,128)(2,1)}, bf16[512,1024]{1,0:T(8,128)(2,1)S(1)}, u32[]{:S(2)}) copy-start(bf16[512,1024]{1,0:T(8,128)(2,1)S(1)} %get-tuple-element.290) | copy-start | bytes 3145732
  108.4 24.2 %collective-permute-start.23 = (bf16[128,1024]{1,0:T(8,128)(2,1)S(1)}, bf16[128,1024]{1,0:T(8,128)(2,1)S(1)}, u32[]{:S(2)}, u32[]{:S(2)}) collective-permute-start(bf16[128,1024]{1,0:T(8,128)(2,1)S(1)} %get-tuple-element.198), channel_id=1, source_target_pairs={{0,3},{1,2},{2,1},{3,0},{4,7},{5,6},{6,5},{7,4},{8,11},{9,10},{10,... | collective-permute-start | bytes 786440 | tf_op jit(solution)/shard_map/ppermute | solution.py:338
  111.0 23.4 %collective-permute-start.22 = (bf16[128,1024]{1,0:T(8,128)(2,1)S(1)}, bf16[128,1024]{1,0:T(8,128)(2,1)S(1)}, u32[]{:S(2)}, u32[]{:S(2)}) collective-permute-start(bf16[128,1024]{1,0:T(8,128)(2,1)S(1)} %get-tuple-element.199), channel_id=1, source_target_pairs={{0,2},{1,3},{2,0},{3,1},{4,6},{5,7},{6,4},{7,5},{8,10},{9,11},{10,... | collective-permute-start | bytes 786440 | tf_op jit(solution)/shard_map/ppermute | solution.py:338
  111.0 23.4 %collective-permute-start.21 = (bf16[128,1024]{1,0:T(8,128)(2,1)S(1)}, bf16[128,1024]{1,0:T(8,128)(2,1)S(1)}, u32[]{:S(2)}, u32[]{:S(2)}) collective-permute-start(bf16[128,1024]{1,0:T(8,128)(2,1)S(1)} %get-tuple-element.197), channel_id=1, source_target_pairs={{0,1},{1,0},{2,3},{3,2},{4,5},{5,4},{6,7},{7,6},{8,9},{9,8},{10,11... | collective-permute-start | bytes 786440 | tf_op jit(solution)/shard_map/ppermute | solution.py:338
  137.1 13.5 %collective-permute-start.24 = (f32[5,1024]{0,1:T(8,128)S(1)}, f32[5,1024]{0,1:T(8,128)S(1)}, u32[]{:S(2)}, u32[]{:S(2)}) collective-permute-start(f32[5,1024]{0,1:T(8,128)S(1)} %copy.103), channel_id=1, source_target_pairs={{0,1},{1,0},{2,3},{3,2},{4,5},{5,4},{6,7},{7,6},{8,9},{9,8},{10,11... | collective-permute-start | bytes 61448 | tf_op jit(solution)/shard_map/ppermute | solution.py:338
  150.7 27.3 %copy-start.33 = (bf16[128,768]{0,1:T(8,128)(2,1)S(1)}, bf16[128,768]{0,1:T(8,128)(2,1)}, u32[]{:S(2)}) copy-start(bf16[128,768]{0,1:T(8,128)(2,1)} %get-tuple-element.190) | copy-start | bytes 589828
  150.7 28.3 %copy-start.32 = (bf16[128,768]{0,1:T(8,128)(2,1)S(1)}, bf16[128,768]{0,1:T(8,128)(2,1)}, u32[]{:S(2)}) copy-start(bf16[128,768]{0,1:T(8,128)(2,1)} %get-tuple-element.189) | copy-start | bytes 589828
  150.7 24.9 %collective-permute-start.25 = (f32[5,1024]{0,1:T(8,128)S(1)}, f32[5,1024]{0,1:T(8,128)}, u32[]{:S(2)}, u32[]{:S(2)}) collective-permute-start(f32[5,1024]{0,1:T(8,128)S(1)} %add.334), channel_id=1, source_target_pairs={{0,2},{1,3},{2,0},{3,1},{4,6},{5,7},{6,4},{7,5},{8,10},{9,11},{10,... | collective-permute-start | bytes 61448 | tf_op jit(solution)/shard_map/ppermute | solution.py:338
  151.5 28.4 %copy-start.31 = (bf16[128,768]{0,1:T(8,128)(2,1)S(1)}, bf16[128,768]{0,1:T(8,128)(2,1)}, u32[]{:S(2)}) copy-start(bf16[128,768]{0,1:T(8,128)(2,1)} %get-tuple-element.188) | copy-start | bytes 589828
  151.5 28.4 %copy-start.51 = (bf16[128,128]{0,1:T(8,128)(2,1)S(1)}, bf16[128,128]{0,1:T(8,128)(2,1)}, u32[]{:S(2)}) copy-start(bf16[128,128]{0,1:T(8,128)(2,1)} %get-tuple-element.238) | copy-start | bytes 98308
  151.5 28.4 %copy-start.52 = (bf16[128,128]{0,1:T(8,128)(2,1)S(1)}, bf16[128,128]{0,1:T(8,128)(2,1)}, u32[]{:S(2)}) copy-start(bf16[128,128]{0,1:T(8,128)(2,1)} %get-tuple-element.239) | copy-start | bytes 98308
  151.9 28.1 %copy-start.30 = (bf16[128,768]{0,1:T(8,128)(2,1)S(1)}, bf16[128,768]{0,1:T(8,128)(2,1)}, u32[]{:S(2)}) copy-start(bf16[128,768]{0,1:T(8,128)(2,1)} %get-tuple-element.187) | copy-start | bytes 589828
  151.9 28.1 %copy-start.49 = (bf16[128,128]{0,1:T(8,128)(2,1)S(1)}, bf16[128,128]{0,1:T(8,128)(2,1)}, u32[]{:S(2)}) copy-start(bf16[128,128]{0,1:T(8,128)(2,1)} %get-tuple-element.236) | copy-start | bytes 98308
  151.9 28.1 %copy-start.50 = (bf16[128,128]{0,1:T(8,128)(2,1)S(1)}, bf16[128,128]{0,1:T(8,128)(2,1)}, u32[]{:S(2)}) copy-start(bf16[128,128]{0,1:T(8,128)(2,1)} %get-tuple-element.237) | copy-start | bytes 98308
  176.8 3.5 %copy-start.28 = (bf16[128,768]{0,1:T(8,128)(2,1)S(1)}, bf16[128,768]{0,1:T(8,128)(2,1)}, u32[]{:S(2)}) copy-start(bf16[128,768]{0,1:T(8,128)(2,1)} %get-tuple-element.185) | copy-start | bytes 589828
  181.0 11.5 %collective-permute-start.26 = (bf16[4,128,1152]{1,2,0:T(8,128)(2,1)S(1)}, bf16[4,128,1152]{1,2,0:T(8,128)(2,1)S(1)}, u32[]{:S(2)}, u32[]{:S(2)}) collective-permute-start(bf16[4,128,1152]{1,2,0:T(8,128)(2,1)S(1)} %pad_maximum_fusion.3), channel_id=1, source_target_pairs={{0,4},{4,0},{8,12},{12,8},{16,20},{20,16},{24,28},{28,24},{1,5},{5... | collective-permute-start | bytes 3538952 | tf_op jit(solution)/shard_map/ppermute | solution.py:323
  182.6 11.9 %collective-permute-start.30 = (bf16[4,128,2048]{1,2,0:T(8,128)(2,1)S(1)}, bf16[4,128,2048]{1,2,0:T(8,128)(2,1)S(1)}, u32[]{:S(2)}, u32[]{:S(2)}) collective-permute-start(bf16[4,128,2048]{1,2,0:T(8,128)(2,1)S(1)} %pad_maximum_fusion), channel_id=1, source_target_pairs={{0,4},{4,0},{8,12},{12,8},{16,20},{20,16},{24,28},{28,24},{1,5},{5... | collective-permute-start | bytes 6291464 | tf_op jit(solution)/shard_map/ppermute | solution.py:323
  188.1 25.2 %collective-permute-start.17 = (bf16[128,1024]{1,0:T(8,128)(2,1)}, bf16[128,1024]{1,0:T(8,128)(2,1)}, u32[]{:S(2)}, u32[]{:S(2)}) collective-permute-start(bf16[128,1024]{1,0:T(8,128)(2,1)} %get-tuple-element.201), channel_id=1, source_target_pairs={{0,3},{1,2},{2,1},{3,0},{4,7},{5,6},{6,5},{7,4},{8,11},{9,10},{10,... | collective-permute-start | bytes 786440 | tf_op jit(solution)/shard_map/ppermute | solution.py:338
  189.8 23.5 %collective-permute-start.16 = (bf16[128,1024]{1,0:T(8,128)(2,1)}, bf16[128,1024]{1,0:T(8,128)(2,1)}, u32[]{:S(2)}, u32[]{:S(2)}) collective-permute-start(bf16[128,1024]{1,0:T(8,128)(2,1)} %get-tuple-element.202), channel_id=1, source_target_pairs={{0,2},{1,3},{2,0},{3,1},{4,6},{5,7},{6,4},{7,5},{8,10},{9,11},{10,... | collective-permute-start | bytes 786440 | tf_op jit(solution)/shard_map/ppermute | solution.py:338
  189.8 23.5 %collective-permute-start.15 = (bf16[128,1024]{1,0:T(8,128)(2,1)}, bf16[128,1024]{1,0:T(8,128)(2,1)}, u32[]{:S(2)}, u32[]{:S(2)}) collective-permute-start(bf16[128,1024]{1,0:T(8,128)(2,1)} %get-tuple-element.200), channel_id=1, source_target_pairs={{0,1},{1,0},{2,3},{3,2},{4,5},{5,4},{6,7},{7,6},{8,9},{9,8},{10,11... | collective-permute-start | bytes 786440 | tf_op jit(solution)/shard_map/ppermute | solution.py:338
  192.9 6.8 %collective-permute-start.27 = (bf16[128,1152]{0,1:T(8,128)(2,1)S(1)}, bf16[128,1152]{0,1:T(8,128)(2,1)S(1)}, u32[]{:S(2)}, u32[]{:S(2)}) collective-permute-start(bf16[128,1152]{0,1:T(8,128)(2,1)S(1)} %get-tuple-element.194), channel_id=1, source_target_pairs={{0,16},{4,12},{8,24},{12,4},{16,0},{20,28},{24,8},{28,20},{1,17},{... | collective-permute-start | bytes 884744 | tf_op jit(solution)/shard_map/ppermute | solution.py:333
  195.1 14.6 %copy-start = (f32[4,128,2048]{1,2,0:T(8,128)}, f32[4,128,2048]{1,2,0:T(8,128)S(1)}, u32[]{:S(2)}) copy-start(f32[4,128,2048]{1,2,0:T(8,128)S(1)} %get-tuple-element.79) | copy-start | bytes 12582916
  195.2 14.5 %collective-permute-start.31 = (bf16[128,2048]{0,1:T(8,128)(2,1)S(1)}, bf16[128,2048]{0,1:T(8,128)(2,1)S(1)}, u32[]{:S(2)}, u32[]{:S(2)}) collective-permute-start(bf16[128,2048]{0,1:T(8,128)(2,1)S(1)} %get-tuple-element.98), channel_id=1, source_target_pairs={{0,16},{4,12},{8,24},{12,4},{16,0},{20,28},{24,8},{28,20},{1,17},{... | collective-permute-start | bytes 1572872 | tf_op jit(solution)/shard_map/ppermute | solution.py:333
  199.8 12.5 %collective-permute-start.28 = (bf16[2,128,1152]{1,2,0:T(8,128)(2,1)S(1)}, bf16[2,128,1152]{1,2,0:T(8,128)(2,1)S(1)}, u32[]{:S(2)}, u32[]{:S(2)}) collective-permute-start(bf16[2,128,1152]{1,2,0:T(8,128)(2,1)S(1)} %pad_maximum_fusion.31), channel_id=1, source_target_pairs={{0,8},{4,20},{8,0},{12,28},{16,24},{20,4},{24,16},{28,12},{1,9},{5... | collective-permute-start | bytes 1769480 | tf_op jit(solution)/shard_map/ppermute | solution.py:328
  209.7 3.6 %copy-start.57 = (f32[1,8,128]{2,0,1:T(1,128)S(1)}, f32[1,8,128]{2,0,1:T(1,128)}, u32[]{:S(2)}) copy-start(f32[1,8,128]{2,0,1:T(1,128)} %get-tuple-element.272) | copy-start | bytes 12292
  210.9 15.1 %collective-permute-start.32 = (bf16[2,128,2048]{1,2,0:T(8,128)(2,1)}, bf16[2,128,2048]{1,2,0:T(8,128)(2,1)}, u32[]{:S(2)}, u32[]{:S(2)}) collective-permute-start(bf16[2,128,2048]{1,2,0:T(8,128)(2,1)} %pad_maximum_fusion.14), channel_id=1, source_target_pairs={{0,8},{4,20},{8,0},{12,28},{16,24},{20,4},{24,16},{28,12},{1,9},{5... | collective-permute-start | bytes 3145736 | tf_op jit(solution)/shard_map/ppermute | solution.py:328
  213.2 2.3 collective-permute-start.29
  227.1 3.0 %collective-permute-start.33 = (bf16[128,2048]{0,1:T(8,128)(2,1)S(1)}, bf16[128,2048]{0,1:T(8,128)(2,1)S(1)}, u32[]{:S(2)}, u32[]{:S(2)}) collective-permute-start(bf16[128,2048]{0,1:T(8,128)(2,1)S(1)} %slice_bitcast_fusion.3), channel_id=1, source_target_pairs={{0,4},{4,0},{8,12},{12,8},{16,20},{20,16},{24,28},{28,24},{1,5},{5... | collective-permute-start | bytes 1572872 | tf_op jit(solution)/shard_map/ppermute | solution.py:323
  228.8 4.9 %copy-start.73 = (f32[32]{0:T(128)}, f32[32]{0:T(128)S(1)}, u32[]{:S(2)}) copy-start(f32[32]{0:T(128)S(1)} %get-tuple-element.329) | copy-start | bytes 388
  (50 other events, 81.0 us)

commit v2 on v0

--- a/solution.py
+++ b/solution.py
@@ -1,6 +1,10 @@
+import functools
+
 import jax
 import jax.numpy as jnp
 from jax import lax
+from jax.experimental import pallas as pl
+from jax.experimental.pallas import tpu as pltpu
 from jax.sharding import PartitionSpec as P
 
 H = 16
@@ -13,6 +17,10 @@
 ROOT_HALF = 0.7071067811865476
 INV_ROOT_TAU = 0.3989422804014327
 MASKED = -1e30
+UNROLL = True
+FSDP = "fsdp"
+TENSOR = "tensor"
+VMEM_LIMIT = 18 * 1024 * 1024
 
 
 def normalize_rows(token_row_block):
@@ -86,7 +94,7 @@
     return jnp.where(mask, product * scale, MASKED)
 
 
-def shards(
+def plain_shards(
     layer_input,
     out_grad,
     segments,
@@ -105,31 +113,31 @@
     feedforward_norm_bias,
 ):
     attention_gain, attention_bias, feedforward_gain, feedforward_bias, bias_dense, bias_outer = (
-        lax.all_gather(attention_norm_gain, ("fsdp", "tensor"), axis=0, tiled=True),
-        lax.all_gather(attention_norm_bias, ("fsdp", "tensor"), axis=0, tiled=True),
-        lax.all_gather(feedforward_norm_gain, ("fsdp", "tensor"), axis=0, tiled=True),
-        lax.all_gather(feedforward_norm_bias, ("fsdp", "tensor"), axis=0, tiled=True),
-        lax.all_gather(dense_bias, ("fsdp", "tensor"), axis=0, tiled=True),
-        lax.all_gather(outer_bias, ("fsdp", "tensor"), axis=0, tiled=True),
+        lax.all_gather(attention_norm_gain, (FSDP, TENSOR), axis=0, tiled=True),
+        lax.all_gather(attention_norm_bias, (FSDP, TENSOR), axis=0, tiled=True),
+        lax.all_gather(feedforward_norm_gain, (FSDP, TENSOR), axis=0, tiled=True),
+        lax.all_gather(feedforward_norm_bias, (FSDP, TENSOR), axis=0, tiled=True),
+        lax.all_gather(dense_bias, (FSDP, TENSOR), axis=0, tiled=True),
+        lax.all_gather(outer_bias, (FSDP, TENSOR), axis=0, tiled=True),
     )
     scale = HD ** (-0.5)
     microbatch = 0
     weights = unpack(
         (
-            lax.all_gather(qkv_weight, "fsdp", axis=0, tiled=True),
-            lax.all_gather(qkv_bias, "fsdp", axis=1, tiled=True),
-            lax.all_gather(dense_weight, "fsdp", axis=1, tiled=True),
-            lax.all_gather(inner_weight, "fsdp", axis=0, tiled=True),
-            lax.all_gather(inner_bias, "fsdp", axis=1, tiled=True),
-            lax.all_gather(outer_weight, "fsdp", axis=1, tiled=True),
+            lax.all_gather(qkv_weight, FSDP, axis=0, tiled=True),
+            lax.all_gather(qkv_bias, FSDP, axis=1, tiled=True),
+            lax.all_gather(dense_weight, FSDP, axis=1, tiled=True),
+            lax.all_gather(inner_weight, FSDP, axis=0, tiled=True),
+            lax.all_gather(inner_bias, FSDP, axis=1, tiled=True),
+            lax.all_gather(outer_weight, FSDP, axis=1, tiled=True),
         )
     )
     qkv_w, qkv_b, dense_w, inner_w, inner_b, outer_w = weights
-    token_row_block = lax.all_gather(layer_input[microbatch], "tensor", axis=0, tiled=True)
+    token_row_block = lax.all_gather(layer_input[microbatch], TENSOR, axis=0, tiled=True)
     segs = segments[microbatch]
     seqs, length = segs.shape
     heads = qkv_w.shape[1] // (3 * HD)
-    normalized_input, unused_result = normalize_rows(token_row_block)
+    normalized_input, _ = normalize_rows(token_row_block)
     first_branch = (normalized_input * attention_gain + attention_bias).astype(jnp.bfloat16)
     second_branch = (normalized_input * feedforward_gain + feedforward_bias).astype(jnp.bfloat16)
     packed = (jnp.dot(first_branch, qkv_w, preferred_element_type=jnp.float32) + qkv_b).reshape(
@@ -157,7 +165,7 @@
             jnp.dot(ctx_rows, dense_w, preferred_element_type=jnp.float32)
             + jnp.dot(act_rows, outer_w, preferred_element_type=jnp.float32)
         ).astype(jnp.bfloat16),
-        "tensor",
+        TENSOR,
         scatter_dimension=0,
         tiled=True,
     ).astype(jnp.float32)
@@ -186,12 +194,12 @@
     microbatch = 0
     weights = unpack(
         (
-            lax.all_gather(qkv_weight, "fsdp", axis=0, tiled=True),
-            lax.all_gather(qkv_bias, "fsdp", axis=1, tiled=True),
-            lax.all_gather(dense_weight, "fsdp", axis=1, tiled=True),
-            lax.all_gather(inner_weight, "fsdp", axis=0, tiled=True),
-            lax.all_gather(inner_bias, "fsdp", axis=1, tiled=True),
-            lax.all_gather(outer_weight, "fsdp", axis=1, tiled=True),
+            lax.all_gather(qkv_weight, FSDP, axis=0, tiled=True),
+            lax.all_gather(qkv_bias, FSDP, axis=1, tiled=True),
+            lax.all_gather(dense_weight, FSDP, axis=1, tiled=True),
+            lax.all_gather(inner_weight, FSDP, axis=0, tiled=True),
+            lax.all_gather(inner_bias, FSDP, axis=1, tiled=True),
+            lax.all_gather(outer_weight, FSDP, axis=1, tiled=True),
         )
     )
     qkv_w, qkv_b, dense_w, inner_w, inner_b, outer_w = weights
@@ -211,7 +219,7 @@
     segs = segments[microbatch]
     seqs, length = segs.shape
     heads = qkv_w.shape[1] // (3 * HD)
-    cot_rows = lax.all_gather(out_grad[microbatch], "tensor", axis=0, tiled=True)
+    cot_rows = lax.all_gather(out_grad[microbatch], TENSOR, axis=0, tiled=True)
     own_cot = out_grad[microbatch].astype(jnp.float32)
     g_bias = jnp.sum(own_cot, 0)
     d_act = matmul(cot_rows, outer_w, 1, 1)
@@ -250,10 +258,10 @@
     first_branch_gradient = matmul(d_packed_b, qkv_w, 1, 1)
     local_normalized_input, local_inverse_deviation = normalize_rows(layer_input[microbatch])
     local_first_branch = lax.psum_scatter(
-        first_branch_gradient.astype(jnp.bfloat16), "tensor", scatter_dimension=0, tiled=True
+        first_branch_gradient.astype(jnp.bfloat16), TENSOR, scatter_dimension=0, tiled=True
     ).astype(jnp.float32)
     local_second_branch = lax.psum_scatter(
-        second_branch_gradient.astype(jnp.bfloat16), "tensor", scatter_dimension=0, tiled=True
+        second_branch_gradient.astype(jnp.bfloat16), TENSOR, scatter_dimension=0, tiled=True
     ).astype(jnp.float32)
     attention_gain_gradient = jnp.sum(local_first_branch * local_normalized_input, 0)
     g_shift1 = jnp.sum(local_first_branch, 0)
@@ -271,34 +279,34 @@
     in_grads = [input_gradient.astype(jnp.bfloat16)]
     s_qkv, s_qkv_b, s_dense, s_inner, s_inner_b, s_outer = (
         lax.psum_scatter(
-            g_qkv.astype(jnp.bfloat16), "fsdp", scatter_dimension=0, tiled=True
+            g_qkv.astype(jnp.bfloat16), FSDP, scatter_dimension=0, tiled=True
         ).astype(jnp.float32),
         lax.psum_scatter(
-            g_qkv_b.astype(jnp.bfloat16), "fsdp", scatter_dimension=1, tiled=True
+            g_qkv_b.astype(jnp.bfloat16), FSDP, scatter_dimension=1, tiled=True
         ).astype(jnp.float32),
         lax.psum_scatter(
-            g_dense.astype(jnp.bfloat16), "fsdp", scatter_dimension=1, tiled=True
+            g_dense.astype(jnp.bfloat16), FSDP, scatter_dimension=1, tiled=True
         ).astype(jnp.float32),
         lax.psum_scatter(
-            g_inner.astype(jnp.bfloat16), "fsdp", scatter_dimension=0, tiled=True
+            g_inner.astype(jnp.bfloat16), FSDP, scatter_dimension=0, tiled=True
         ).astype(jnp.float32),
         lax.psum_scatter(
-            g_inner_b.astype(jnp.bfloat16), "fsdp", scatter_dimension=1, tiled=True
+            g_inner_b.astype(jnp.bfloat16), FSDP, scatter_dimension=1, tiled=True
         ).astype(jnp.float32),
         lax.psum_scatter(
-            g_outer.astype(jnp.bfloat16), "fsdp", scatter_dimension=1, tiled=True
+            g_outer.astype(jnp.bfloat16), FSDP, scatter_dimension=1, tiled=True
         ).astype(jnp.float32),
     )
     s_bias, s_gain1, s_shift1, s_gain2, s_shift2 = (
-        lax.psum_scatter(g_bias, ("fsdp", "tensor"), scatter_dimension=0, tiled=True),
+        lax.psum_scatter(g_bias, (FSDP, TENSOR), scatter_dimension=0, tiled=True),
         lax.psum_scatter(
-            attention_gain_gradient, ("fsdp", "tensor"), scatter_dimension=0, tiled=True
+            attention_gain_gradient, (FSDP, TENSOR), scatter_dimension=0, tiled=True
         ),
-        lax.psum_scatter(g_shift1, ("fsdp", "tensor"), scatter_dimension=0, tiled=True),
+        lax.psum_scatter(g_shift1, (FSDP, TENSOR), scatter_dimension=0, tiled=True),
         lax.psum_scatter(
-            feedforward_gain_gradient, ("fsdp", "tensor"), scatter_dimension=0, tiled=True
+            feedforward_gain_gradient, (FSDP, TENSOR), scatter_dimension=0, tiled=True
         ),
-        lax.psum_scatter(g_shift2, ("fsdp", "tensor"), scatter_dimension=0, tiled=True),
+        lax.psum_scatter(g_shift2, (FSDP, TENSOR), scatter_dimension=0, tiled=True),
     )
     return (
         jnp.stack(outputs),
@@ -318,44 +326,657 @@
     )
 
 
+def swap(value, axis, partner):
+    count = lax.axis_size(axis)
+    return lax.ppermute(value, axis, [(i, partner(i)) for i in range(count)])
+
+
+def core_swap(value):
+    return swap(value, FSDP, lambda i: i ^ 1)
+
+
+def near_swap(value):
+    return swap(value, FSDP, lambda i: i ^ (4 if i & 1 else 2))
+
+
+def far_swap(value):
+    return swap(value, FSDP, lambda i: i ^ (2 if i & 1 else 4))
+
+
+def depth_swap(value, mask):
+    return swap(value, TENSOR, lambda i: i ^ mask)
+
+
+def depth_gather(value):
+    second = depth_swap(value, 2)
+    first = depth_swap(value, 1)
+    return [value, first, second, depth_swap(second, 1)]
+
+
+def depth_scatter(parts):
+    third = depth_swap(parts[3], 1)
+    first = depth_swap(parts[1], 1)
+    (second,) = call(
+        one_sum_body, [(third.shape, jnp.bfloat16)], [jnp.zeros((1,), jnp.int32), parts[2], third]
+    )
+    return [parts[0], first, depth_swap(second, 2)]
+
+
+def slot_masks():
+    core = lax.axis_index(FSDP) & 1
+    near = jnp.where(core == 0, 2, 4)
+    far = 6 - near
+    return [0, 1, near, near + 1, far, far + 1, 6, 7]
+
+
+def gather_blocks(shard):
+    partner = core_swap(shard)
+    near_own = near_swap(shard)
+    near_partner = near_swap(partner)
+    across = far_swap(near_own)
+    far_partner = core_swap(near_own)
+    far_own = core_swap(near_partner)
+    across_partner = core_swap(across)
+    return [shard, partner, near_own, near_partner, far_own, far_partner, across, across_partner]
+
+
+def scatter_sum(keep, send):
+    shape = keep.shape[1:]
+    got = core_swap(send)
+    own, near_own, near_partner, across = call(
+        four_sums_body, [(shape, jnp.bfloat16)] * 4, [jnp.zeros((1,), jnp.int32), keep, got]
+    )
+    across = far_swap(across)
+    near_partner = near_swap(near_partner)
+    (near_own,) = call(one_sum_body, [(shape, jnp.bfloat16)], [jnp.zeros((1,), jnp.int32), near_own, across])
+    near_own = near_swap(near_own)
+    far = core_swap(near_partner)
+    return [own, near_own, far]
+
+
+def turn_tables(positions):
+    half = ROT // 2
+    lane = jnp.arange(2 * HD) % HD
+    freq = jnp.power(10000.0, -(lane % half).astype(jnp.float32) * (2.0 / ROT))
+    angle = positions.astype(jnp.float32) * freq
+    sine = jnp.sin(angle)
+    return (
+        jnp.where(lane < ROT, jnp.cos(angle), 1.0),
+        jnp.where(lane < half, -sine, 0.0),
+        jnp.where((lane >= half) & (lane < ROT), sine, 0.0),
+    )
+
+
+def erf_value(value):
+    v = jnp.clip(value, -4.0, 4.0)
+    s = v * v
+    top = jnp.full_like(s, -2.72614225801306e-10)
+    for c in (2.77068142495902e-08, -2.10102402082508e-06, -5.69250639462346e-05, -7.34990630326855e-04, -2.95459980854025e-03, -1.60960333262415e-02):
+        top = top * s + c
+    low = jnp.full_like(s, -1.45660718464996e-05)
+    for c in (-2.13374055278905e-04, -1.68282697438203e-03, -7.37332916720468e-03, -1.42647390514189e-02):
+        low = low * s + c
+    return v * top / low
+
+
+def call(body, outs, ins, scratch=(), final=False, loose=False):
+    specs = [pl.BlockSpec(memory_space=pltpu.SMEM)] + [pl.BlockSpec(memory_space=pltpu.VMEM)] * (len(ins) - 1)
+    return pl.pallas_call(
+        body,
+        out_shape=[jax.ShapeDtypeStruct(*out) if final else pltpu.VMEM(*out) for out in outs],
+        in_specs=specs,
+        out_specs=[pl.BlockSpec(memory_space=pltpu.VMEM)] * len(outs),
+        scratch_shapes=list(scratch),
+        compiler_params=pltpu.CompilerParams(vmem_limit_bytes=VMEM_LIMIT),
+    )(ins[0], *[pltpu.with_memory_space_constraint(a, pltpu.HBM if loose else pltpu.VMEM) for a in ins[1:]])
+
+
+def four_sums_body(scal, keep, got, *outs):
+    for i, out in enumerate(outs):
+        out[...] = (keep[i].astype(jnp.float32) + got[i].astype(jnp.float32)).astype(out.dtype)
+
+
+def one_sum_body(scal, one, two, out):
+    out[...] = (one[...].astype(jnp.float32) + two[...].astype(jnp.float32)).astype(out.dtype)
+
+
+def pack_body(inner, outer, dense, x, g, message, x_copy, g_copy):
+    x_copy[...] = x[...]
+    g_copy[...] = g[...]
+    strip, units = inner.shape
+    message[:, :units] = inner[...]
+    for i in range(outer.shape[0] // strip):
+        message[:, units + strip * i : units + strip * (i + 1)] = outer[strip * i : strip * (i + 1), :]
+    for i in range(dense.shape[0] // strip):
+        message[:, 2 * units + strip * i : 2 * units + strip * (i + 1)] = dense[strip * i : strip * (i + 1), :]
+
+
+def in_three(value):
+    high = value.astype(jnp.bfloat16)
+    rest = value - high.astype(jnp.float32)
+    middle = rest.astype(jnp.bfloat16)
+    return [part.astype(jnp.float32) for part in (high, middle, rest - middle.astype(jnp.float32))]
+
+
+def placed(value, lanes, shift):
+    rows, count = value.shape
+    wide = jnp.concatenate([value, jnp.zeros((rows, lanes - count), value.dtype)], axis=1)
+    return pltpu.roll(wide, shift, 1)
+
+
+def pack_attend_body(scal, *refs):
+    vectors, qkv, qkv_bias, inner_bias, message = refs[:6], refs[6], refs[7], refs[8], refs[9]
+    strip, cols = qkv.shape
+    lanes = vectors[0].shape[1]
+    rows = [ref[...] for ref in vectors[:4]] + [vectors[4][...] + vectors[5][...]]
+    parts = in_three(jnp.concatenate(rows, axis=0))
+    three = jnp.concatenate(parts + [jnp.zeros((1, lanes), jnp.float32)], axis=0)
+    biases = []
+    for ref in (qkv_bias, inner_bias):
+        value = placed(ref[...].astype(jnp.float32), 2 * strip, scal[9] * ref.shape[1])
+        biases += [value[:, :strip], value[:, strip:]]
+    small = jnp.concatenate([placed(three, strip, scal[8] * lanes)] + biases, axis=0)
+    message[:, :cols] = qkv[...]
+    message[:, cols:] = jnp.concatenate(
+        [small, jnp.zeros((strip - small.shape[0], strip), jnp.float32)], axis=0
+    ).astype(jnp.bfloat16)
+
+
+def share_body(cols, scal, *refs):
+    blocks, out = refs[:-1], refs[-1]
+    for i, block in enumerate(blocks):
+        out[i] = block[0:16, cols:]
+
+
+def unpack_big_body(units, wide, scal, own, near, far, inner, outer, dense):
+    total = own[...].astype(jnp.float32) + near[...].astype(jnp.float32) + far[...].astype(jnp.float32)
+    strip = total.shape[0]
+    inner[...] = total[:, :units]
+    for i in range(units // strip):
+        outer[strip * i : strip * (i + 1), :] = total[:, units + strip * i : units + strip * (i + 1)]
+    for i in range(wide // strip):
+        dense[strip * i : strip * (i + 1), :] = total[:, 2 * units + strip * i : 2 * units + strip * (i + 1)]
+
+
+def unpack_rest_body(sizes, scal, own, near, far, qkv, qkv_b, inner_b, *fives):
+    strip, cols, heads, lanes = sizes
+    total = own[...].astype(jnp.float32) + near[...].astype(jnp.float32) + far[...].astype(jnp.float32)
+    qkv[...] = total[:, :cols]
+    tiny = total[:, cols:]
+    for i, out in enumerate((qkv_b, inner_b)):
+        at = 8 + 2 * heads * i
+        pair = jnp.concatenate([tiny[at : at + heads], tiny[at + heads : at + 2 * heads]], axis=1)
+        count = out.shape[1]
+        out[...] = pltpu.roll(pair, 2 * strip - scal[9] * count, 1)[:, :count]
+    for k, out in enumerate(fives):
+        out[...] = pltpu.roll(tiny[0:8], strip - (scal[8] ^ k) * lanes, 1)[:, :lanes]
+
+
+def result_body(m, scal, x, vec, *refs):
+    total = x[...].astype(jnp.float32) + vec[4:5, :]
+    for part in refs[:m]:
+        total = total + part[...].astype(jnp.float32)
+    refs[m][...] = total.astype(refs[m].dtype)
+
+
+def standardize(values):
+    centre = values - jnp.mean(values, -1, keepdims=True)
+    scale = lax.rsqrt(jnp.mean(centre * centre, -1, keepdims=True) + EPS)
+    return centre * scale, scale
+
+
+def rotate(pair, cosine, low, high):
+    lanes = pair.shape[-1]
+    half = ROT // 2
+    return pair * cosine + pltpu.roll(pair, lanes - half, 1) * low + pltpu.roll(pair, half, 1) * high
+
+
+def rotate_back(pair, cosine, low, high):
+    lanes = pair.shape[-1]
+    half = ROT // 2
+    return pair * cosine - pltpu.roll(pair, lanes - half, 1) * low - pltpu.roll(pair, half, 1) * high
+
+
+def attend_body(m, heads, sizes, scal, *refs):
+    strip, qkv_cols = sizes
+    xs, blocks, shares = refs[:m], refs[m : m + 8], refs[m + 8 : 2 * m + 7]
+    segs, cosine, low, high = refs[2 * m + 7 : 2 * m + 11]
+    first, second, turned, probs, context, weight, vec, inner_b, smalls = refs[2 * m + 11 :]
+    count = 8
+    biases = jnp.zeros((4 * heads, strip), jnp.float32)
+    for slot, view in enumerate(blocks):
+        k = scal[slot]
+        weight[pl.ds(pl.multiple_of(k * strip, strip), strip), :] = view[:, :qkv_cols]
+        biases = biases + view[16 : 16 + 4 * heads, qkv_cols:].astype(jnp.float32)
+        part = view[0:16, qkv_cols:].astype(jnp.float32)
+        for share in shares:
+            part = part + share[slot].astype(jnp.float32)
+        smalls[k] = part
+    for k in range(count):
+        s = smalls[k]
+        vec[0:5, strip * k : strip * (k + 1)] = s[0:5] + s[5:10] + s[10:15]
+    rest = 3 * HD - strip
+    qkv_b = jnp.concatenate(
+        [piece for h in range(heads) for piece in (biases[h : h + 1], biases[heads + h : heads + h + 1, :rest])], axis=1
+    )
+    inner_b[...] = jnp.concatenate(
+        [biases[at + h : at + h + 1] for h in range(heads) for at in (2 * heads, 3 * heads)], axis=1
+    )
+    rows = xs[0].shape[0]
+    scale = HD ** (-0.5)
+    after = lax.broadcasted_iota(jnp.int32, (rows, rows), 0) >= lax.broadcasted_iota(jnp.int32, (rows, rows), 1)
+    for s in range(m):
+        at = slice(rows * s, rows * (s + 1))
+        xhat, _ = standardize(xs[s][...].astype(jnp.float32))
+        one = (xhat * vec[0:1, :] + vec[1:2, :]).astype(jnp.bfloat16)
+        first[at, :] = one
+        second[at, :] = (xhat * vec[2:3, :] + vec[3:4, :]).astype(jnp.bfloat16)
+    packed = jnp.dot(first[...], weight[...], preferred_element_type=jnp.float32) + qkv_b
+    cos, lo, hi = cosine[...], low[...], high[...]
+    for h in range(heads):
+        base = 3 * HD * h
+        pair = packed[:, base : base + 2 * HD]
+        turned[:, base : base + 2 * HD] = rotate(pair, cos, lo, hi).astype(jnp.bfloat16)
+        turned[:, base + 2 * HD : base + 3 * HD] = packed[:, base + 2 * HD : base + 3 * HD].astype(jnp.bfloat16)
+    def one_sequence(s, unused):
+        at = pl.ds(pl.multiple_of(s * rows, rows), rows)
+        seg = jnp.broadcast_to(segs[pl.ds(scal[8] ^ s, 1), :].astype(jnp.float32), (rows, rows))
+        mask = (seg == jnp.transpose(seg)) & after
+        for h in range(heads):
+            base = 3 * HD * h
+            query = turned[at, base : base + HD]
+            keyed = turned[at, base + HD : base + 2 * HD]
+            value = turned[at, base + 2 * HD : base + 3 * HD]
+            scores = jnp.where(mask, matmul(query, keyed, 1, 1) * scale, MASKED)
+            peak = jnp.max(scores, -1, keepdims=True)
+            raised = jnp.exp(scores - peak)
+            prob = raised / jnp.sum(raised, -1, keepdims=True)
+            probs[s * heads + h] = prob
+            context[at, HD * h : HD * (h + 1)] = jnp.dot(
+                prob.astype(jnp.bfloat16), value, preferred_element_type=jnp.float32
+            ).astype(jnp.bfloat16)
+        return unused
+
+    lax.fori_loop(0, m, one_sequence, 0, unroll=UNROLL)
+
+
+def feed_body(m, sizes, scal, *refs):
+    strip, units, wide = sizes
+    second, context, inner_b, blocks = refs[0], refs[1], refs[2], refs[3:11]
+    inner, outer, dense, bend, act = refs[11:16]
+    outs = refs[16:]
+    for slot, view in enumerate(blocks):
+        k = scal[slot]
+        at = pl.ds(pl.multiple_of(k * strip, strip), strip)
+        inner[at, :] = view[:, :units]
+        for i in range(units // strip):
+            outer[strip * i : strip * (i + 1), at] = view[:, units + strip * i : units + strip * (i + 1)]
+        for i in range(wide // strip):
+            dense[strip * i : strip * (i + 1), at] = view[:, 2 * units + strip * i : 2 * units + strip * (i + 1)]
+    rows = outs[0].shape[0]
+    for s in range(m):
+        at = slice(rows * s, rows * (s + 1))
+        value = jnp.dot(second[at, :], inner[...], preferred_element_type=jnp.float32) + inner_b[...]
+        half = 0.5 * (1.0 + erf_value(value * ROOT_HALF))
+        act[at, :] = (value * half).astype(jnp.bfloat16)
+        bend[at, :] = half + value * jnp.exp(-0.5 * value * value) * INV_ROOT_TAU
+    for s in range(m):
+        at = slice(rows * s, rows * (s + 1))
+        mixed = jnp.dot(act[at, :], outer[...], preferred_element_type=jnp.float32)
+        mixed = mixed + jnp.dot(context[at, :], dense[...], preferred_element_type=jnp.float32)
+        outs[s][...] = mixed.astype(outs[s].dtype)
+
+
+def destinations(scal, keep, send):
+    places = [(scal[slot], keep.at[j]) for j, slot in enumerate((0, 2, 3, 6))]
+    places += [(scal[slot], send.at[j]) for j, slot in enumerate((1, 5, 4, 7))]
+    return [places[i : i + 2] for i in range(0, len(places), 2)]
+
+
+def two_blocks(source, pair, strip):
+    return jnp.concatenate(
+        [source[:, pl.ds(pl.multiple_of(k * strip, strip), strip)] for k, unused_result in pair], axis=1
+    )
+
+
+def feed_back_body(m, sizes, scal, *refs):
+    strip, units, wide = sizes
+    gs = refs[:m]
+    act, bend, second, context, outer = refs[m : m + 5]
+    keep, send, slope, g_inner_b, cot = refs[m + 5 :]
+    rows = gs[0].shape[0]
+    for s in range(m):
+        cot[rows * s : rows * (s + 1), :] = gs[s][...]
+    pairs = destinations(scal, keep, send)
+    for pair in pairs:
+        columns = two_blocks(cot, pair, strip)
+        for source, count, start in ((act, units, units), (context, wide, 2 * units)):
+            grad = matmul(source[...], columns, 0, 0).astype(jnp.bfloat16)
+            for j, (unused_result, place) in enumerate(pair):
+                for i in range(count // strip):
+                    place[:, start + strip * i : start + strip * (i + 1)] = grad[
+                        strip * i : strip * (i + 1), strip * j : strip * (j + 1)
+                    ]
+    total = jnp.zeros((1, units), jnp.float32)
+    for s in range(m):
+        at = slice(rows * s, rows * (s + 1))
+        grad = matmul(cot[at, :], outer[...], 1, 1) * bend[at, :]
+        total = total + jnp.sum(grad, 0, keepdims=True)
+        slope[at, :] = grad.astype(jnp.bfloat16)
+    g_inner_b[...] = total
+    for pair in pairs:
+        grad = matmul(two_blocks(second, pair, strip), slope[...], 0, 0).astype(jnp.bfloat16)
+        for j, (unused_result, place) in enumerate(pair):
+            place[:, :units] = grad[strip * j : strip * (j + 1)]
+
+
+def attend_back_body(start, stop, heads, scal, *refs):
+    cot, context, dense, turned, probs, cosine, low, high = refs[:8]
+    d_packed_b, qkv_grad, d_packed, d_context = refs[8:]
+    rows = d_context.shape[0] // (stop - start)
+    scale = HD ** (-0.5)
+    d_context[...] = matmul(cot[rows * start : rows * stop, :], dense[...], 1, 1).astype(jnp.bfloat16)
+
+    for s in range(start, stop):
+        at = slice(rows * s, rows * (s + 1))
+        out = slice(rows * (s - start), rows * (s - start + 1))
+        for h in range(heads):
+            base = 3 * HD * h
+            query = turned[at, base : base + HD]
+            keyed = turned[at, base + HD : base + 2 * HD]
+            value = turned[at, base + 2 * HD : base + 3 * HD]
+            d_ctx = d_context[out, HD * h : HD * (h + 1)]
+            ctx = context[at, HD * h : HD * (h + 1)]
+            prob = probs[s * heads + h]
+            delta = jnp.sum(d_ctx.astype(jnp.float32) * ctx.astype(jnp.float32), -1, keepdims=True)
+            d_prob = matmul(d_ctx, value, 1, 1)
+            d_score = (prob * (d_prob - delta)).astype(jnp.bfloat16)
+            d_query = jnp.dot(d_score, keyed, preferred_element_type=jnp.float32) * scale
+            d_key = matmul(d_score, query, 0, 0) * scale
+            pair = rotate_back(
+                jnp.concatenate([d_query, d_key], axis=1), cosine[at, :], low[at, :], high[at, :]
+            )
+            d_packed[out, base : base + 2 * HD] = pair
+            d_packed[out, base + 2 * HD : base + 3 * HD] = matmul(prob.astype(jnp.bfloat16), d_ctx, 0, 0)
+    qkv_grad[...] = jnp.sum(d_packed[...], 0, keepdims=True)
+    d_packed_b[...] = d_packed[...].astype(jnp.bfloat16)
+
+
+def norm_back_body(m, scal, *refs):
+    xs = refs[:m]
+    cot, head_half, tail_half, weight, slope, inner, vec = refs[m : m + 7]
+    outs, five = refs[m + 7 : 2 * m + 7], refs[2 * m + 7]
+    rows, width = xs[0].shape
+    sums = [jnp.zeros((1, width), jnp.float32) for _ in range(4)]
+    for s in range(m):
+        at = slice(rows * s, rows * (s + 1))
+        half, row = (head_half, rows * s) if s < m // 2 else (tail_half, rows * (s - m // 2))
+        d_one = matmul(half[row : row + rows, :], weight[...], 1, 1)
+        d_two = matmul(slope[at, :], inner[...], 1, 1)
+        xhat, _ = standardize(xs[s][...].astype(jnp.float32))
+        for i, part in enumerate((d_one * xhat, d_one, d_two * xhat, d_two)):
+            sums[i] = sums[i] + jnp.sum(part, 0, keepdims=True)
+        outs[s][...] = (d_one * vec[0:1, :] + d_two * vec[2:3, :]).astype(outs[s].dtype)
+    own = jnp.sum(cot[:rows, :].astype(jnp.float32), 0, keepdims=True)
+    five[...] = jnp.concatenate([own] + sums + [jnp.zeros((3, width), jnp.float32)], axis=0)
+
+
+def rest_body(sizes, scal, first, head_half, tail_half, head_grad, tail_grad, inner_grad, *refs):
+    strip, qkv_cols, heads = sizes
+    five, keep, send, d_packed_b = refs
+    count = head_half.shape[0]
+    d_packed_b[:count, :] = head_half[...]
+    d_packed_b[count:, :] = tail_half[...]
+    qkv_grad = head_grad[...] + tail_grad[...]
+    pairs = destinations(scal, keep, send)
+    for pair in pairs:
+        grad = matmul(two_blocks(first, pair, strip), d_packed_b[...], 0, 0).astype(jnp.bfloat16)
+        for j, (unused_result, place) in enumerate(pair):
+            place[:, :qkv_cols] = grad[strip * j : strip * (j + 1)]
+    rows = [[], [], [], []]
+    for h in range(heads):
+        at = 3 * HD * h
+        rows[0].append(qkv_grad[:, at : at + strip])
+        rows[1].append(
+            jnp.concatenate(
+                [qkv_grad[:, at + strip : at + 3 * HD], jnp.zeros((1, 2 * strip - 3 * HD), jnp.float32)], axis=1
+            )
+        )
+        rows[2].append(inner_grad[:, 2 * strip * h : 2 * strip * h + strip])
+        rows[3].append(inner_grad[:, 2 * strip * h + strip : 2 * strip * (h + 1)])
+    tail = jnp.concatenate(sum(rows, []) + [jnp.zeros((strip - 8 - 4 * heads, strip), jnp.float32)], axis=0)
+    for k, place in sum(pairs, []):
+        five_k = five[0:8, pl.ds(pl.multiple_of(k * strip, strip), strip)]
+        place[:, qkv_cols : qkv_cols + strip] = jnp.concatenate([five_k, tail], axis=0).astype(jnp.bfloat16)
+
+
+def five_body(scal, *refs):
+    parts, outs = refs[:-5], refs[-5:]
+    total = parts[0][...]
+    for part in parts[1:]:
+        total = total + part[...]
+    for k, out in enumerate(outs):
+        out[...] = total[k : k + 1]
+
+
+def finish_body(m, scal, *refs):
+    x, g = refs[0], refs[1]
+    parts = refs[2 : 2 + m]
+    (grad,) = refs[2 + m :]
+    xhat, scale = standardize(x[...].astype(jnp.float32))
+    total = parts[0][...].astype(jnp.float32)
+    for part in parts[1:]:
+        total = total + part[...].astype(jnp.float32)
+    grad[...] = (
+        g[...].astype(jnp.float32)
+        + scale * (total - jnp.mean(total, -1, keepdims=True) - xhat * jnp.mean(total * xhat, -1, keepdims=True))
+    ).astype(grad.dtype)
+
+
+def pair_shards(
+    layer_input,
+    out_grad,
+    segments,
+    positions,
+    qkv_weight,
+    qkv_bias,
+    dense_weight,
+    dense_bias,
+    inner_weight,
+    inner_bias,
+    outer_weight,
+    outer_bias,
+    attention_norm_gain,
+    attention_norm_bias,
+    feedforward_norm_gain,
+    feedforward_norm_bias,
+):
+    n = lax.axis_size(FSDP)
+    m = lax.axis_size(TENSOR)
+    f = lax.axis_index(FSDP)
+    t = lax.axis_index(TENSOR)
+    x = layer_input[0]
+    g = out_grad[0]
+    rows, width = x.shape
+    strip = width // n
+    heads = qkv_bias.shape[0]
+    wide = heads * HD
+    qkv_cols = qkv_weight.shape[1]
+    units = inner_weight.shape[1]
+    lanes = attention_norm_gain.shape[0]
+
+    bf, fl = jnp.bfloat16, jnp.float32
+    masks = slot_masks()
+    slot_to_block = [f ^ masks[s] for s in range(8)]
+    scal = jnp.stack(slot_to_block + [t, f]).astype(jnp.int32)
+
+    second_msg, x_own, g_own = pl.pallas_call(
+        pack_body,
+        out_shape=[pltpu.VMEM((strip, 2 * units + wide), bf), pltpu.VMEM(x.shape, bf), pltpu.VMEM(x.shape, bf)],
+    )(inner_weight, outer_weight, dense_weight, x, g)
+    x_slots = [x_own] + depth_gather(x)[1:]
+    as_row = lambda v: v.reshape(1, lanes)
+    vectors = (
+        attention_norm_gain, attention_norm_bias, feedforward_norm_gain, feedforward_norm_bias, dense_bias, outer_bias
+    )
+    (first_msg,) = call(
+        pack_attend_body,
+        [((strip, qkv_cols + strip), bf)],
+        [scal, *[as_row(v) for v in vectors], qkv_weight, qkv_bias, inner_bias],
+        loose=True,
+    )
+    second_blocks = gather_blocks(second_msg)
+    first_blocks = gather_blocks(first_msg)
+    (share,) = call(functools.partial(share_body, qkv_cols), [((8, 16, strip), bf)], [scal, *first_blocks])
+    shares = [depth_swap(share, k) for k in range(1, m)]
+    g_slots = [g_own] + depth_gather(g)[1:]
+    poss = jnp.concatenate([lax.dynamic_slice_in_dim(positions[0], t ^ k, 1, 0) for k in range(m)])
+    tables = turn_tables(poss.reshape(m * rows, 1))
+    segs = segments[0]
+    tokens = m * rows
+    sizes = (strip, qkv_cols)
+    first, second, turned, probs, context, qkv_w, vec, inner_b = call(
+        functools.partial(attend_body, m, heads, sizes),
+        [
+            ((tokens, width), bf),
+            ((tokens, width), bf),
+            ((tokens, qkv_cols), bf),
+            ((m * heads, rows, rows), fl),
+            ((tokens, wide), bf),
+            ((width, qkv_cols), bf),
+            ((8, width), fl),
+            ((1, units), fl),
+        ],
+        [scal, *x_slots, *first_blocks, *shares, segs, *tables],
+        [pltpu.VMEM((8, 16, strip), fl)],
+    )
+    inner_w, outer_w, dense_w, bend, act, *partial = call(
+        functools.partial(feed_body, m, (strip, units, wide)),
+        [((width, units), bf), ((units, width), bf), ((wide, width), bf), ((tokens, units), fl), ((tokens, units), bf)]
+        + [((rows, width), bf)] * m,
+        [scal, second, context, inner_b, *second_blocks],
+    )
+    mixed = depth_scatter(partial)
+    big_keep, big_send, slope, inner_grad, cot = call(
+        functools.partial(feed_back_body, m, (strip, units, wide)),
+        [
+            ((4, strip, 2 * units + wide), bf),
+            ((4, strip, 2 * units + wide), bf),
+            ((tokens, units), bf),
+            ((1, units), fl),
+            ((tokens, width), bf),
+        ],
+        [scal, *g_slots, act, bend, second, context, outer_w],
+    )
+    big = scatter_sum(big_keep, big_send)
+    halves, grads = [], []
+    for start, stop in ((0, m // 2), (m // 2, m)):
+        half, part = call(
+            functools.partial(attend_back_body, start, stop, heads),
+            [((rows * (stop - start), qkv_cols), bf), ((1, qkv_cols), fl)],
+            [scal, cot, context, dense_w, turned, probs, *tables],
+            [pltpu.VMEM((rows * (stop - start), qkv_cols), fl), pltpu.VMEM((rows * (stop - start), wide), bf)],
+        )
+        halves.append(half)
+        grads.append(part)
+    *norms, five = call(
+        functools.partial(norm_back_body, m),
+        [((rows, width), bf)] * m + [((8, width), fl)],
+        [scal, *x_slots, cot, *halves, qkv_w, slope, inner_w, vec],
+    )
+    rest_keep, rest_send = call(
+        functools.partial(rest_body, (strip, qkv_cols, heads)),
+        [((4, strip, qkv_cols + strip), bf)] * 2,
+        [scal, first, *halves, *grads, inner_grad, five],
+        [pltpu.VMEM((tokens, qkv_cols), bf)],
+    )
+    arrived = depth_scatter(norms)
+    rest = scatter_sum(rest_keep, rest_send)
+    (result,) = call(
+        functools.partial(result_body, len(mixed)), [((rows, width), bf)], [scal, x_own, vec, *mixed], final=True
+    )
+    s_inner, s_outer, s_dense = call(
+        functools.partial(unpack_big_body, units, wide),
+        [((strip, units), fl), ((units, strip), fl), ((wide, strip), fl)],
+        [scal, *big],
+        final=True,
+    )
+    s_qkv, s_qkv_b, s_inner_b, *fives = call(
+        functools.partial(unpack_rest_body, (strip, qkv_cols, heads, lanes)),
+        [((strip, qkv_cols), fl), (qkv_bias.shape, fl), (inner_bias.shape, fl)] + [((8, lanes), fl)] * m,
+        [scal, *rest],
+        final=True,
+    )
+    (in_grad,) = call(
+        functools.partial(finish_body, len(arrived)), [((rows, width), bf)], [scal, x_own, g_own, *arrived], final=True
+    )
+    fives = [fives[0]] + [depth_swap(fives[k], k) for k in range(1, m)]
+    five = call(five_body, [((1, lanes), fl)] * 5, [scal, *fives], final=True)
+    five = [v.reshape(lanes) for v in five]
+    return (
+        result[None],
+        in_grad[None],
+        s_qkv,
+        s_qkv_b,
+        s_dense,
+        five[0],
+        s_inner,
+        s_inner_b,
+        s_outer,
+        five[0],
+        five[1],
+        five[2],
+        five[3],
+        five[4],
+    )
+
+
 def solution(mesh):
+    n, m = mesh.shape[FSDP], mesh.shape[TENSOR]
+    paired = n == 8 and m == 4
+    shards = plain_shards
+    if paired:
+
+        def shards(*args):
+            return pair_shards(*args)
+
     placed = (
-        P(None, ("fsdp", "tensor"), None),
-        P(None, ("fsdp", "tensor"), None),
-        P(None, "fsdp", None),
-        P(None, "fsdp", None),
-        P("fsdp", "tensor"),
-        P("tensor", "fsdp"),
-        P("tensor", "fsdp"),
-        P(("fsdp", "tensor")),
-        P("fsdp", "tensor"),
-        P("tensor", "fsdp"),
-        P("tensor", "fsdp"),
-        P(("fsdp", "tensor")),
-        P(("fsdp", "tensor")),
-        P(("fsdp", "tensor")),
-        P(("fsdp", "tensor")),
-        P(("fsdp", "tensor")),
+        P(None, (FSDP, TENSOR), None),
+        P(None, (FSDP, TENSOR), None),
+        P(None, FSDP, None),
+        P(None, FSDP, None),
+        P(FSDP, TENSOR),
+        P(TENSOR, FSDP),
+        P(TENSOR, FSDP),
+        P((FSDP, TENSOR)),
+        P(FSDP, TENSOR),
+        P(TENSOR, FSDP),
+        P(TENSOR, FSDP),
+        P((FSDP, TENSOR)),
+        P((FSDP, TENSOR)),
+        P((FSDP, TENSOR)),
+        P((FSDP, TENSOR)),
+        P((FSDP, TENSOR)),
     )
     return jax.shard_map(
         shards,
         mesh=mesh,
         in_specs=placed,
         out_specs=(
-            P(None, ("fsdp", "tensor"), None),
-            P(None, ("fsdp", "tensor"), None),
-            P("fsdp", "tensor"),
-            P("tensor", "fsdp"),
-            P("tensor", "fsdp"),
-            P(("fsdp", "tensor")),
-            P("fsdp", "tensor"),
-            P("tensor", "fsdp"),
-            P("tensor", "fsdp"),
-            P(("fsdp", "tensor")),
-            P(("fsdp", "tensor")),
-            P(("fsdp", "tensor")),
-            P(("fsdp", "tensor")),
-            P(("fsdp", "tensor")),
+            P(None, (FSDP, TENSOR), None),
+            P(None, (FSDP, TENSOR), None),
+            P(FSDP, TENSOR),
+            P(TENSOR, FSDP),
+            P(TENSOR, FSDP),
+            P((FSDP, TENSOR)),
+            P(FSDP, TENSOR),
+            P(TENSOR, FSDP),
+            P(TENSOR, FSDP),
+            P((FSDP, TENSOR)),
+            P((FSDP, TENSOR)),
+            P((FSDP, TENSOR)),
+            P((FSDP, TENSOR)),
+            P((FSDP, TENSOR)),
         ),
         check_vma=False,
     )

time: 457 us -> 168 us (0.37)
  waiting for transfers between devices: 237 us -> 73 us
  blocking collectives: 123 us -> 0 us
  Pallas kernels: 0 us -> 47.7 us
  matrix products: 42.6 us -> 0 us
  starting transfers between devices: 0.7 us -> 41.6 us
  local copies, waits for them, and re-layouts: 21.9 us -> 2.91 us
  other arithmetic: 15.2 us -> 1.05 us
  between operations: 15 us -> 0.91 us
    reduce_scatter x5 -> x0, waiting for transfers between devices: 139 us -> none  [the longest x1 42.5 us: shards(): lax.psum_scatter(g_inner.astype(jnp.bfloat16), 'fsdp', scatter_dimension=...]
    unnamed x3 -> x0, blocking collectives: 94.4 us -> none
    ppermute x0 -> x42, waiting for transfers between devices: none -> 73 us  [swap(): return lax.ppermute(value, axis, [(i, partner(i)) for i in range(count)])]
    unnamed x16 -> x0, waiting for transfers between devices: 49.7 us -> none
    all_gather x5 -> x0, waiting for transfers between devices: 48.8 us -> none  [the longest x1 25.3 us: shards(): lax.all_gather(outer_weight, 'fsdp', axis=1, tiled=True)]
    pallas_call x0 -> x21, Pallas kernels: none -> 47.7 us  [the longest x20 46.4 us: call(): pl.pallas_call(body, out_shape=[jax.ShapeDtypeStruct(*out) if final else...]
    dot_general x18 -> x0, matrix products: 42.6 us -> none  [the longest x8 27.3 us: matmul(): lax.dot_general(left, right, (((left_dim,), (right_dim,)), ((), ())), pre...]
    ppermute x0 -> x42, starting transfers between devices: none -> 41.6 us  [swap(): return lax.ppermute(value, axis, [(i, partner(i)) for i in range(count)])]
  transfers between devices with their start and end apart: 13 -> 42, of which waited for: 9 -> 15; matrix products, arithmetic and copies ran while one was open for 17% -> 1% of each run, Pallas kernels for 0% -> 23%
where the time goes in v2:
time: 168 us; the launch traced here: 167 us
  waiting for transfers between devices  73 us (43%)
  Pallas kernels  47.7 us (28%)
  starting transfers between devices  41.6 us (25%)
  local copies, waits for them, and re-layouts  2.91 us (2%)
    ppermute x42, waiting for transfers between devices, swap(): return lax.ppermute(value, axis, [(i, partner(i)) for i in range(count)])  73 us
    pallas_call x20, Pallas kernels, call(): pl.pallas_call(body, out_shape=[jax.ShapeDtypeStruct(*out) if final else...  46.4 us
    ppermute x42, starting transfers between devices, swap(): return lax.ppermute(value, axis, [(i, partner(i)) for i in range(count)])  41.6 us
  transfers between devices with their start and end apart: 42, of which 15 were waited for; matrix products, arithmetic and copies ran while one was open for 1% of the time, Pallas kernels for 23%

profile of v2, /device:TPU:0, one launch (start us, length us, event | category | flops | bytes accessed | tf_op | source)
XLA Modules:
  0.0 167.3 jit_solution(10207916012001342559)
XLA Ops:
  0.7 1.4 shard_map.263
  2.0 3.0 %collective-permute-start.14 = (bf16[128,2304]{1,0:T(8,128)(2,1)S(1)}, bf16[128,2304]{1,0:T(8,128)(2,1)}, u32[]{:S(2)}, u32[]{:S(2)}) collective-permute-start(bf16[128,2304]{1,0:T(8,128)(2,1)S(1)} %get-tuple-element.78.refs_3_), channel_id=1, source_target_pairs={{0,8},{4,20},{8,0},{12,28},{16,24},{20,4},{24,16},{28,12},{1,9},{5... | collective-permute-start | bytes 1769480 | tf_op jit(solution)/shard_map/ppermute | solution.py:331
  5.1 0.8 copy-done
  6.0 1.1 shard_map.264.refs_0_.refs_4_
  7.1 1.1 collective-permute-start.4
  8.2 0.7 collective-permute-start.3
  8.9 2.6 %collective-permute-start.1 = (bf16[128,1024]{1,0:T(8,128)(2,1)}, bf16[128,1024]{1,0:T(8,128)(2,1)S(1)}, u32[]{:S(2)}, u32[]{:S(2)}) collective-permute-start(bf16[128,1024]{1,0:T(8,128)(2,1)} %bitcast.37), channel_id=1, source_target_pairs={{0,2},{1,3},{2,0},{3,1},{4,6},{5,7},{6,4},{7,5},{8,10},{9,11},{10,... | collective-permute-start | bytes 786440 | tf_op jit(solution)/shard_map/ppermute | solution.py:331
  11.5 3.9 %collective-permute-done.4.refs_2_.refs_6_ = bf16[128,896]{1,0:T(8,128)(2,1)S(1)} collective-permute-done((bf16[128,896]{1,0:T(8,128)(2,1)S(1)}, bf16[128,896]{1,0:T(8,128)(2,1)S(1)}, u32[]{:S(2)}, u32[]{:S(2)}) %collective-permute-start.4) | collective-permute-done | bytes 229408 | tf_op jit(solution)/shard_map/ppermute | solution.py:331
  15.4 2.1 %collective-permute-start = (bf16[128,1024]{1,0:T(8,128)(2,1)}, bf16[128,1024]{1,0:T(8,128)(2,1)S(1)}, u32[]{:S(2)}, u32[]{:S(2)}) collective-permute-start(bf16[128,1024]{1,0:T(8,128)(2,1)} %bitcast.38), channel_id=1, source_target_pairs={{0,1},{1,0},{2,3},{3,2},{4,5},{5,4},{6,7},{7,6},{8,9},{9,8},{10,11... | collective-permute-start | bytes 786440 | tf_op jit(solution)/shard_map/ppermute | solution.py:331
  17.5 1.5 collective-permute-start.18
  19.0 1.5 collective-permute-start.15
  20.5 0.5 collective-permute-start.8
  21.0 2.9 %collective-permute-done.1.refs_2_ = bf16[128,1024]{1,0:T(8,128)(2,1)S(1)} collective-permute-done((bf16[128,1024]{1,0:T(8,128)(2,1)}, bf16[128,1024]{1,0:T(8,128)(2,1)S(1)}, u32[]{:S(2)}, u32[]{:S(2)}) %collective-permute-start.1) | collective-permute-done | bytes 262176 | tf_op jit(solution)/shard_map/ppermute | solution.py:331
  24.0 0.8 collective-permute-start.5
  24.7 2.9 %collective-permute-done.refs_1_ = bf16[128,1024]{1,0:T(8,128)(2,1)S(1)} collective-permute-done((bf16[128,1024]{1,0:T(8,128)(2,1)}, bf16[128,1024]{1,0:T(8,128)(2,1)S(1)}, u32[]{:S(2)}, u32[]{:S(2)}) %collective-permute-start) | collective-permute-done | bytes 262176 | tf_op jit(solution)/shard_map/ppermute | solution.py:331
  27.7 10.1 %collective-permute-done.8.refs_6_.refs_10_ = bf16[128,896]{1,0:T(8,128)(2,1)S(1)} collective-permute-done((bf16[128,896]{1,0:T(8,128)(2,1)S(1)}, bf16[128,896]{1,0:T(8,128)(2,1)S(1)}, u32[]{:S(2)}, u32[]{:S(2)}) %collective-permute-start.8) | collective-permute-done | bytes 229408 | tf_op jit(solution)/shard_map/ppermute | solution.py:331
  37.8 0.5 collective-permute-start.6
  38.3 2.6 %collective-permute-start.24 = (bf16[128,1024]{1,0:T(8,128)(2,1)}, bf16[128,1024]{1,0:T(8,128)(2,1)S(1)}, u32[]{:S(2)}, u32[]{:S(2)}) collective-permute-start(bf16[128,1024]{1,0:T(8,128)(2,1)} %bitcast.40), channel_id=1, source_target_pairs={{0,2},{1,3},{2,0},{3,1},{4,6},{5,7},{6,4},{7,5},{8,10},{9,11},{10,... | collective-permute-start | bytes 786440 | tf_op jit(solution)/shard_map/ppermute | solution.py:331
  40.9 0.5 collective-permute-start.2
  41.3 0.8 fusion.5
  42.2 0.5 collective-permute-start.19
  42.8 0.5 shard_map.265
  43.4 9.9 %collective-permute-done.24.refs_2_ = bf16[128,1024]{1,0:T(8,128)(2,1)S(1)} collective-permute-done((bf16[128,1024]{1,0:T(8,128)(2,1)}, bf16[128,1024]{1,0:T(8,128)(2,1)S(1)}, u32[]{:S(2)}, u32[]{:S(2)}) %collective-permute-start.24) | collective-permute-done | bytes 262176 | tf_op jit(solution)/shard_map/ppermute | solution.py:331
  53.3 2.5 %collective-permute-start.12 = (bf16[8,16,128]{2,1,0:T(8,128)(2,1)S(1)}, bf16[8,16,128]{2,1,0:T(8,128)(2,1)S(1)}, u32[]{:S(2)}, u32[]{:S(2)}) collective-permute-start(bf16[8,16,128]{2,1,0:T(8,128)(2,1)S(1)} %shard_map.265), channel_id=1, source_target_pairs={{0,3},{1,2},{2,1},{3,0},{4,7},{5,6},{6,5},{7,4},{8,11},{9,10},{10,... | collective-permute-start | bytes 98312 | tf_op jit(solution)/shard_map/ppermute | solution.py:331
  55.9 3.1 %collective-permute-done.12.refs_14_ = bf16[8,16,128]{2,1,0:T(8,128)(2,1)S(1)} collective-permute-done((bf16[8,16,128]{2,1,0:T(8,128)(2,1)S(1)}, bf16[8,16,128]{2,1,0:T(8,128)(2,1)S(1)}, u32[]{:S(2)}, u32[]{:S(2)}) %collective-permute-start.12) | collective-permute-done | bytes 32800 | tf_op jit(solution)/shard_map/ppermute | solution.py:331
  59.0 1.7 %collective-permute-done.11.refs_13_ = bf16[8,16,128]{2,1,0:T(8,128)(2,1)S(1)} collective-permute-done((bf16[8,16,128]{2,1,0:T(8,128)(2,1)S(1)}, bf16[8,16,128]{2,1,0:T(8,128)(2,1)S(1)}, u32[]{:S(2)}, u32[]{:S(2)}) %collective-permute-start.11) | collective-permute-done | bytes 32800 | tf_op jit(solution)/shard_map/ppermute | solution.py:331
  60.7 0.4 collective-permute-start.23
  61.1 2.2 %collective-permute-done.10.refs_12_ = bf16[8,16,128]{2,1,0:T(8,128)(2,1)S(1)} collective-permute-done((bf16[8,16,128]{2,1,0:T(8,128)(2,1)S(1)}, bf16[8,16,128]{2,1,0:T(8,128)(2,1)S(1)}, u32[]{:S(2)}, u32[]{:S(2)}) %collective-permute-start.10) | collective-permute-done | bytes 32800 | tf_op jit(solution)/shard_map/ppermute | solution.py:331
  63.3 1.0 fusion
  64.3 7.9 %shard_map.266 = (bf16[512,1024]{1,0:T(8,128)(2,1)S(1)}, bf16[512,1024]{1,0:T(8,128)(2,1)S(1)}, bf16[512,768]{1,0:T(8,128)(2,1)S(1)}, f32[16,128,128]{2,1,0:T(8,...) custom-call(s32[10]{0:T(128)S(1)} %stack.40.scal, ...), custom_call_target="tpu_custom_call" | custom-call | tf_op jit(solution)/shard_map/pallas_call | solution.py:424
  72.3 7.6 %shard_map.267 = (bf16[1024,1024]{1,0:T(8,128)(2,1)S(1)}, bf16[1024,1024]{1,0:T(8,128)(2,1)S(1)}, bf16[256,1024]{1,0:T(8,128)(2,1)S(1)}, f32[512,1024]{1,0:T(8,1...) custom-call(s32[10]{0:T(128)S(1)} %stack.40.scal, ...), custom_call_target="tpu_custom_call" | custom-call | tf_op jit(solution)/shard_map/pallas_call | solution.py:424
  79.9 6.1 %shard_map.270 = (bf16[4,128,2304]{2,1,0:T(8,128)(2,1)S(1)}, bf16[4,128,2304]{2,1,0:T(8,128)(2,1)S(1)}, bf16[512,1024]{1,0:T(8,128)(2,1)S(1)}, f32[1,1024]{1,0:T(1,128)S(1)}, bf16[512,1024]{1,0:T(8,128)(2,1)S(1)}) custom-call(s32[10]{0:T(128)S(1)} %stack.40.scal, bf16[128,1024]{1,0:T(8,128)(2,1)S(1)} %get-tuple-element.83.refs_0_.refs_1_, ...), custom_call_target="tpu_custom_call" | custom-call | tf_op jit(solution)/shard_map/pallas_call | solution.py:424
  86.2 3.6 %shard_map.272 = (bf16[256,768]{1,0:T(8,128)(2,1)S(1)}, f32[1,768]{1,0:T(1,128)S(1)}) custom-call(s32[10]{0:T(128)S(1)} %stack.40.scal, bf16[512,1024]{1,0:T(8,128)(2,1)S(1)} %get-tuple-element.87.refs_0_.refs_4_, bf16[512,256]{1,0:T(8,128)(2,1)S(1)} %get-tuple-element.76.refs_1_.refs_7_, bf16[256,1024]{1,0:T(8,128)(2,1)S(1)} %get-tuple-element.88.refs_2_, ...), custom_call_target="tpu_custom_call" | custom-call | tf_op jit(solution)/shard_map/pallas_call | solution.py:424
  89.7 3.5 %shard_map.271 = (bf16[256,768]{1,0:T(8,128)(2,1)S(1)}, f32[1,768]{1,0:T(1,128)S(1)}) custom-call(s32[10]{0:T(128)S(1)} %stack.40.scal, bf16[512,1024]{1,0:T(8,128)(2,1)S(1)} %get-tuple-element.87.refs_0_.refs_4_, bf16[512,256]{1,0:T(8,128)(2,1)S(1)} %get-tuple-element.76.refs_1_.refs_7_, bf16[256,1024]{1,0:T(8,128)(2,1)S(1)} %get-tuple-element.88.refs_2_, ...), custom_call_target="tpu_custom_call" | custom-call | tf_op jit(solution)/shard_map/pallas_call | solution.py:424
  93.3 6.1 %shard_map.273 = (bf16[128,1024]{1,0:T(8,128)(2,1)S(1)}, bf16[128,1024]{1,0:T(8,128)(2,1)S(1)}, bf16[128,1024]{1,0:T(8,128)(2,1)S(1)}, bf16[128,1024]{1,0:T(8,128)(2,1)S(1)}, f32[8,1024]{1,0:T(8,128)S(1)}) custom-call(s32[10]{0:T(128)S(1)} %stack.40.scal, bf16[128,1024]{1,0:T(8,128)(2,1)S(1)} %get-tuple-element.73.refs_0_.x, ...), custom_call_target="tpu_custom_call" | custom-call | tf_op jit(solution)/shard_map/pallas_call | solution.py:424
  99.3 1.6 shard_map.276
  100.9 0.6 collective-permute-start.29
  101.5 0.5 shard_map.280
  102.0 1.6 collective-permute-start.35
  103.6 0.5 collective-permute-start.37
  104.1 2.0 %collective-permute-start.20 = (bf16[128,1024]{1,0:T(8,128)(2,1)S(1)}, bf16[128,1024]{1,0:T(8,128)(2,1)S(1)}, u32[]{:S(2)}, u32[]{:S(2)}) collective-permute-start(bf16[128,1024]{1,0:T(8,128)(2,1)S(1)} %get-tuple-element.80), channel_id=1, source_target_pairs={{0,1},{1,0},{2,3},{3,2},{4,5},{5,4},{6,7},{7,6},{8,9},{9,8},{10,11... | collective-permute-start | bytes 786440 | tf_op jit(solution)/shard_map/ppermute | solution.py:331
  106.2 0.2 shard_map.277
  106.4 0.6 collective-permute-start.30
  107.0 0.4 collective-permute-start.21
  107.4 10.2 %collective-permute-done.35.two = bf16[128,2304]{1,0:T(8,128)(2,1)S(1)} collective-permute-done((bf16[128,2304]{1,0:T(8,128)(2,1)S(1)}, bf16[128,2304]{1,0:T(8,128)(2,1)S(1)}, u32[]{:S(2)}, u32[]{:S(2)}) %collective-permute-start.35) | collective-permute-done | bytes 589856 | tf_op jit(solution)/shard_map/ppermute | solution.py:331
  117.6 1.0 collective-permute-start.32
  118.8 1.1 collective-permute-start.36
  119.9 1.9 %collective-permute-done.30.two = bf16[128,896]{1,0:T(8,128)(2,1)S(1)} collective-permute-done((bf16[128,896]{1,0:T(8,128)(2,1)S(1)}, bf16[128,896]{1,0:T(8,128)(2,1)S(1)}, u32[]{:S(2)}, u32[]{:S(2)}) %collective-permute-start.30) | collective-permute-done | bytes 229408 | tf_op jit(solution)/shard_map/ppermute | solution.py:331
  121.8 2.0 %collective-permute-start.27 = (bf16[128,1024]{1,0:T(8,128)(2,1)S(1)}, bf16[128,1024]{1,0:T(8,128)(2,1)S(1)}, u32[]{:S(2)}, u32[]{:S(2)}) collective-permute-start(bf16[128,1024]{1,0:T(8,128)(2,1)S(1)} %get-tuple-element.99), channel_id=1, source_target_pairs={{0,1},{1,0},{2,3},{3,2},{4,5},{5,4},{6,7},{7,6},{8,9},{9,8},{10,11... | collective-permute-start | bytes 786440 | tf_op jit(solution)/shard_map/ppermute | solution.py:331
  123.8 1.8 %collective-permute-start.31 = (bf16[128,896]{1,0:T(8,128)(2,1)S(1)}, bf16[128,896]{1,0:T(8,128)(2,1)S(1)}, u32[]{:S(2)}, u32[]{:S(2)}) collective-permute-start(bf16[128,896]{1,0:T(8,128)(2,1)S(1)} %shard_map.278), channel_id=1, source_target_pairs={{0,8},{4,20},{8,0},{12,28},{16,24},{20,4},{24,16},{28,12},{1,9},{5... | collective-permute-start | bytes 688136 | tf_op jit(solution)/shard_map/ppermute | solution.py:331
  125.8 3.1 %collective-permute-done.27.two = bf16[128,1024]{1,0:T(8,128)(2,1)S(1)} collective-permute-done((bf16[128,1024]{1,0:T(8,128)(2,1)S(1)}, bf16[128,1024]{1,0:T(8,128)(2,1)S(1)}, u32[]{:S(2)}, u32[]{:S(2)}) %collective-permute-start.27) | collective-permute-done | bytes 262176 | tf_op jit(solution)/shard_map/ppermute | solution.py:331
  128.9 1.7 %collective-permute-start.26 = (bf16[128,1024]{1,0:T(8,128)(2,1)S(1)}, bf16[128,1024]{1,0:T(8,128)(2,1)S(1)}, u32[]{:S(2)}, u32[]{:S(2)}) collective-permute-start(bf16[128,1024]{1,0:T(8,128)(2,1)S(1)} %get-tuple-element.97), channel_id=1, source_target_pairs={{0,1},{1,0},{2,3},{3,2},{4,5},{5,4},{6,7},{7,6},{8,9},{9,8},{10,11... | collective-permute-start | bytes 786440 | tf_op jit(solution)/shard_map/ppermute | solution.py:331
  130.6 1.8 %collective-permute-done.31.near = bf16[128,896]{1,0:T(8,128)(2,1)S(1)} collective-permute-done((bf16[128,896]{1,0:T(8,128)(2,1)S(1)}, bf16[128,896]{1,0:T(8,128)(2,1)S(1)}, u32[]{:S(2)}, u32[]{:S(2)}) %collective-permute-start.31) | collective-permute-done | bytes 229408 | tf_op jit(solution)/shard_map/ppermute | solution.py:331
  132.4 3.1 %collective-permute-start.22 = (bf16[128,1024]{1,0:T(8,128)(2,1)S(1)}, bf16[128,1024]{1,0:T(8,128)(2,1)S(1)}, u32[]{:S(2)}, u32[]{:S(2)}) collective-permute-start(bf16[128,1024]{1,0:T(8,128)(2,1)S(1)} %shard_map.268), channel_id=1, source_target_pairs={{0,2},{1,3},{2,0},{3,1},{4,6},{5,7},{6,4},{7,5},{8,10},{9,11},{10,... | collective-permute-start | bytes 786440 | tf_op jit(solution)/shard_map/ppermute | solution.py:331
  135.7 1.4 shard_map.279
  137.1 1.9 %collective-permute-start.39 = (f32[8,32]{1,0:T(8,128)S(1)}, f32[8,32]{1,0:T(8,128)S(1)}, u32[]{:S(2)}, u32[]{:S(2)}) collective-permute-start(f32[8,32]{1,0:T(8,128)S(1)} %get-tuple-element.121), channel_id=1, source_target_pairs={{0,1},{1,0},{2,3},{3,2},{4,5},{5,4},{6,7},{7,6},{8,9},{9,8},{10,11... | collective-permute-start | bytes 3080 | tf_op jit(solution)/shard_map/ppermute | solution.py:331
  138.9 14.7 %collective-permute-done.22.refs_2_ = bf16[128,1024]{1,0:T(8,128)(2,1)S(1)} collective-permute-done((bf16[128,1024]{1,0:T(8,128)(2,1)S(1)}, bf16[128,1024]{1,0:T(8,128)(2,1)S(1)}, u32[]{:S(2)}, u32[]{:S(2)}) %collective-permute-start.22) | collective-permute-done | bytes 262176 | tf_op jit(solution)/shard_map/ppermute | solution.py:331
  153.6 4.4 %collective-permute-done.28.refs_4_ = bf16[128,1024]{1,0:T(8,128)(2,1)S(1)} collective-permute-done((bf16[128,1024]{1,0:T(8,128)(2,1)S(1)}, bf16[128,1024]{1,0:T(8,128)(2,1)S(1)}, u32[]{:S(2)}, u32[]{:S(2)}) %collective-permute-start.28) | collective-permute-done | bytes 262176 | tf_op jit(solution)/shard_map/ppermute | solution.py:331
  158.0 2.1 %collective-permute-start.41 = (f32[8,32]{1,0:T(8,128)S(1)}, f32[8,32]{1,0:T(8,128)S(1)}, u32[]{:S(2)}, u32[]{:S(2)}) collective-permute-start(f32[8,32]{1,0:T(8,128)S(1)} %get-tuple-element.123), channel_id=1, source_target_pairs={{0,3},{1,2},{2,1},{3,0},{4,7},{5,6},{6,5},{7,4},{8,11},{9,10},{10,... | collective-permute-start | bytes 3080 | tf_op jit(solution)/shard_map/ppermute | solution.py:331
  160.1 1.4 shard_map.269
  161.5 1.7 %shard_map.275 = bf16[128,1024]{1,0:T(8,128)(2,1)} custom-call(s32[10]{0:T(128)S(1)} %stack.40.scal, bf16[128,1024]{1,0:T(8,128)(2,1)S(1)} %get-tuple-element.73.refs_0_.x, bf16[128,1024]{1,0:T(8,128)(2,1)S(1)} %get-tuple-element.83.refs_0_.refs_1_, bf16[128,1024]{1,0:T(8,128)(2,1)S(1)} %get-tuple-element.96.refs_2_, ...), custom_call_target="tpu_custom_call" | custom-call | tf_op jit(solution)/shard_map/pallas_call | solution.py:424
  163.4 1.1 shard_map.283
  164.5 1.6 shard_map.282
  166.1 1.2 copy.31
  (57 shorter events, 1.1 us)
Async XLA Ops:
  0.6 60.1 %copy-start.3 = (bf16[1,128,1024]{2,1,0:T(8,128)(2,1)S(1)}, bf16[1,128,1024]{2,1,0:T(8,128)(2,1)}, u32[]{:S(2)}) copy-start(bf16[1,128,1024]{2,1,0:T(8,128)(2,1)} %param.17) | copy-start | bytes 786436
  0.7 63.6 %copy-start.2 = (s32[1,4,128]{2,1,0:T(4,128)S(1)}, s32[1,4,128]{2,1,0:T(4,128)}, u32[]{:S(2)}) copy-start(s32[1,4,128]{2,1,0:T(4,128)} %param.18) | copy-start | bytes 6148
  2.0 15.5 %collective-permute-start.14 = (bf16[128,2304]{1,0:T(8,128)(2,1)S(1)}, bf16[128,2304]{1,0:T(8,128)(2,1)}, u32[]{:S(2)}, u32[]{:S(2)}) collective-permute-start(bf16[128,2304]{1,0:T(8,128)(2,1)S(1)} %get-tuple-element.78.refs_3_), channel_id=1, source_target_pairs={{0,8},{4,20},{8,0},{12,28},{16,24},{20,4},{24,16},{28,12},{1,9},{5... | collective-permute-start | bytes 1769480 | tf_op jit(solution)/shard_map/ppermute | solution.py:331
  5.1 14.0 %collective-permute-start.13 = (bf16[128,2304]{1,0:T(8,128)(2,1)S(1)}, bf16[128,2304]{1,0:T(8,128)(2,1)}, u32[]{:S(2)}, u32[]{:S(2)}) collective-permute-start(bf16[128,2304]{1,0:T(8,128)(2,1)S(1)} %get-tuple-element.78.refs_3_), channel_id=1, source_target_pairs={{0,4},{4,0},{8,12},{12,8},{16,20},{20,16},{24,28},{28,24},{1,5},{5... | collective-permute-start | bytes 1769480 | tf_op jit(solution)/shard_map/ppermute | solution.py:331
  5.1 0.8 copy-start
  7.1 8.3 %collective-permute-start.4 = (bf16[128,896]{1,0:T(8,128)(2,1)S(1)}, bf16[128,896]{1,0:T(8,128)(2,1)S(1)}, u32[]{:S(2)}, u32[]{:S(2)}) collective-permute-start(bf16[128,896]{1,0:T(8,128)(2,1)S(1)} %shard_map.264.refs_0_.refs_4_), channel_id=1, source_target_pairs={{0,8},{4,20},{8,0},{12,28},{16,24},{20,4},{24,16},{28,12},{1,9},{5... | collective-permute-start | bytes 688136 | tf_op jit(solution)/shard_map/ppermute | solution.py:331
  8.2 12.3 %collective-permute-start.3 = (bf16[128,896]{1,0:T(8,128)(2,1)S(1)}, bf16[128,896]{1,0:T(8,128)(2,1)S(1)}, u32[]{:S(2)}, u32[]{:S(2)}) collective-permute-start(bf16[128,896]{1,0:T(8,128)(2,1)S(1)} %shard_map.264.refs_0_.refs_4_), channel_id=1, source_target_pairs={{0,4},{4,0},{8,12},{12,8},{16,20},{20,16},{24,28},{28,24},{1,5},{5... | collective-permute-start | bytes 688136 | tf_op jit(solution)/shard_map/ppermute | solution.py:331
  8.9 15.0 %collective-permute-start.1 = (bf16[128,1024]{1,0:T(8,128)(2,1)}, bf16[128,1024]{1,0:T(8,128)(2,1)S(1)}, u32[]{:S(2)}, u32[]{:S(2)}) collective-permute-start(bf16[128,1024]{1,0:T(8,128)(2,1)} %bitcast.37), channel_id=1, source_target_pairs={{0,2},{1,3},{2,0},{3,1},{4,6},{5,7},{6,4},{7,5},{8,10},{9,11},{10,... | collective-permute-start | bytes 786440 | tf_op jit(solution)/shard_map/ppermute | solution.py:331
  15.4 12.3 %collective-permute-start = (bf16[128,1024]{1,0:T(8,128)(2,1)}, bf16[128,1024]{1,0:T(8,128)(2,1)S(1)}, u32[]{:S(2)}, u32[]{:S(2)}) collective-permute-start(bf16[128,1024]{1,0:T(8,128)(2,1)} %bitcast.38), channel_id=1, source_target_pairs={{0,1},{1,0},{2,3},{3,2},{4,5},{5,4},{6,7},{7,6},{8,9},{9,8},{10,11... | collective-permute-start | bytes 786440 | tf_op jit(solution)/shard_map/ppermute | solution.py:331
  17.5 24.8 %collective-permute-start.18 = (bf16[128,2304]{1,0:T(8,128)(2,1)}, bf16[128,2304]{1,0:T(8,128)(2,1)}, u32[]{:S(2)}, u32[]{:S(2)}) collective-permute-start(bf16[128,2304]{1,0:T(8,128)(2,1)} %collective-permute-done.14.refs_5_), channel_id=1, source_target_pairs={{0,16},{4,12},{8,24},{12,4},{16,0},{20,28},{24,8},{28,20},{1,17},{... | collective-permute-start | bytes 1769480 | tf_op jit(solution)/shard_map/ppermute | solution.py:331
  19.0 23.7 %collective-permute-start.15 = (bf16[128,2304]{1,0:T(8,128)(2,1)}, bf16[128,2304]{1,0:T(8,128)(2,1)}, u32[]{:S(2)}, u32[]{:S(2)}) collective-permute-start(bf16[128,2304]{1,0:T(8,128)(2,1)} %collective-permute-done.13.refs_4_), channel_id=1, source_target_pairs={{0,8},{4,20},{8,0},{12,28},{16,24},{20,4},{24,16},{28,12},{1,9},{5... | collective-permute-start | bytes 1769480 | tf_op jit(solution)/shard_map/ppermute | solution.py:331
  20.5 17.3 %collective-permute-start.8 = (bf16[128,896]{1,0:T(8,128)(2,1)S(1)}, bf16[128,896]{1,0:T(8,128)(2,1)S(1)}, u32[]{:S(2)}, u32[]{:S(2)}) collective-permute-start(bf16[128,896]{1,0:T(8,128)(2,1)S(1)} %collective-permute-done.4.refs_2_.refs_6_), channel_id=1, source_target_pairs={{0,16},{4,12},{8,24},{12,4},{16,0},{20,28},{24,8},{28,20},{1,17},{... | collective-permute-start | bytes 688136 | tf_op jit(solution)/shard_map/ppermute | solution.py:331
  24.0 13.8 %collective-permute-start.5 = (bf16[128,896]{1,0:T(8,128)(2,1)S(1)}, bf16[128,896]{1,0:T(8,128)(2,1)S(1)}, u32[]{:S(2)}, u32[]{:S(2)}) collective-permute-start(bf16[128,896]{1,0:T(8,128)(2,1)S(1)} %collective-permute-done.3.refs_1_.refs_5_), channel_id=1, source_target_pairs={{0,8},{4,20},{8,0},{12,28},{16,24},{20,4},{24,16},{28,12},{1,9},{5... | collective-permute-start | bytes 688136 | tf_op jit(solution)/shard_map/ppermute | solution.py:331
  27.6 10.6 %collective-permute-start.7 = (bf16[128,896]{1,0:T(8,128)(2,1)S(1)}, bf16[128,896]{1,0:T(8,128)(2,1)S(1)}, u32[]{:S(2)}, u32[]{:S(2)}) collective-permute-start(bf16[128,896]{1,0:T(8,128)(2,1)S(1)} %collective-permute-done.4.refs_2_.refs_6_), channel_id=1, source_target_pairs={{0,4},{4,0},{8,12},{12,8},{16,20},{20,16},{24,28},{28,24},{1,5},{5... | collective-permute-start | bytes 688136 | tf_op jit(solution)/shard_map/ppermute | solution.py:331
  37.8 3.1 %collective-permute-start.9 = (bf16[128,896]{1,0:T(8,128)(2,1)S(1)}, bf16[128,896]{1,0:T(8,128)(2,1)S(1)}, u32[]{:S(2)}, u32[]{:S(2)}) collective-permute-start(bf16[128,896]{1,0:T(8,128)(2,1)S(1)} %collective-permute-done.8.refs_6_.refs_10_), channel_id=1, source_target_pairs={{0,4},{4,0},{8,12},{12,8},{16,20},{20,16},{24,28},{28,24},{1,5},{5... | collective-permute-start | bytes 688136 | tf_op jit(solution)/shard_map/ppermute | solution.py:331
  37.8 4.4 %collective-permute-start.6 = (bf16[128,896]{1,0:T(8,128)(2,1)S(1)}, bf16[128,896]{1,0:T(8,128)(2,1)S(1)}, u32[]{:S(2)}, u32[]{:S(2)}) collective-permute-start(bf16[128,896]{1,0:T(8,128)(2,1)S(1)} %collective-permute-done.5.refs_3_.refs_7_), channel_id=1, source_target_pairs={{0,4},{4,0},{8,12},{12,8},{16,20},{20,16},{24,28},{28,24},{1,5},{5... | collective-permute-start | bytes 688136 | tf_op jit(solution)/shard_map/ppermute | solution.py:331
  38.3 15.0 %collective-permute-start.24 = (bf16[128,1024]{1,0:T(8,128)(2,1)}, bf16[128,1024]{1,0:T(8,128)(2,1)S(1)}, u32[]{:S(2)}, u32[]{:S(2)}) collective-permute-start(bf16[128,1024]{1,0:T(8,128)(2,1)} %bitcast.40), channel_id=1, source_target_pairs={{0,2},{1,3},{2,0},{3,1},{4,6},{5,7},{6,4},{7,5},{8,10},{9,11},{10,... | collective-permute-start | bytes 786440 | tf_op jit(solution)/shard_map/ppermute | solution.py:331
  40.9 14.9 %collective-permute-start.2 = (bf16[128,1024]{1,0:T(8,128)(2,1)S(1)}, bf16[128,1024]{1,0:T(8,128)(2,1)S(1)}, u32[]{:S(2)}, u32[]{:S(2)}) collective-permute-start(bf16[128,1024]{1,0:T(8,128)(2,1)S(1)} %collective-permute-done.1.refs_2_), channel_id=1, source_target_pairs={{0,1},{1,0},{2,3},{3,2},{4,5},{5,4},{6,7},{7,6},{8,9},{9,8},{10,11... | collective-permute-start | bytes 786440 | tf_op jit(solution)/shard_map/ppermute | solution.py:331
  42.2 30.1 %collective-permute-start.17 = (bf16[128,2304]{1,0:T(8,128)(2,1)}, bf16[128,2304]{1,0:T(8,128)(2,1)S(1)}, u32[]{:S(2)}, u32[]{:S(2)}) collective-permute-start(bf16[128,2304]{1,0:T(8,128)(2,1)} %collective-permute-done.14.refs_5_), channel_id=1, source_target_pairs={{0,4},{4,0},{8,12},{12,8},{16,20},{20,16},{24,28},{28,24},{1,5},{5... | collective-permute-start | bytes 1769480 | tf_op jit(solution)/shard_map/ppermute | solution.py:331
  42.2 30.0 %collective-permute-start.19 = (bf16[128,2304]{1,0:T(8,128)(2,1)}, bf16[128,2304]{1,0:T(8,128)(2,1)S(1)}, u32[]{:S(2)}, u32[]{:S(2)}) collective-permute-start(bf16[128,2304]{1,0:T(8,128)(2,1)} %collective-permute-done.18.refs_9_), channel_id=1, source_target_pairs={{0,4},{4,0},{8,12},{12,8},{16,20},{20,16},{24,28},{28,24},{1,5},{5... | collective-permute-start | bytes 1769480 | tf_op jit(solution)/shard_map/ppermute | solution.py:331
  42.7 29.5 %collective-permute-start.16 = (bf16[128,2304]{1,0:T(8,128)(2,1)}, bf16[128,2304]{1,0:T(8,128)(2,1)S(1)}, u32[]{:S(2)}, u32[]{:S(2)}) collective-permute-start(bf16[128,2304]{1,0:T(8,128)(2,1)} %collective-permute-done.15.refs_6_), channel_id=1, source_target_pairs={{0,4},{4,0},{8,12},{12,8},{16,20},{20,16},{24,28},{28,24},{1,5},{5... | collective-permute-start | bytes 1769480 | tf_op jit(solution)/shard_map/ppermute | solution.py:331
  53.3 5.7 %collective-permute-start.12 = (bf16[8,16,128]{2,1,0:T(8,128)(2,1)S(1)}, bf16[8,16,128]{2,1,0:T(8,128)(2,1)S(1)}, u32[]{:S(2)}, u32[]{:S(2)}) collective-permute-start(bf16[8,16,128]{2,1,0:T(8,128)(2,1)S(1)} %shard_map.265), channel_id=1, source_target_pairs={{0,3},{1,2},{2,1},{3,0},{4,7},{5,6},{6,5},{7,4},{8,11},{9,10},{10,... | collective-permute-start | bytes 98312 | tf_op jit(solution)/shard_map/ppermute | solution.py:331
  55.8 4.9 %collective-permute-start.11 = (bf16[8,16,128]{2,1,0:T(8,128)(2,1)S(1)}, bf16[8,16,128]{2,1,0:T(8,128)(2,1)S(1)}, u32[]{:S(2)}, u32[]{:S(2)}) collective-permute-start(bf16[8,16,128]{2,1,0:T(8,128)(2,1)S(1)} %shard_map.265), channel_id=1, source_target_pairs={{0,2},{1,3},{2,0},{3,1},{4,6},{5,7},{6,4},{7,5},{8,10},{9,11},{10,... | collective-permute-start | bytes 98312 | tf_op jit(solution)/shard_map/ppermute | solution.py:331
  59.0 4.3 %collective-permute-start.10 = (bf16[8,16,128]{2,1,0:T(8,128)(2,1)S(1)}, bf16[8,16,128]{2,1,0:T(8,128)(2,1)S(1)}, u32[]{:S(2)}, u32[]{:S(2)}) collective-permute-start(bf16[8,16,128]{2,1,0:T(8,128)(2,1)S(1)} %shard_map.265), channel_id=1, source_target_pairs={{0,1},{1,0},{2,3},{3,2},{4,5},{5,4},{6,7},{7,6},{8,9},{9,8},{10,11... | collective-permute-start | bytes 98312 | tf_op jit(solution)/shard_map/ppermute | solution.py:331
  60.7 19.2 %collective-permute-start.23 = (bf16[128,1024]{1,0:T(8,128)(2,1)S(1)}, bf16[128,1024]{1,0:T(8,128)(2,1)S(1)}, u32[]{:S(2)}, u32[]{:S(2)}) collective-permute-start(bf16[128,1024]{1,0:T(8,128)(2,1)S(1)} %bitcast.41), channel_id=1, source_target_pairs={{0,1},{1,0},{2,3},{3,2},{4,5},{5,4},{6,7},{7,6},{8,9},{9,8},{10,11... | collective-permute-start | bytes 786440 | tf_op jit(solution)/shard_map/ppermute | solution.py:331
  63.3 16.7 %collective-permute-start.25 = (bf16[128,1024]{1,0:T(8,128)(2,1)S(1)}, bf16[128,1024]{1,0:T(8,128)(2,1)S(1)}, u32[]{:S(2)}, u32[]{:S(2)}) collective-permute-start(bf16[128,1024]{1,0:T(8,128)(2,1)S(1)} %collective-permute-done.24.refs_2_), channel_id=1, source_target_pairs={{0,1},{1,0},{2,3},{3,2},{4,5},{5,4},{6,7},{7,6},{8,9},{9,8},{10,11... | collective-permute-start | bytes 786440 | tf_op jit(solution)/shard_map/ppermute | solution.py:331
  63.3 9.0 %copy-start.1 = (bf16[128,2304]{1,0:T(8,128)(2,1)S(1)}, bf16[128,2304]{1,0:T(8,128)(2,1)}, u32[]{:S(2)}) copy-start(bf16[128,2304]{1,0:T(8,128)(2,1)} %copy-done) | copy-start | bytes 1769476
  86.1 15.4 %collective-permute-start.34 = (bf16[4,128,2304]{2,1,0:T(8,128)(2,1)S(1)}, bf16[4,128,2304]{2,1,0:T(8,128)(2,1)S(1)}, u32[]{:S(2)}, u32[]{:S(2)}) collective-permute-start(bf16[4,128,2304]{2,1,0:T(8,128)(2,1)S(1)} %get-tuple-element.114), channel_id=1, source_target_pairs={{0,4},{4,0},{8,12},{12,8},{16,20},{20,16},{24,28},{28,24},{1,5},{5... | collective-permute-start | bytes 7077896 | tf_op jit(solution)/shard_map/ppermute | solution.py:331
  100.9 5.2 %collective-permute-start.29 = (bf16[4,128,896]{2,1,0:T(8,128)(2,1)S(1)}, bf16[4,128,896]{2,1,0:T(8,128)(2,1)S(1)}, u32[]{:S(2)}, u32[]{:S(2)}) collective-permute-start(bf16[4,128,896]{2,1,0:T(8,128)(2,1)S(1)} %get-tuple-element.106), channel_id=1, source_target_pairs={{0,4},{4,0},{8,12},{12,8},{16,20},{20,16},{24,28},{28,24},{1,5},{5... | collective-permute-start | bytes 2752520 | tf_op jit(solution)/shard_map/ppermute | solution.py:331
  102.0 15.6 %collective-permute-start.35 = (bf16[128,2304]{1,0:T(8,128)(2,1)S(1)}, bf16[128,2304]{1,0:T(8,128)(2,1)S(1)}, u32[]{:S(2)}, u32[]{:S(2)}) collective-permute-start(bf16[128,2304]{1,0:T(8,128)(2,1)S(1)} %get-tuple-element.117), channel_id=1, source_target_pairs={{0,16},{4,12},{8,24},{12,4},{16,0},{20,28},{24,8},{28,20},{1,17},{... | collective-permute-start | bytes 1769480 | tf_op jit(solution)/shard_map/ppermute | solution.py:331
  103.6 16.2 %collective-permute-start.37 = (bf16[128,2304]{1,0:T(8,128)(2,1)S(1)}, bf16[128,2304]{1,0:T(8,128)(2,1)S(1)}, u32[]{:S(2)}, u32[]{:S(2)}) collective-permute-start(bf16[128,2304]{1,0:T(8,128)(2,1)S(1)} %get-tuple-element.118), channel_id=1, source_target_pairs={{0,8},{4,20},{8,0},{12,28},{16,24},{20,4},{24,16},{28,12},{1,9},{5... | collective-permute-start | bytes 1769480 | tf_op jit(solution)/shard_map/ppermute | solution.py:331
  104.1 14.6 %collective-permute-start.20 = (bf16[128,1024]{1,0:T(8,128)(2,1)S(1)}, bf16[128,1024]{1,0:T(8,128)(2,1)S(1)}, u32[]{:S(2)}, u32[]{:S(2)}) collective-permute-start(bf16[128,1024]{1,0:T(8,128)(2,1)S(1)} %get-tuple-element.80), channel_id=1, source_target_pairs={{0,1},{1,0},{2,3},{3,2},{4,5},{5,4},{6,7},{7,6},{8,9},{9,8},{10,11... | collective-permute-start | bytes 786440 | tf_op jit(solution)/shard_map/ppermute | solution.py:331
  106.4 15.4 %collective-permute-start.30 = (bf16[128,896]{1,0:T(8,128)(2,1)S(1)}, bf16[128,896]{1,0:T(8,128)(2,1)S(1)}, u32[]{:S(2)}, u32[]{:S(2)}) collective-permute-start(bf16[128,896]{1,0:T(8,128)(2,1)S(1)} %get-tuple-element.109), channel_id=1, source_target_pairs={{0,16},{4,12},{8,24},{12,4},{16,0},{20,28},{24,8},{28,20},{1,17},{... | collective-permute-start | bytes 688136 | tf_op jit(solution)/shard_map/ppermute | solution.py:331
  107.0 16.9 %collective-permute-start.21 = (bf16[128,1024]{1,0:T(8,128)(2,1)S(1)}, bf16[128,1024]{1,0:T(8,128)(2,1)S(1)}, u32[]{:S(2)}, u32[]{:S(2)}) collective-permute-start(bf16[128,1024]{1,0:T(8,128)(2,1)S(1)} %get-tuple-element.82), channel_id=1, source_target_pairs={{0,1},{1,0},{2,3},{3,2},{4,5},{5,4},{6,7},{7,6},{8,9},{9,8},{10,11... | collective-permute-start | bytes 786440 | tf_op jit(solution)/shard_map/ppermute | solution.py:331
  117.6 8.0 %collective-permute-start.32 = (bf16[128,896]{1,0:T(8,128)(2,1)S(1)}, bf16[128,896]{1,0:T(8,128)(2,1)S(1)}, u32[]{:S(2)}, u32[]{:S(2)}) collective-permute-start(bf16[128,896]{1,0:T(8,128)(2,1)S(1)} %get-tuple-element.110), channel_id=1, source_target_pairs={{0,8},{4,20},{8,0},{12,28},{16,24},{20,4},{24,16},{28,12},{1,9},{5... | collective-permute-start | bytes 688136 | tf_op jit(solution)/shard_map/ppermute | solution.py:331
  118.8 45.7 %collective-permute-start.36 = (bf16[128,2304]{1,0:T(8,128)(2,1)S(1)}, bf16[128,2304]{1,0:T(8,128)(2,1)S(1)}, u32[]{:S(2)}, u32[]{:S(2)}) collective-permute-start(bf16[128,2304]{1,0:T(8,128)(2,1)S(1)} %shard_map.281), channel_id=1, source_target_pairs={{0,8},{4,20},{8,0},{12,28},{16,24},{20,4},{24,16},{28,12},{1,9},{5... | collective-permute-start | bytes 1769480 | tf_op jit(solution)/shard_map/ppermute | solution.py:331
  119.9 44.6 %collective-permute-start.38 = (bf16[128,2304]{1,0:T(8,128)(2,1)S(1)}, bf16[128,2304]{1,0:T(8,128)(2,1)S(1)}, u32[]{:S(2)}, u32[]{:S(2)}) collective-permute-start(bf16[128,2304]{1,0:T(8,128)(2,1)S(1)} %collective-permute-done.37), channel_id=1, source_target_pairs={{0,4},{4,0},{8,12},{12,8},{16,20},{20,16},{24,28},{28,24},{1,5},{5... | collective-permute-start | bytes 1769480 | tf_op jit(solution)/shard_map/ppermute | solution.py:331
  121.8 7.1 %collective-permute-start.27 = (bf16[128,1024]{1,0:T(8,128)(2,1)S(1)}, bf16[128,1024]{1,0:T(8,128)(2,1)S(1)}, u32[]{:S(2)}, u32[]{:S(2)}) collective-permute-start(bf16[128,1024]{1,0:T(8,128)(2,1)S(1)} %get-tuple-element.99), channel_id=1, source_target_pairs={{0,1},{1,0},{2,3},{3,2},{4,5},{5,4},{6,7},{7,6},{8,9},{9,8},{10,11... | collective-permute-start | bytes 786440 | tf_op jit(solution)/shard_map/ppermute | solution.py:331
  123.8 8.6 %collective-permute-start.31 = (bf16[128,896]{1,0:T(8,128)(2,1)S(1)}, bf16[128,896]{1,0:T(8,128)(2,1)S(1)}, u32[]{:S(2)}, u32[]{:S(2)}) collective-permute-start(bf16[128,896]{1,0:T(8,128)(2,1)S(1)} %shard_map.278), channel_id=1, source_target_pairs={{0,8},{4,20},{8,0},{12,28},{16,24},{20,4},{24,16},{28,12},{1,9},{5... | collective-permute-start | bytes 688136 | tf_op jit(solution)/shard_map/ppermute | solution.py:331
  125.7 9.9 %collective-permute-start.33 = (bf16[128,896]{1,0:T(8,128)(2,1)S(1)}, bf16[128,896]{1,0:T(8,128)(2,1)S(1)}, u32[]{:S(2)}, u32[]{:S(2)}) collective-permute-start(bf16[128,896]{1,0:T(8,128)(2,1)S(1)} %collective-permute-done.32), channel_id=1, source_target_pairs={{0,4},{4,0},{8,12},{12,8},{16,20},{20,16},{24,28},{28,24},{1,5},{5... | collective-permute-start | bytes 688136 | tf_op jit(solution)/shard_map/ppermute | solution.py:331
  128.9 8.2 %collective-permute-start.26 = (bf16[128,1024]{1,0:T(8,128)(2,1)S(1)}, bf16[128,1024]{1,0:T(8,128)(2,1)S(1)}, u32[]{:S(2)}, u32[]{:S(2)}) collective-permute-start(bf16[128,1024]{1,0:T(8,128)(2,1)S(1)} %get-tuple-element.97), channel_id=1, source_target_pairs={{0,1},{1,0},{2,3},{3,2},{4,5},{5,4},{6,7},{7,6},{8,9},{9,8},{10,11... | collective-permute-start | bytes 786440 | tf_op jit(solution)/shard_map/ppermute | solution.py:331
  132.4 21.1 %collective-permute-start.22 = (bf16[128,1024]{1,0:T(8,128)(2,1)S(1)}, bf16[128,1024]{1,0:T(8,128)(2,1)S(1)}, u32[]{:S(2)}, u32[]{:S(2)}) collective-permute-start(bf16[128,1024]{1,0:T(8,128)(2,1)S(1)} %shard_map.268), channel_id=1, source_target_pairs={{0,2},{1,3},{2,0},{3,1},{4,6},{5,7},{6,4},{7,5},{8,10},{9,11},{10,... | collective-permute-start | bytes 786440 | tf_op jit(solution)/shard_map/ppermute | solution.py:331
  135.6 22.4 %collective-permute-start.28 = (bf16[128,1024]{1,0:T(8,128)(2,1)S(1)}, bf16[128,1024]{1,0:T(8,128)(2,1)S(1)}, u32[]{:S(2)}, u32[]{:S(2)}) collective-permute-start(bf16[128,1024]{1,0:T(8,128)(2,1)S(1)} %shard_map.274), channel_id=1, source_target_pairs={{0,2},{1,3},{2,0},{3,1},{4,6},{5,7},{6,4},{7,5},{8,10},{9,11},{10,... | collective-permute-start | bytes 786440 | tf_op jit(solution)/shard_map/ppermute | solution.py:331
  137.1 26.2 %collective-permute-start.39 = (f32[8,32]{1,0:T(8,128)S(1)}, f32[8,32]{1,0:T(8,128)S(1)}, u32[]{:S(2)}, u32[]{:S(2)}) collective-permute-start(f32[8,32]{1,0:T(8,128)S(1)} %get-tuple-element.121), channel_id=1, source_target_pairs={{0,1},{1,0},{2,3},{3,2},{4,5},{5,4},{6,7},{7,6},{8,9},{9,8},{10,11... | collective-permute-start | bytes 3080 | tf_op jit(solution)/shard_map/ppermute | solution.py:331
  153.6 9.7 %collective-permute-start.40 = (f32[8,32]{1,0:T(8,128)S(1)}, f32[8,32]{1,0:T(8,128)S(1)}, u32[]{:S(2)}, u32[]{:S(2)}) collective-permute-start(f32[8,32]{1,0:T(8,128)S(1)} %get-tuple-element.122), channel_id=1, source_target_pairs={{0,2},{1,3},{2,0},{3,1},{4,6},{5,7},{6,4},{7,5},{8,10},{9,11},{10,... | collective-permute-start | bytes 3080 | tf_op jit(solution)/shard_map/ppermute | solution.py:331
  158.0 5.4 %collective-permute-start.41 = (f32[8,32]{1,0:T(8,128)S(1)}, f32[8,32]{1,0:T(8,128)S(1)}, u32[]{:S(2)}, u32[]{:S(2)}) collective-permute-start(f32[8,32]{1,0:T(8,128)S(1)} %get-tuple-element.123), channel_id=1, source_target_pairs={{0,3},{1,2},{2,1},{3,0},{4,7},{5,6},{6,5},{7,4},{8,11},{9,10},{10,... | collective-permute-start | bytes 3080 | tf_op jit(solution)/shard_map/ppermute | solution.py:331

commit v3 on v2

--- a/solution.py
+++ b/solution.py
@@ -440,7 +440,8 @@
     out[...] = (one[...].astype(jnp.float32) + two[...].astype(jnp.float32)).astype(out.dtype)
 
 
-def pack_body(inner, outer, dense, x, g, message, x_copy, g_copy):
+def pack_body(inner, outer, dense, x, g, segs, message, x_copy, g_copy, segs_copy):
+    segs_copy[...] = segs[...]
     x_copy[...] = x[...]
     g_copy[...] = g[...]
     strip, units = inner.shape
@@ -498,18 +499,21 @@
         dense[strip * i : strip * (i + 1), :] = total[:, 2 * units + strip * i : 2 * units + strip * (i + 1)]
 
 
-def unpack_rest_body(sizes, scal, own, near, far, qkv, qkv_b, inner_b, *fives):
-    strip, cols, heads, lanes = sizes
-    total = own[...].astype(jnp.float32) + near[...].astype(jnp.float32) + far[...].astype(jnp.float32)
-    qkv[...] = total[:, :cols]
-    tiny = total[:, cols:]
+def unpack_rest_body(scal, own, near, far, qkv):
+    qkv[...] = own[...].astype(jnp.float32) + near[...].astype(jnp.float32) + far[...].astype(jnp.float32)
+
+
+def unpack_small_body(sizes, scal, own, near, far, qkv_b, inner_b, *fives):
+    strip, heads, lanes = sizes
+    tiny = own[...].astype(jnp.float32) + near[...].astype(jnp.float32) + far[...].astype(jnp.float32)
     for i, out in enumerate((qkv_b, inner_b)):
         at = 8 + 2 * heads * i
         pair = jnp.concatenate([tiny[at : at + heads], tiny[at + heads : at + 2 * heads]], axis=1)
         count = out.shape[1]
         out[...] = pltpu.roll(pair, 2 * strip - scal[9] * count, 1)[:, :count]
+    mine = pltpu.roll(tiny[0:8], strip - scal[8] * lanes, 1)[:, :lanes]
     for k, out in enumerate(fives):
-        out[...] = pltpu.roll(tiny[0:8], strip - (scal[8] ^ k) * lanes, 1)[:, :lanes]
+        out[...] = mine[k]
 
 
 def result_body(m, scal, x, vec, *refs):
@@ -600,26 +604,33 @@
     lax.fori_loop(0, m, one_sequence, 0, unroll=UNROLL)
 
 
-def feed_body(m, sizes, scal, *refs):
-    strip, units, wide = sizes
-    second, context, inner_b, blocks = refs[0], refs[1], refs[2], refs[3:11]
-    inner, outer, dense, bend, act = refs[11:16]
-    outs = refs[16:]
+def feed_act_body(m, sizes, scal, *refs):
+    strip, units = sizes
+    second, inner_b, blocks = refs[0], refs[1], refs[2:10]
+    inner, bend, act = refs[10:]
     for slot, view in enumerate(blocks):
-        k = scal[slot]
-        at = pl.ds(pl.multiple_of(k * strip, strip), strip)
-        inner[at, :] = view[:, :units]
-        for i in range(units // strip):
-            outer[strip * i : strip * (i + 1), at] = view[:, units + strip * i : units + strip * (i + 1)]
-        for i in range(wide // strip):
-            dense[strip * i : strip * (i + 1), at] = view[:, 2 * units + strip * i : 2 * units + strip * (i + 1)]
-    rows = outs[0].shape[0]
+        inner[pl.ds(pl.multiple_of(scal[slot] * strip, strip), strip), :] = view[:, :units]
+    rows = second.shape[0] // m
     for s in range(m):
         at = slice(rows * s, rows * (s + 1))
         value = jnp.dot(second[at, :], inner[...], preferred_element_type=jnp.float32) + inner_b[...]
         half = 0.5 * (1.0 + erf_value(value * ROOT_HALF))
         act[at, :] = (value * half).astype(jnp.bfloat16)
         bend[at, :] = half + value * jnp.exp(-0.5 * value * value) * INV_ROOT_TAU
+
+
+def feed_out_body(m, sizes, scal, *refs):
+    strip, units, wide = sizes
+    act, context, blocks = refs[0], refs[1], refs[2:10]
+    outer, dense = refs[10:12]
+    outs = refs[12:]
+    for slot, view in enumerate(blocks):
+        at = pl.ds(pl.multiple_of(scal[slot] * strip, strip), strip)
+        for i in range(units // strip):
+            outer[strip * i : strip * (i + 1), at] = view[:, units + strip * i : units + strip * (i + 1)]
+        for i in range(wide // strip):
+            dense[strip * i : strip * (i + 1), at] = view[:, 2 * units + strip * i : 2 * units + strip * (i + 1)]
+    rows = outs[0].shape[0]
     for s in range(m):
         at = slice(rows * s, rows * (s + 1))
         mixed = jnp.dot(act[at, :], outer[...], preferred_element_type=jnp.float32)
@@ -721,18 +732,24 @@
     five[...] = jnp.concatenate([own] + sums + [jnp.zeros((3, width), jnp.float32)], axis=0)
 
 
-def rest_body(sizes, scal, first, head_half, tail_half, head_grad, tail_grad, inner_grad, *refs):
-    strip, qkv_cols, heads = sizes
-    five, keep, send, d_packed_b = refs
+def rest_body(strip, scal, first, head_half, tail_half, keep, send, d_packed_b):
     count = head_half.shape[0]
     d_packed_b[:count, :] = head_half[...]
     d_packed_b[count:, :] = tail_half[...]
-    qkv_grad = head_grad[...] + tail_grad[...]
-    pairs = destinations(scal, keep, send)
-    for pair in pairs:
+    for pair in destinations(scal, keep, send):
         grad = matmul(two_blocks(first, pair, strip), d_packed_b[...], 0, 0).astype(jnp.bfloat16)
         for j, (unused_result, place) in enumerate(pair):
-            place[:, :qkv_cols] = grad[strip * j : strip * (j + 1)]
+            place[...] = grad[strip * j : strip * (j + 1)]
+
+
+def small_body(sizes, scal, head_grad, tail_grad, inner_grad, *refs):
+    strip, heads = sizes
+    fives, (keep, send, five) = refs[:-3], refs[-3:]
+    total = fives[0][...]
+    for part in fives[1:]:
+        total = total + part[...]
+    five[...] = total
+    qkv_grad = head_grad[...] + tail_grad[...]
     rows = [[], [], [], []]
     for h in range(heads):
         at = 3 * HD * h
@@ -744,19 +761,11 @@
         )
         rows[2].append(inner_grad[:, 2 * strip * h : 2 * strip * h + strip])
         rows[3].append(inner_grad[:, 2 * strip * h + strip : 2 * strip * (h + 1)])
-    tail = jnp.concatenate(sum(rows, []) + [jnp.zeros((strip - 8 - 4 * heads, strip), jnp.float32)], axis=0)
-    for k, place in sum(pairs, []):
+    spare = keep.shape[1] - 8 - 4 * heads
+    tail = jnp.concatenate(sum(rows, []) + [jnp.zeros((spare, strip), jnp.float32)], axis=0)
+    for k, place in sum(destinations(scal, keep, send), []):
         five_k = five[0:8, pl.ds(pl.multiple_of(k * strip, strip), strip)]
-        place[:, qkv_cols : qkv_cols + strip] = jnp.concatenate([five_k, tail], axis=0).astype(jnp.bfloat16)
-
-
-def five_body(scal, *refs):
-    parts, outs = refs[:-5], refs[-5:]
-    total = parts[0][...]
-    for part in parts[1:]:
-        total = total + part[...]
-    for k, out in enumerate(outs):
-        out[...] = total[k : k + 1]
+        place[...] = jnp.concatenate([five_k, tail], axis=0).astype(jnp.bfloat16)
 
 
 def finish_body(m, scal, *refs):
@@ -810,10 +819,10 @@
     slot_to_block = [f ^ masks[s] for s in range(8)]
     scal = jnp.stack(slot_to_block + [t, f]).astype(jnp.int32)
 
-    second_msg, x_own, g_own = pl.pallas_call(
+    second_msg, x_own, g_own, segs = pl.pallas_call(
         pack_body,
-        out_shape=[pltpu.VMEM((strip, 2 * units + wide), bf), pltpu.VMEM(x.shape, bf), pltpu.VMEM(x.shape, bf)],
-    )(inner_weight, outer_weight, dense_weight, x, g)
+        out_shape=[pltpu.VMEM((strip, 2 * units + wide), bf), pltpu.VMEM(x.shape, bf), pltpu.VMEM(x.shape, bf), pltpu.VMEM(segments.shape[1:], jnp.int32)],
+    )(inner_weight, outer_weight, dense_weight, x, g, segments[0])
     x_slots = [x_own] + depth_gather(x)[1:]
     as_row = lambda v: v.reshape(1, lanes)
     vectors = (
@@ -832,7 +841,6 @@
     g_slots = [g_own] + depth_gather(g)[1:]
     poss = jnp.concatenate([lax.dynamic_slice_in_dim(positions[0], t ^ k, 1, 0) for k in range(m)])
     tables = turn_tables(poss.reshape(m * rows, 1))
-    segs = segments[0]
     tokens = m * rows
     sizes = (strip, qkv_cols)
     first, second, turned, probs, context, qkv_w, vec, inner_b = call(
@@ -850,13 +858,17 @@
         [scal, *x_slots, *first_blocks, *shares, segs, *tables],
         [pltpu.VMEM((8, 16, strip), fl)],
     )
-    inner_w, outer_w, dense_w, bend, act, *partial = call(
-        functools.partial(feed_body, m, (strip, units, wide)),
-        [((width, units), bf), ((units, width), bf), ((wide, width), bf), ((tokens, units), fl), ((tokens, units), bf)]
-        + [((rows, width), bf)] * m,
-        [scal, second, context, inner_b, *second_blocks],
-    )
-    mixed = depth_scatter(partial)
+    inner_w, bend, act = call(
+        functools.partial(feed_act_body, m, (strip, units)),
+        [((width, units), bf), ((tokens, units), fl), ((tokens, units), bf)],
+        [scal, second, inner_b, *second_blocks],
+    )
+    outer_w, dense_w, *partial = call(
+        functools.partial(feed_out_body, m, (strip, units, wide)),
+        [((units, width), bf), ((wide, width), bf)] + [((rows, width), bf)] * m,
+        [scal, act, context, *second_blocks],
+    )
+    mixed = [partial[0]] + [depth_swap(partial[k], k) for k in range(1, m)]
     big_keep, big_send, slope, inner_grad, cot = call(
         functools.partial(feed_back_body, m, (strip, units, wide)),
         [
@@ -885,13 +897,22 @@
         [scal, *x_slots, cot, *halves, qkv_w, slope, inner_w, vec],
     )
     rest_keep, rest_send = call(
-        functools.partial(rest_body, (strip, qkv_cols, heads)),
-        [((4, strip, qkv_cols + strip), bf)] * 2,
-        [scal, first, *halves, *grads, inner_grad, five],
+        functools.partial(rest_body, strip),
+        [((4, strip, qkv_cols), bf)] * 2,
+        [scal, first, *halves],
         [pltpu.VMEM((tokens, qkv_cols), bf)],
+    )
+    fives = [five] + [depth_swap(five, k) for k in range(1, m)]
+    small_rows = -(-(8 + 4 * heads) // 16) * 16
+    small_keep, small_send = call(
+        functools.partial(small_body, (strip, heads)),
+        [((4, small_rows, strip), bf)] * 2,
+        [scal, *grads, inner_grad, *fives],
+        [pltpu.VMEM((8, width), fl)],
     )
     arrived = depth_scatter(norms)
     rest = scatter_sum(rest_keep, rest_send)
+    small = scatter_sum(small_keep, small_send)
     (result,) = call(
         functools.partial(result_body, len(mixed)), [((rows, width), bf)], [scal, x_own, vec, *mixed], final=True
     )
@@ -901,18 +922,16 @@
         [scal, *big],
         final=True,
     )
-    s_qkv, s_qkv_b, s_inner_b, *fives = call(
-        functools.partial(unpack_rest_body, (strip, qkv_cols, heads, lanes)),
-        [((strip, qkv_cols), fl), (qkv_bias.shape, fl), (inner_bias.shape, fl)] + [((8, lanes), fl)] * m,
-        [scal, *rest],
+    (s_qkv,) = call(unpack_rest_body, [((strip, qkv_cols), fl)], [scal, *rest], final=True)
+    s_qkv_b, s_inner_b, *five = call(
+        functools.partial(unpack_small_body, (strip, heads, lanes)),
+        [(qkv_bias.shape, fl), (inner_bias.shape, fl)] + [((lanes,), fl)] * 5,
+        [scal, *small],
         final=True,
     )
     (in_grad,) = call(
         functools.partial(finish_body, len(arrived)), [((rows, width), bf)], [scal, x_own, g_own, *arrived], final=True
     )
-    fives = [fives[0]] + [depth_swap(fives[k], k) for k in range(1, m)]
-    five = call(five_body, [((1, lanes), fl)] * 5, [scal, *fives], final=True)
-    five = [v.reshape(lanes) for v in five]
     return (
         result[None],
         in_grad[None],

time: 168 us -> 181 us (1.077)
  starting transfers between devices: 41.6 us -> 53.2 us
  waiting for transfers between devices: 73 us -> 67.4 us
  local copies, waits for them, and re-layouts: 2.91 us -> 7.72 us
  Pallas kernels: 47.7 us -> 50.1 us
    ppermute x42 -> x47, starting transfers between devices: 41.6 us -> 53.2 us  [swap(): return lax.ppermute(value, axis, [(i, partner(i)) for i in range(count)])]
    ppermute x42 -> x47, waiting for transfers between devices: 73 us -> 67.4 us  [swap(): return lax.ppermute(value, axis, [(i, partner(i)) for i in range(count)])]
    unnamed x9 -> x27, local copies, waits for them, and re-layouts: 1.99 us -> 6.8 us
    pallas_call x20 -> x23, Pallas kernels: 46.4 us -> 48.8 us  [call(): pl.pallas_call(body, out_shape=[jax.ShapeDtypeStruct(*out) if final else...]
  transfers between devices with their start and end apart: 42 -> 47, of which waited for: 15 -> 19; matrix products, arithmetic and copies ran while one was open for 1% -> 1% of each run, Pallas kernels for 23% -> 23%
where the time goes in v3:
time: 181 us; the launch traced here: 180 us
  waiting for transfers between devices  67.4 us (37%)
  starting transfers between devices  53.2 us (29%)
  Pallas kernels  50.1 us (28%)
  local copies, waits for them, and re-layouts  7.72 us (4%)
    ppermute x47, waiting for transfers between devices, swap(): return lax.ppermute(value, axis, [(i, partner(i)) for i in range(count)])  67.4 us
    ppermute x47, starting transfers between devices, swap(): return lax.ppermute(value, axis, [(i, partner(i)) for i in range(count)])  53.2 us
    pallas_call x23, Pallas kernels, call(): pl.pallas_call(body, out_shape=[jax.ShapeDtypeStruct(*out) if final else...  48.8 us
    unnamed x27, local copies, waits for them, and re-layouts  6.8 us
  transfers between devices with their start and end apart: 47, of which 19 were waited for; matrix products, arithmetic and copies ran while one was open for 1% of the time, Pallas kernels for 23%

profile of v3, /device:TPU:0, one launch (start us, length us, event | category | flops | bytes accessed | tf_op | source)
XLA Modules:
  0.0 180.5 jit_solution(12075815600690328767)
XLA Ops:
  0.6 1.3 shard_map.263
  2.0 0.7 copy-done.2
  3.2 2.5 %collective-permute-start.14 = (bf16[128,2304]{1,0:T(8,128)(2,1)S(1)}, bf16[128,2304]{1,0:T(8,128)(2,1)S(1)}, u32[]{:S(2)}, u32[]{:S(2)}) collective-permute-start(bf16[128,2304]{1,0:T(8,128)(2,1)S(1)} %get-tuple-element.80.refs_2_), channel_id=1, source_target_pairs={{0,8},{4,20},{8,0},{12,28},{16,24},{20,4},{24,16},{28,12},{1,9},{5... | collective-permute-start | bytes 1769480 | tf_op jit(solution)/shard_map/ppermute | solution.py:331
  5.7 1.1 shard_map.264.refs_0_.refs_4_
  7.2 1.5 collective-permute-start.4
  8.7 1.6 collective-permute-start
  10.3 2.6 %collective-permute-start.1 = (bf16[128,1024]{1,0:T(8,128)(2,1)}, bf16[128,1024]{1,0:T(8,128)(2,1)}, u32[]{:S(2)}, u32[]{:S(2)}) collective-permute-start(bf16[128,1024]{1,0:T(8,128)(2,1)} %bitcast.32), channel_id=1, source_target_pairs={{0,2},{1,3},{2,0},{3,1},{4,6},{5,7},{6,4},{7,5},{8,10},{9,11},{10,... | collective-permute-start | bytes 786440 | tf_op jit(solution)/shard_map/ppermute | solution.py:331
  13.5 2.1 %collective-permute-start.18 = (bf16[128,2304]{1,0:T(8,128)(2,1)S(1)}, bf16[128,2304]{1,0:T(8,128)(2,1)S(1)}, u32[]{:S(2)}, u32[]{:S(2)}) collective-permute-start(bf16[128,2304]{1,0:T(8,128)(2,1)S(1)} %collective-permute-done.14.refs_4_), channel_id=1, source_target_pairs={{0,16},{4,12},{8,24},{12,4},{16,0},{20,28},{24,8},{28,20},{1,17},{... | collective-permute-start | bytes 1769480 | tf_op jit(solution)/shard_map/ppermute | solution.py:331
  16.0 2.2 %collective-permute-start.5 = (bf16[128,896]{1,0:T(8,128)(2,1)S(1)}, bf16[128,896]{1,0:T(8,128)(2,1)}, u32[]{:S(2)}, u32[]{:S(2)}) collective-permute-start(bf16[128,896]{1,0:T(8,128)(2,1)S(1)} %collective-permute-done.3.refs_1_.refs_5_), channel_id=1, source_target_pairs={{0,8},{4,20},{8,0},{12,28},{16,24},{20,4},{24,16},{28,12},{1,9},{5... | collective-permute-start | bytes 688136 | tf_op jit(solution)/shard_map/ppermute | solution.py:331
  18.2 0.7 copy-done.4
  18.9 3.7 %collective-permute-done.refs_1_ = bf16[128,1024]{1,0:T(8,128)(2,1)S(1)} collective-permute-done((bf16[128,1024]{1,0:T(8,128)(2,1)}, bf16[128,1024]{1,0:T(8,128)(2,1)S(1)}, u32[]{:S(2)}, u32[]{:S(2)}) %collective-permute-start) | collective-permute-done | bytes 262176 | tf_op jit(solution)/shard_map/ppermute | solution.py:331
  22.6 0.7 copy-done
  23.8 1.3 collective-permute-done.1.refs_2_
  25.1 0.7 copy-done.6
  25.8 7.9 %collective-permute-done.5.refs_3_.refs_7_ = bf16[128,896]{1,0:T(8,128)(2,1)} collective-permute-done((bf16[128,896]{1,0:T(8,128)(2,1)S(1)}, bf16[128,896]{1,0:T(8,128)(2,1)}, u32[]{:S(2)}, u32[]{:S(2)}) %collective-permute-start.5) | collective-permute-done | bytes 229408 | tf_op jit(solution)/shard_map/ppermute | solution.py:331
  34.2 0.7 copy-done.9
  34.9 3.0 %collective-permute-start.24 = (bf16[128,1024]{1,0:T(8,128)(2,1)}, bf16[128,1024]{1,0:T(8,128)(2,1)}, u32[]{:S(2)}, u32[]{:S(2)}) collective-permute-start(bf16[128,1024]{1,0:T(8,128)(2,1)} %bitcast.34), channel_id=1, source_target_pairs={{0,2},{1,3},{2,0},{3,1},{4,6},{5,7},{6,4},{7,5},{8,10},{9,11},{10,... | collective-permute-start | bytes 786440 | tf_op jit(solution)/shard_map/ppermute | solution.py:331
  38.0 1.6 collective-permute-start.2
  39.5 0.8 fusion.5
  41.1 0.9 copy-done.5
  42.0 0.9 copy-done.7
  42.9 0.9 copy-done.10
  43.9 1.3 shard_map.265
  45.2 5.2 %collective-permute-done.24.refs_2_ = bf16[128,1024]{1,0:T(8,128)(2,1)} collective-permute-done((bf16[128,1024]{1,0:T(8,128)(2,1)}, bf16[128,1024]{1,0:T(8,128)(2,1)}, u32[]{:S(2)}, u32[]{:S(2)}) %collective-permute-start.24) | collective-permute-done | bytes 262176 | tf_op jit(solution)/shard_map/ppermute | solution.py:331
  50.5 0.6 collective-permute-start.10
  51.1 3.4 %collective-permute-start.11 = (bf16[8,16,128]{2,1,0:T(8,128)(2,1)S(1)}, bf16[8,16,128]{2,1,0:T(8,128)(2,1)S(1)}, u32[]{:S(2)}, u32[]{:S(2)}) collective-permute-start(bf16[8,16,128]{2,1,0:T(8,128)(2,1)S(1)} %shard_map.265), channel_id=1, source_target_pairs={{0,2},{1,3},{2,0},{3,1},{4,6},{5,7},{6,4},{7,5},{8,10},{9,11},{10,... | collective-permute-start | bytes 98312 | tf_op jit(solution)/shard_map/ppermute | solution.py:331
  54.5 3.6 %collective-permute-start.12 = (bf16[8,16,128]{2,1,0:T(8,128)(2,1)S(1)}, bf16[8,16,128]{2,1,0:T(8,128)(2,1)S(1)}, u32[]{:S(2)}, u32[]{:S(2)}) collective-permute-start(bf16[8,16,128]{2,1,0:T(8,128)(2,1)S(1)} %shard_map.265), channel_id=1, source_target_pairs={{0,3},{1,2},{2,1},{3,0},{4,7},{5,6},{6,5},{7,4},{8,11},{9,10},{10,... | collective-permute-start | bytes 98312 | tf_op jit(solution)/shard_map/ppermute | solution.py:331
  58.3 2.1 %collective-permute-done.12.refs_14_ = bf16[8,16,128]{2,1,0:T(8,128)(2,1)S(1)} collective-permute-done((bf16[8,16,128]{2,1,0:T(8,128)(2,1)S(1)}, bf16[8,16,128]{2,1,0:T(8,128)(2,1)S(1)}, u32[]{:S(2)}, u32[]{:S(2)}) %collective-permute-start.12) | collective-permute-done | bytes 32800 | tf_op jit(solution)/shard_map/ppermute | solution.py:331
  60.4 1.0 fusion
  61.4 8.7 %shard_map.266 = (bf16[512,1024]{1,0:T(8,128)(2,1)S(1)}, bf16[512,1024]{1,0:T(8,128)(2,1)S(1)}, bf16[512,768]{1,0:T(8,128)(2,1)S(1)}, f32[16,128,128]{2,1,0:T(8,...) custom-call(s32[10]{0:T(128)S(1)} %stack.40.scal, ...), custom_call_target="tpu_custom_call" | custom-call | tf_op jit(solution)/shard_map/pallas_call | solution.py:424
  70.2 4.2 %shard_map.267 = (bf16[1024,1024]{1,0:T(8,128)(2,1)S(1)}, f32[512,1024]{1,0:T(8,128)S(1)}, bf16[512,1024]{1,0:T(8,128)(2,1)S(1)}) custom-call(s32[10]{0:T(128)S(1)} %stack.40.scal, bf16[512,1024]{1,0:T(8,128)(2,1)S(1)} %get-tuple-element.78.refs_0_.refs_6_, f32[1,1024]{1,0:T(1,128)S(1)} %get-tuple-element.79.refs_1_, ...), custom_call_target="tpu_custom_call" | custom-call | tf_op jit(solution)/shard_map/pallas_call | solution.py:424
  74.4 3.0 %shard_map.268 = (bf16[1024,1024]{1,0:T(8,128)(2,1)S(1)}, bf16[256,1024]{1,0:T(8,128)(2,1)S(1)}, bf16[128,1024]{1,0:T(8,128)(2,1)S(1)}, bf16[128,1024]{1,0:T(8,1...) custom-call(s32[10]{0:T(128)S(1)} %stack.40.scal, ...), custom_call_target="tpu_custom_call" | custom-call | tf_op jit(solution)/shard_map/pallas_call | solution.py:424
  77.4 6.5 %shard_map.270 = (bf16[4,128,2304]{2,1,0:T(8,128)(2,1)S(1)}, bf16[4,128,2304]{2,1,0:T(8,128)(2,1)S(1)}, bf16[512,1024]{1,0:T(8,128)(2,1)S(1)}, f32[1,1024]{1,0:T(1,128)S(1)}, bf16[512,1024]{1,0:T(8,128)(2,1)S(1)}) custom-call(s32[10]{0:T(128)S(1)} %stack.40.scal, bf16[128,1024]{1,0:T(8,128)(2,1)S(1)} %copy-done.3, ...), custom_call_target="tpu_custom_call" | custom-call | tf_op jit(solution)/shard_map/pallas_call | solution.py:424
  83.9 3.5 %shard_map.271 = (bf16[256,768]{1,0:T(8,128)(2,1)S(1)}, f32[1,768]{1,0:T(1,128)S(1)}) custom-call(s32[10]{0:T(128)S(1)} %stack.40.scal, bf16[512,1024]{1,0:T(8,128)(2,1)S(1)} %get-tuple-element.90.refs_0_.refs_4_, bf16[512,256]{1,0:T(8,128)(2,1)S(1)} %get-tuple-element.82.refs_1_.refs_7_, bf16[256,1024]{1,0:T(8,128)(2,1)S(1)} %get-tuple-element.91.refs_2_, ...), custom_call_target="tpu_custom_call" | custom-call | tf_op jit(solution)/shard_map/pallas_call | solution.py:424
  87.5 3.5 %shard_map.272 = (bf16[256,768]{1,0:T(8,128)(2,1)S(1)}, f32[1,768]{1,0:T(1,128)S(1)}) custom-call(s32[10]{0:T(128)S(1)} %stack.40.scal, bf16[512,1024]{1,0:T(8,128)(2,1)S(1)} %get-tuple-element.90.refs_0_.refs_4_, bf16[512,256]{1,0:T(8,128)(2,1)S(1)} %get-tuple-element.82.refs_1_.refs_7_, bf16[256,1024]{1,0:T(8,128)(2,1)S(1)} %get-tuple-element.91.refs_2_, ...), custom_call_target="tpu_custom_call" | custom-call | tf_op jit(solution)/shard_map/pallas_call | solution.py:424
  91.0 1.6 shard_map.276
  93.7 1.6 collective-permute-start.43
  95.3 1.5 collective-permute-start.45
  96.8 2.0 %collective-permute-start.20 = (bf16[128,1024]{1,0:T(8,128)(2,1)S(1)}, bf16[128,1024]{1,0:T(8,128)(2,1)S(1)}, u32[]{:S(2)}, u32[]{:S(2)}) collective-permute-start(bf16[128,1024]{1,0:T(8,128)(2,1)S(1)} %get-tuple-element.84), channel_id=1, source_target_pairs={{0,1},{1,0},{2,3},{3,2},{4,5},{5,4},{6,7},{7,6},{8,9},{9,8},{10,11... | collective-permute-start | bytes 786440 | tf_op jit(solution)/shard_map/ppermute | solution.py:331
  98.8 6.4 %shard_map.273 = (bf16[128,1024]{1,0:T(8,128)(2,1)S(1)}, bf16[128,1024]{1,0:T(8,128)(2,1)S(1)}, bf16[128,1024]{1,0:T(8,128)(2,1)S(1)}, bf16[128,1024]{1,0:T(8,128)(2,1)S(1)}, f32[8,1024]{1,0:T(8,128)S(1)}) custom-call(s32[10]{0:T(128)S(1)} %stack.40.scal, bf16[128,1024]{1,0:T(8,128)(2,1)S(1)} %get-tuple-element.75.refs_0_.x, ...), custom_call_target="tpu_custom_call" | custom-call | tf_op jit(solution)/shard_map/pallas_call | solution.py:424
  105.3 3.9 %collective-permute-done.34.refs_1_ = f32[8,1024]{1,0:T(8,128)S(1)} collective-permute-done((f32[8,1024]{1,0:T(8,128)S(1)}, f32[8,1024]{1,0:T(8,128)S(1)}, u32[]{:S(2)}, u32[]{:S(2)}) %collective-permute-start.34) | collective-permute-done | bytes 32800 | tf_op jit(solution)/shard_map/ppermute | solution.py:331
  109.2 2.4 %collective-permute-start.35 = (f32[8,1024]{1,0:T(8,128)S(1)}, f32[8,1024]{1,0:T(8,128)S(1)}, u32[]{:S(2)}, u32[]{:S(2)}) collective-permute-start(f32[8,1024]{1,0:T(8,128)S(1)} %get-tuple-element.113.refs_0_), channel_id=1, source_target_pairs={{0,2},{1,3},{2,0},{3,1},{4,6},{5,7},{6,4},{7,5},{8,10},{9,11},{10,... | collective-permute-start | bytes 98312 | tf_op jit(solution)/shard_map/ppermute | solution.py:331
  111.7 2.4 %collective-permute-done.35.refs_2_ = f32[8,1024]{1,0:T(8,128)S(1)} collective-permute-done((f32[8,1024]{1,0:T(8,128)S(1)}, f32[8,1024]{1,0:T(8,128)S(1)}, u32[]{:S(2)}, u32[]{:S(2)}) %collective-permute-start.35) | collective-permute-done | bytes 32800 | tf_op jit(solution)/shard_map/ppermute | solution.py:331
  114.0 4.1 %collective-permute-start.36 = (f32[8,1024]{1,0:T(8,128)S(1)}, f32[8,1024]{1,0:T(8,128)S(1)}, u32[]{:S(2)}, u32[]{:S(2)}) collective-permute-start(f32[8,1024]{1,0:T(8,128)S(1)} %get-tuple-element.113.refs_0_), channel_id=1, source_target_pairs={{0,3},{1,2},{2,1},{3,0},{4,7},{5,6},{6,5},{7,4},{8,11},{9,10},{10,... | collective-permute-start | bytes 98312 | tf_op jit(solution)/shard_map/ppermute | solution.py:331
  118.1 1.9 %collective-permute-done.36.refs_3_ = f32[8,1024]{1,0:T(8,128)S(1)} collective-permute-done((f32[8,1024]{1,0:T(8,128)S(1)}, f32[8,1024]{1,0:T(8,128)S(1)}, u32[]{:S(2)}, u32[]{:S(2)}) %collective-permute-start.36) | collective-permute-done | bytes 32800 | tf_op jit(solution)/shard_map/ppermute | solution.py:331
  120.0 0.6 shard_map.280
  120.7 1.2 collective-permute-done.37.got
  121.9 0.6 collective-permute-start.38
  122.5 3.1 %collective-permute-done.38.two = bf16[32,128]{1,0:T(8,128)(2,1)S(1)} collective-permute-done((bf16[32,128]{1,0:T(8,128)(2,1)S(1)}, bf16[32,128]{1,0:T(8,128)(2,1)S(1)}, u32[]{:S(2)}, u32[]{:S(2)}) %collective-permute-start.38) | collective-permute-done | bytes 8224 | tf_op jit(solution)/shard_map/ppermute | solution.py:331
  126.2 3.1 %collective-permute-done.40 = bf16[32,128]{1,0:T(8,128)(2,1)S(1)} collective-permute-done((bf16[32,128]{1,0:T(8,128)(2,1)S(1)}, bf16[32,128]{1,0:T(8,128)(2,1)S(1)}, u32[]{:S(2)}, u32[]{:S(2)}) %collective-permute-start.40) | collective-permute-done | bytes 8224 | tf_op jit(solution)/shard_map/ppermute | solution.py:331
  129.9 3.1 %collective-permute-done.39.near = bf16[32,128]{1,0:T(8,128)(2,1)S(1)} collective-permute-done((bf16[32,128]{1,0:T(8,128)(2,1)S(1)}, bf16[32,128]{1,0:T(8,128)(2,1)S(1)}, u32[]{:S(2)}, u32[]{:S(2)}) %collective-permute-start.39) | collective-permute-done | bytes 8224 | tf_op jit(solution)/shard_map/ppermute | solution.py:331
  133.0 1.2 collective-permute-done.41.far
  134.5 3.5 %collective-permute-start.22 = (bf16[128,1024]{1,0:T(8,128)(2,1)S(1)}, bf16[128,1024]{1,0:T(8,128)(2,1)S(1)}, u32[]{:S(2)}, u32[]{:S(2)}) collective-permute-start(bf16[128,1024]{1,0:T(8,128)(2,1)S(1)} %get-tuple-element.86), channel_id=1, source_target_pairs={{0,3},{1,2},{2,1},{3,0},{4,7},{5,6},{6,5},{7,4},{8,11},{9,10},{10,... | collective-permute-start | bytes 786440 | tf_op jit(solution)/shard_map/ppermute | solution.py:331
  138.0 0.6 collective-permute-start.27
  138.7 0.6 collective-permute-start.44
  139.5 15.9 %collective-permute-done.21.refs_2_ = bf16[128,1024]{1,0:T(8,128)(2,1)S(1)} collective-permute-done((bf16[128,1024]{1,0:T(8,128)(2,1)S(1)}, bf16[128,1024]{1,0:T(8,128)(2,1)S(1)}, u32[]{:S(2)}, u32[]{:S(2)}) %collective-permute-start.21) | collective-permute-done | bytes 262176 | tf_op jit(solution)/shard_map/ppermute | solution.py:331
  156.0 4.9 %collective-permute-start.26 = (bf16[128,1024]{1,0:T(8,128)(2,1)S(1)}, bf16[128,1024]{1,0:T(8,128)(2,1)S(1)}, u32[]{:S(2)}, u32[]{:S(2)}) collective-permute-start(bf16[128,1024]{1,0:T(8,128)(2,1)S(1)} %get-tuple-element.100), channel_id=1, source_target_pairs={{0,1},{1,0},{2,3},{3,2},{4,5},{5,4},{6,7},{7,6},{8,9},{9,8},{10,11... | collective-permute-start | bytes 786440 | tf_op jit(solution)/shard_map/ppermute | solution.py:331
  161.6 9.6 %collective-permute-done.26.refs_3_ = bf16[128,1024]{1,0:T(8,128)(2,1)S(1)} collective-permute-done((bf16[128,1024]{1,0:T(8,128)(2,1)S(1)}, bf16[128,1024]{1,0:T(8,128)(2,1)S(1)}, u32[]{:S(2)}, u32[]{:S(2)}) %collective-permute-start.26) | collective-permute-done | bytes 262176 | tf_op jit(solution)/shard_map/ppermute | solution.py:331
  171.5 1.2 shard_map.283
  172.7 1.4 shard_map.269
  174.1 0.9 collective-permute-done.28.refs_4_
  175.0 1.7 shard_map.275
  176.9 1.4 shard_map.279
  178.3 1.6 shard_map.286
  (88 shorter events, 9.1 us)
Async XLA Ops:
  2.0 0.7 copy-start.2
  2.7 10.2 %collective-permute-start.13 = (bf16[128,2304]{1,0:T(8,128)(2,1)S(1)}, bf16[128,2304]{1,0:T(8,128)(2,1)S(1)}, u32[]{:S(2)}, u32[]{:S(2)}) collective-permute-start(bf16[128,2304]{1,0:T(8,128)(2,1)S(1)} %get-tuple-element.80.refs_2_), channel_id=1, source_target_pairs={{0,4},{4,0},{8,12},{12,8},{16,20},{20,16},{24,28},{28,24},{1,5},{5... | collective-permute-start | bytes 1769480 | tf_op jit(solution)/shard_map/ppermute | solution.py:331
  3.2 10.3 %collective-permute-start.14 = (bf16[128,2304]{1,0:T(8,128)(2,1)S(1)}, bf16[128,2304]{1,0:T(8,128)(2,1)S(1)}, u32[]{:S(2)}, u32[]{:S(2)}) collective-permute-start(bf16[128,2304]{1,0:T(8,128)(2,1)S(1)} %get-tuple-element.80.refs_2_), channel_id=1, source_target_pairs={{0,8},{4,20},{8,0},{12,28},{16,24},{20,4},{24,16},{28,12},{1,9},{5... | collective-permute-start | bytes 1769480 | tf_op jit(solution)/shard_map/ppermute | solution.py:331
  6.9 3.4 %collective-permute-start.3 = (bf16[128,896]{1,0:T(8,128)(2,1)S(1)}, bf16[128,896]{1,0:T(8,128)(2,1)S(1)}, u32[]{:S(2)}, u32[]{:S(2)}) collective-permute-start(bf16[128,896]{1,0:T(8,128)(2,1)S(1)} %shard_map.264.refs_0_.refs_4_), channel_id=1, source_target_pairs={{0,4},{4,0},{8,12},{12,8},{16,20},{20,16},{24,28},{28,24},{1,5},{5... | collective-permute-start | bytes 688136 | tf_op jit(solution)/shard_map/ppermute | solution.py:331
  7.2 8.8 %collective-permute-start.4 = (bf16[128,896]{1,0:T(8,128)(2,1)S(1)}, bf16[128,896]{1,0:T(8,128)(2,1)S(1)}, u32[]{:S(2)}, u32[]{:S(2)}) collective-permute-start(bf16[128,896]{1,0:T(8,128)(2,1)S(1)} %shard_map.264.refs_0_.refs_4_), channel_id=1, source_target_pairs={{0,8},{4,20},{8,0},{12,28},{16,24},{20,4},{24,16},{28,12},{1,9},{5... | collective-permute-start | bytes 688136 | tf_op jit(solution)/shard_map/ppermute | solution.py:331
  8.7 13.9 %collective-permute-start = (bf16[128,1024]{1,0:T(8,128)(2,1)}, bf16[128,1024]{1,0:T(8,128)(2,1)S(1)}, u32[]{:S(2)}, u32[]{:S(2)}) collective-permute-start(bf16[128,1024]{1,0:T(8,128)(2,1)} %bitcast.31), channel_id=1, source_target_pairs={{0,1},{1,0},{2,3},{3,2},{4,5},{5,4},{6,7},{7,6},{8,9},{9,8},{10,11... | collective-permute-start | bytes 786440 | tf_op jit(solution)/shard_map/ppermute | solution.py:331
  10.3 14.8 %collective-permute-start.1 = (bf16[128,1024]{1,0:T(8,128)(2,1)}, bf16[128,1024]{1,0:T(8,128)(2,1)}, u32[]{:S(2)}, u32[]{:S(2)}) collective-permute-start(bf16[128,1024]{1,0:T(8,128)(2,1)} %bitcast.32), channel_id=1, source_target_pairs={{0,2},{1,3},{2,0},{3,1},{4,6},{5,7},{6,4},{7,5},{8,10},{9,11},{10,... | collective-permute-start | bytes 786440 | tf_op jit(solution)/shard_map/ppermute | solution.py:331
  12.9 27.6 %collective-permute-start.15 = (bf16[128,2304]{1,0:T(8,128)(2,1)S(1)}, bf16[128,2304]{1,0:T(8,128)(2,1)S(1)}, u32[]{:S(2)}, u32[]{:S(2)}) collective-permute-start(bf16[128,2304]{1,0:T(8,128)(2,1)S(1)} %collective-permute-done.13.refs_3_), channel_id=1, source_target_pairs={{0,8},{4,20},{8,0},{12,28},{16,24},{20,4},{24,16},{28,12},{1,9},{5... | collective-permute-start | bytes 1769480 | tf_op jit(solution)/shard_map/ppermute | solution.py:331
  13.5 27.4 %collective-permute-start.18 = (bf16[128,2304]{1,0:T(8,128)(2,1)S(1)}, bf16[128,2304]{1,0:T(8,128)(2,1)S(1)}, u32[]{:S(2)}, u32[]{:S(2)}) collective-permute-start(bf16[128,2304]{1,0:T(8,128)(2,1)S(1)} %collective-permute-done.14.refs_4_), channel_id=1, source_target_pairs={{0,16},{4,12},{8,24},{12,4},{16,0},{20,28},{24,8},{28,20},{1,17},{... | collective-permute-start | bytes 1769480 | tf_op jit(solution)/shard_map/ppermute | solution.py:331
  16.0 17.8 %collective-permute-start.5 = (bf16[128,896]{1,0:T(8,128)(2,1)S(1)}, bf16[128,896]{1,0:T(8,128)(2,1)}, u32[]{:S(2)}, u32[]{:S(2)}) collective-permute-start(bf16[128,896]{1,0:T(8,128)(2,1)S(1)} %collective-permute-done.3.refs_1_.refs_5_), channel_id=1, source_target_pairs={{0,8},{4,20},{8,0},{12,28},{16,24},{20,4},{24,16},{28,12},{1,9},{5... | collective-permute-start | bytes 688136 | tf_op jit(solution)/shard_map/ppermute | solution.py:331
  18.2 0.7 copy-start.4
  22.6 0.7 copy-start
  23.3 10.4 %collective-permute-start.8 = (bf16[128,896]{1,0:T(8,128)(2,1)S(1)}, bf16[128,896]{1,0:T(8,128)(2,1)}, u32[]{:S(2)}, u32[]{:S(2)}) collective-permute-start(bf16[128,896]{1,0:T(8,128)(2,1)S(1)} %collective-permute-done.4.refs_2_.refs_6_), channel_id=1, source_target_pairs={{0,16},{4,12},{8,24},{12,4},{16,0},{20,28},{24,8},{28,20},{1,17},{... | collective-permute-start | bytes 688136 | tf_op jit(solution)/shard_map/ppermute | solution.py:331
  25.1 9.1 %collective-permute-start.7 = (bf16[128,896]{1,0:T(8,128)(2,1)S(1)}, bf16[128,896]{1,0:T(8,128)(2,1)S(1)}, u32[]{:S(2)}, u32[]{:S(2)}) collective-permute-start(bf16[128,896]{1,0:T(8,128)(2,1)S(1)} %collective-permute-done.4.refs_2_.refs_6_), channel_id=1, source_target_pairs={{0,4},{4,0},{8,12},{12,8},{16,20},{20,16},{24,28},{28,24},{1,5},{5... | collective-permute-start | bytes 688136 | tf_op jit(solution)/shard_map/ppermute | solution.py:331
  25.1 0.7 copy-start.6
  33.7 4.2 %collective-permute-start.6 = (bf16[128,896]{1,0:T(8,128)(2,1)}, bf16[128,896]{1,0:T(8,128)(2,1)}, u32[]{:S(2)}, u32[]{:S(2)}) collective-permute-start(bf16[128,896]{1,0:T(8,128)(2,1)} %collective-permute-done.5.refs_3_.refs_7_), channel_id=1, source_target_pairs={{0,4},{4,0},{8,12},{12,8},{16,20},{20,16},{24,28},{28,24},{1,5},{5... | collective-permute-start | bytes 688136 | tf_op jit(solution)/shard_map/ppermute | solution.py:331
  33.7 6.6 %collective-permute-start.9 = (bf16[128,896]{1,0:T(8,128)(2,1)}, bf16[128,896]{1,0:T(8,128)(2,1)}, u32[]{:S(2)}, u32[]{:S(2)}) collective-permute-start(bf16[128,896]{1,0:T(8,128)(2,1)} %collective-permute-done.8.refs_6_.refs_10_), channel_id=1, source_target_pairs={{0,4},{4,0},{8,12},{12,8},{16,20},{20,16},{24,28},{28,24},{1,5},{5... | collective-permute-start | bytes 688136 | tf_op jit(solution)/shard_map/ppermute | solution.py:331
  34.2 0.7 copy-start.9
  34.9 15.5 %collective-permute-start.24 = (bf16[128,1024]{1,0:T(8,128)(2,1)}, bf16[128,1024]{1,0:T(8,128)(2,1)}, u32[]{:S(2)}, u32[]{:S(2)}) collective-permute-start(bf16[128,1024]{1,0:T(8,128)(2,1)} %bitcast.34), channel_id=1, source_target_pairs={{0,2},{1,3},{2,0},{3,1},{4,6},{5,7},{6,4},{7,5},{8,10},{9,11},{10,... | collective-permute-start | bytes 786440 | tf_op jit(solution)/shard_map/ppermute | solution.py:331
  38.0 23.4 %copy-start.1 = (bf16[128,1024]{1,0:T(8,128)(2,1)S(1)}, bf16[128,1024]{1,0:T(8,128)(2,1)}, u32[]{:S(2)}) copy-start(bf16[128,1024]{1,0:T(8,128)(2,1)} %copy-done) | copy-start | bytes 786436
  38.0 13.1 %collective-permute-start.2 = (bf16[128,1024]{1,0:T(8,128)(2,1)}, bf16[128,1024]{1,0:T(8,128)(2,1)S(1)}, u32[]{:S(2)}, u32[]{:S(2)}) collective-permute-start(bf16[128,1024]{1,0:T(8,128)(2,1)} %collective-permute-done.1.refs_2_), channel_id=1, source_target_pairs={{0,1},{1,0},{2,3},{3,2},{4,5},{5,4},{6,7},{7,6},{8,9},{9,8},{10,11... | collective-permute-start | bytes 786440 | tf_op jit(solution)/shard_map/ppermute | solution.py:331
  40.4 29.8 %collective-permute-start.17 = (bf16[128,2304]{1,0:T(8,128)(2,1)S(1)}, bf16[128,2304]{1,0:T(8,128)(2,1)S(1)}, u32[]{:S(2)}, u32[]{:S(2)}) collective-permute-start(bf16[128,2304]{1,0:T(8,128)(2,1)S(1)} %collective-permute-done.14.refs_4_), channel_id=1, source_target_pairs={{0,4},{4,0},{8,12},{12,8},{16,20},{20,16},{24,28},{28,24},{1,5},{5... | collective-permute-start | bytes 1769480 | tf_op jit(solution)/shard_map/ppermute | solution.py:331
  40.5 29.7 %collective-permute-start.16 = (bf16[128,2304]{1,0:T(8,128)(2,1)S(1)}, bf16[128,2304]{1,0:T(8,128)(2,1)S(1)}, u32[]{:S(2)}, u32[]{:S(2)}) collective-permute-start(bf16[128,2304]{1,0:T(8,128)(2,1)S(1)} %collective-permute-done.15.refs_5_), channel_id=1, source_target_pairs={{0,4},{4,0},{8,12},{12,8},{16,20},{20,16},{24,28},{28,24},{1,5},{5... | collective-permute-start | bytes 1769480 | tf_op jit(solution)/shard_map/ppermute | solution.py:331
  40.9 29.2 %collective-permute-start.19 = (bf16[128,2304]{1,0:T(8,128)(2,1)S(1)}, bf16[128,2304]{1,0:T(8,128)(2,1)S(1)}, u32[]{:S(2)}, u32[]{:S(2)}) collective-permute-start(bf16[128,2304]{1,0:T(8,128)(2,1)S(1)} %collective-permute-done.18.refs_8_), channel_id=1, source_target_pairs={{0,4},{4,0},{8,12},{12,8},{16,20},{20,16},{24,28},{28,24},{1,5},{5... | collective-permute-start | bytes 1769480 | tf_op jit(solution)/shard_map/ppermute | solution.py:331
  41.0 0.9 copy-start.5
  42.0 0.9 copy-start.7
  42.9 0.9 copy-start.10
  43.9 17.5 %copy-start.8 = (bf16[128,896]{1,0:T(8,128)(2,1)S(1)}, bf16[128,896]{1,0:T(8,128)(2,1)}, u32[]{:S(2)}) copy-start(bf16[128,896]{1,0:T(8,128)(2,1)} %copy-done.6) | copy-start | bytes 688132
  43.9 17.6 %copy-start.11 = (bf16[128,896]{1,0:T(8,128)(2,1)S(1)}, bf16[128,896]{1,0:T(8,128)(2,1)}, u32[]{:S(2)}) copy-start(bf16[128,896]{1,0:T(8,128)(2,1)} %copy-done.9) | copy-start | bytes 688132
  50.5 4.1 %collective-permute-start.10 = (bf16[8,16,128]{2,1,0:T(8,128)(2,1)S(1)}, bf16[8,16,128]{2,1,0:T(8,128)(2,1)S(1)}, u32[]{:S(2)}, u32[]{:S(2)}) collective-permute-start(bf16[8,16,128]{2,1,0:T(8,128)(2,1)S(1)} %shard_map.265), channel_id=1, source_target_pairs={{0,1},{1,0},{2,3},{3,2},{4,5},{5,4},{6,7},{7,6},{8,9},{9,8},{10,11... | collective-permute-start | bytes 98312 | tf_op jit(solution)/shard_map/ppermute | solution.py:331
  51.1 7.1 %collective-permute-start.11 = (bf16[8,16,128]{2,1,0:T(8,128)(2,1)S(1)}, bf16[8,16,128]{2,1,0:T(8,128)(2,1)S(1)}, u32[]{:S(2)}, u32[]{:S(2)}) collective-permute-start(bf16[8,16,128]{2,1,0:T(8,128)(2,1)S(1)} %shard_map.265), channel_id=1, source_target_pairs={{0,2},{1,3},{2,0},{3,1},{4,6},{5,7},{6,4},{7,5},{8,10},{9,11},{10,... | collective-permute-start | bytes 98312 | tf_op jit(solution)/shard_map/ppermute | solution.py:331
  54.5 5.8 %collective-permute-start.12 = (bf16[8,16,128]{2,1,0:T(8,128)(2,1)S(1)}, bf16[8,16,128]{2,1,0:T(8,128)(2,1)S(1)}, u32[]{:S(2)}, u32[]{:S(2)}) collective-permute-start(bf16[8,16,128]{2,1,0:T(8,128)(2,1)S(1)} %shard_map.265), channel_id=1, source_target_pairs={{0,3},{1,2},{2,1},{3,0},{4,7},{5,6},{6,5},{7,4},{8,11},{9,10},{10,... | collective-permute-start | bytes 98312 | tf_op jit(solution)/shard_map/ppermute | solution.py:331
  58.2 19.2 %collective-permute-start.23 = (bf16[128,1024]{1,0:T(8,128)(2,1)}, bf16[128,1024]{1,0:T(8,128)(2,1)S(1)}, u32[]{:S(2)}, u32[]{:S(2)}) collective-permute-start(bf16[128,1024]{1,0:T(8,128)(2,1)} %bitcast.35), channel_id=1, source_target_pairs={{0,1},{1,0},{2,3},{3,2},{4,5},{5,4},{6,7},{7,6},{8,9},{9,8},{10,11... | collective-permute-start | bytes 786440 | tf_op jit(solution)/shard_map/ppermute | solution.py:331
  60.4 17.0 %collective-permute-start.25 = (bf16[128,1024]{1,0:T(8,128)(2,1)}, bf16[128,1024]{1,0:T(8,128)(2,1)S(1)}, u32[]{:S(2)}, u32[]{:S(2)}) collective-permute-start(bf16[128,1024]{1,0:T(8,128)(2,1)} %collective-permute-done.24.refs_2_), channel_id=1, source_target_pairs={{0,1},{1,0},{2,3},{3,2},{4,5},{5,4},{6,7},{7,6},{8,9},{9,8},{10,11... | collective-permute-start | bytes 786440 | tf_op jit(solution)/shard_map/ppermute | solution.py:331
  74.4 3.0 %copy-start.3 = (bf16[128,1024]{1,0:T(8,128)(2,1)S(1)}, bf16[128,1024]{1,0:T(8,128)(2,1)}, u32[]{:S(2)}) copy-start(bf16[128,1024]{1,0:T(8,128)(2,1)} %copy-done.2) | copy-start | bytes 786436
  83.9 9.3 %collective-permute-start.42 = (bf16[4,128,2304]{2,1,0:T(8,128)(2,1)S(1)}, bf16[4,128,2304]{2,1,0:T(8,128)(2,1)S(1)}, u32[]{:S(2)}, u32[]{:S(2)}) collective-permute-start(bf16[4,128,2304]{2,1,0:T(8,128)(2,1)S(1)} %get-tuple-element.122), channel_id=1, source_target_pairs={{0,4},{4,0},{8,12},{12,8},{16,20},{20,16},{24,28},{28,24},{1,5},{5... | collective-permute-start | bytes 7077896 | tf_op jit(solution)/shard_map/ppermute | solution.py:331
  92.6 46.1 %collective-permute-start.29 = (bf16[4,128,768]{2,1,0:T(8,128)(2,1)S(1)}, bf16[4,128,768]{2,1,0:T(8,128)(2,1)S(1)}, u32[]{:S(2)}, u32[]{:S(2)}) collective-permute-start(bf16[4,128,768]{2,1,0:T(8,128)(2,1)S(1)} %get-tuple-element.105), channel_id=1, source_target_pairs={{0,4},{4,0},{8,12},{12,8},{16,20},{20,16},{24,28},{28,24},{1,5},{5... | collective-permute-start | bytes 2359304 | tf_op jit(solution)/shard_map/ppermute | solution.py:331
  93.7 44.3 %collective-permute-start.43 = (bf16[128,2304]{1,0:T(8,128)(2,1)S(1)}, bf16[128,2304]{1,0:T(8,128)(2,1)S(1)}, u32[]{:S(2)}, u32[]{:S(2)}) collective-permute-start(bf16[128,2304]{1,0:T(8,128)(2,1)S(1)} %get-tuple-element.125), channel_id=1, source_target_pairs={{0,16},{4,12},{8,24},{12,4},{16,0},{20,28},{24,8},{28,20},{1,17},{... | collective-permute-start | bytes 1769480 | tf_op jit(solution)/shard_map/ppermute | solution.py:331
  95.3 44.1 %collective-permute-start.45 = (bf16[128,2304]{1,0:T(8,128)(2,1)S(1)}, bf16[128,2304]{1,0:T(8,128)(2,1)S(1)}, u32[]{:S(2)}, u32[]{:S(2)}) collective-permute-start(bf16[128,2304]{1,0:T(8,128)(2,1)S(1)} %get-tuple-element.126), channel_id=1, source_target_pairs={{0,8},{4,20},{8,0},{12,28},{16,24},{20,4},{24,16},{28,12},{1,9},{5... | collective-permute-start | bytes 1769480 | tf_op jit(solution)/shard_map/ppermute | solution.py:331
  96.8 37.7 %collective-permute-start.20 = (bf16[128,1024]{1,0:T(8,128)(2,1)S(1)}, bf16[128,1024]{1,0:T(8,128)(2,1)S(1)}, u32[]{:S(2)}, u32[]{:S(2)}) collective-permute-start(bf16[128,1024]{1,0:T(8,128)(2,1)S(1)} %get-tuple-element.84), channel_id=1, source_target_pairs={{0,1},{1,0},{2,3},{3,2},{4,5},{5,4},{6,7},{7,6},{8,9},{9,8},{10,11... | collective-permute-start | bytes 786440 | tf_op jit(solution)/shard_map/ppermute | solution.py:331
  105.3 4.0 %collective-permute-start.34 = (f32[8,1024]{1,0:T(8,128)S(1)}, f32[8,1024]{1,0:T(8,128)S(1)}, u32[]{:S(2)}, u32[]{:S(2)}) collective-permute-start(f32[8,1024]{1,0:T(8,128)S(1)} %get-tuple-element.113.refs_0_), channel_id=1, source_target_pairs={{0,1},{1,0},{2,3},{3,2},{4,5},{5,4},{6,7},{7,6},{8,9},{9,8},{10,11... | collective-permute-start | bytes 98312 | tf_op jit(solution)/shard_map/ppermute | solution.py:331
  109.2 4.8 %collective-permute-start.35 = (f32[8,1024]{1,0:T(8,128)S(1)}, f32[8,1024]{1,0:T(8,128)S(1)}, u32[]{:S(2)}, u32[]{:S(2)}) collective-permute-start(f32[8,1024]{1,0:T(8,128)S(1)} %get-tuple-element.113.refs_0_), channel_id=1, source_target_pairs={{0,2},{1,3},{2,0},{3,1},{4,6},{5,7},{6,4},{7,5},{8,10},{9,11},{10,... | collective-permute-start | bytes 98312 | tf_op jit(solution)/shard_map/ppermute | solution.py:331
  114.0 6.0 %collective-permute-start.36 = (f32[8,1024]{1,0:T(8,128)S(1)}, f32[8,1024]{1,0:T(8,128)S(1)}, u32[]{:S(2)}, u32[]{:S(2)}) collective-permute-start(f32[8,1024]{1,0:T(8,128)S(1)} %get-tuple-element.113.refs_0_), channel_id=1, source_target_pairs={{0,3},{1,2},{2,1},{3,0},{4,7},{5,6},{6,5},{7,4},{8,11},{9,10},{10,... | collective-permute-start | bytes 98312 | tf_op jit(solution)/shard_map/ppermute | solution.py:331
  120.6 1.3 collective-permute-start.37
  121.9 3.7 %collective-permute-start.38 = (bf16[32,128]{1,0:T(8,128)(2,1)S(1)}, bf16[32,128]{1,0:T(8,128)(2,1)S(1)}, u32[]{:S(2)}, u32[]{:S(2)}) collective-permute-start(bf16[32,128]{1,0:T(8,128)(2,1)S(1)} %get-tuple-element.118), channel_id=1, source_target_pairs={{0,16},{4,12},{8,24},{12,4},{16,0},{20,28},{24,8},{28,20},{1,17},{... | collective-permute-start | bytes 24584 | tf_op jit(solution)/shard_map/ppermute | solution.py:331
  125.6 3.7 %collective-permute-start.40 = (bf16[32,128]{1,0:T(8,128)(2,1)S(1)}, bf16[32,128]{1,0:T(8,128)(2,1)S(1)}, u32[]{:S(2)}, u32[]{:S(2)}) collective-permute-start(bf16[32,128]{1,0:T(8,128)(2,1)S(1)} %get-tuple-element.119), channel_id=1, source_target_pairs={{0,8},{4,20},{8,0},{12,28},{16,24},{20,4},{24,16},{28,12},{1,9},{5... | collective-permute-start | bytes 24584 | tf_op jit(solution)/shard_map/ppermute | solution.py:331
  129.3 3.7 %collective-permute-start.39 = (bf16[32,128]{1,0:T(8,128)(2,1)S(1)}, bf16[32,128]{1,0:T(8,128)(2,1)S(1)}, u32[]{:S(2)}, u32[]{:S(2)}) collective-permute-start(bf16[32,128]{1,0:T(8,128)(2,1)S(1)} %shard_map.282), channel_id=1, source_target_pairs={{0,8},{4,20},{8,0},{12,28},{16,24},{20,4},{24,16},{28,12},{1,9},{5... | collective-permute-start | bytes 24584 | tf_op jit(solution)/shard_map/ppermute | solution.py:331
  132.9 1.2 collective-permute-start.41
  134.1 21.4 %collective-permute-start.21 = (bf16[128,1024]{1,0:T(8,128)(2,1)S(1)}, bf16[128,1024]{1,0:T(8,128)(2,1)S(1)}, u32[]{:S(2)}, u32[]{:S(2)}) collective-permute-start(bf16[128,1024]{1,0:T(8,128)(2,1)S(1)} %get-tuple-element.85), channel_id=1, source_target_pairs={{0,2},{1,3},{2,0},{3,1},{4,6},{5,7},{6,4},{7,5},{8,10},{9,11},{10,... | collective-permute-start | bytes 786440 | tf_op jit(solution)/shard_map/ppermute | solution.py:331
  134.5 21.5 %collective-permute-start.22 = (bf16[128,1024]{1,0:T(8,128)(2,1)S(1)}, bf16[128,1024]{1,0:T(8,128)(2,1)S(1)}, u32[]{:S(2)}, u32[]{:S(2)}) collective-permute-start(bf16[128,1024]{1,0:T(8,128)(2,1)S(1)} %get-tuple-element.86), channel_id=1, source_target_pairs={{0,3},{1,2},{2,1},{3,0},{4,7},{5,6},{6,5},{7,4},{8,11},{9,10},{10,... | collective-permute-start | bytes 786440 | tf_op jit(solution)/shard_map/ppermute | solution.py:331
  138.0 22.9 %collective-permute-start.27 = (bf16[128,1024]{1,0:T(8,128)(2,1)S(1)}, bf16[128,1024]{1,0:T(8,128)(2,1)S(1)}, u32[]{:S(2)}, u32[]{:S(2)}) collective-permute-start(bf16[128,1024]{1,0:T(8,128)(2,1)S(1)} %get-tuple-element.102), channel_id=1, source_target_pairs={{0,1},{1,0},{2,3},{3,2},{4,5},{5,4},{6,7},{7,6},{8,9},{9,8},{10,11... | collective-permute-start | bytes 786440 | tf_op jit(solution)/shard_map/ppermute | solution.py:331
  138.7 39.6 %collective-permute-start.44 = (bf16[128,2304]{1,0:T(8,128)(2,1)S(1)}, bf16[128,2304]{1,0:T(8,128)(2,1)S(1)}, u32[]{:S(2)}, u32[]{:S(2)}) collective-permute-start(bf16[128,2304]{1,0:T(8,128)(2,1)S(1)} %shard_map.285), channel_id=1, source_target_pairs={{0,8},{4,20},{8,0},{12,28},{16,24},{20,4},{24,16},{28,12},{1,9},{5... | collective-permute-start | bytes 1769480 | tf_op jit(solution)/shard_map/ppermute | solution.py:331
  139.4 38.9 %collective-permute-start.46 = (bf16[128,2304]{1,0:T(8,128)(2,1)S(1)}, bf16[128,2304]{1,0:T(8,128)(2,1)S(1)}, u32[]{:S(2)}, u32[]{:S(2)}) collective-permute-start(bf16[128,2304]{1,0:T(8,128)(2,1)S(1)} %collective-permute-done.45), channel_id=1, source_target_pairs={{0,4},{4,0},{8,12},{12,8},{16,20},{20,16},{24,28},{28,24},{1,5},{5... | collective-permute-start | bytes 1769480 | tf_op jit(solution)/shard_map/ppermute | solution.py:331
  155.5 6.0 %collective-permute-start.30 = (bf16[128,768]{1,0:T(8,128)(2,1)S(1)}, bf16[128,768]{1,0:T(8,128)(2,1)S(1)}, u32[]{:S(2)}, u32[]{:S(2)}) collective-permute-start(bf16[128,768]{1,0:T(8,128)(2,1)S(1)} %get-tuple-element.108), channel_id=1, source_target_pairs={{0,16},{4,12},{8,24},{12,4},{16,0},{20,28},{24,8},{28,20},{1,17},{... | collective-permute-start | bytes 589832 | tf_op jit(solution)/shard_map/ppermute | solution.py:331
  156.0 15.3 %collective-permute-start.26 = (bf16[128,1024]{1,0:T(8,128)(2,1)S(1)}, bf16[128,1024]{1,0:T(8,128)(2,1)S(1)}, u32[]{:S(2)}, u32[]{:S(2)}) collective-permute-start(bf16[128,1024]{1,0:T(8,128)(2,1)S(1)} %get-tuple-element.100), channel_id=1, source_target_pairs={{0,1},{1,0},{2,3},{3,2},{4,5},{5,4},{6,7},{7,6},{8,9},{9,8},{10,11... | collective-permute-start | bytes 786440 | tf_op jit(solution)/shard_map/ppermute | solution.py:331
  160.9 10.6 %collective-permute-start.32 = (bf16[128,768]{1,0:T(8,128)(2,1)S(1)}, bf16[128,768]{1,0:T(8,128)(2,1)S(1)}, u32[]{:S(2)}, u32[]{:S(2)}) collective-permute-start(bf16[128,768]{1,0:T(8,128)(2,1)S(1)} %get-tuple-element.109), channel_id=1, source_target_pairs={{0,8},{4,20},{8,0},{12,28},{16,24},{20,4},{24,16},{28,12},{1,9},{5... | collective-permute-start | bytes 589832 | tf_op jit(solution)/shard_map/ppermute | solution.py:331
  161.5 13.5 %collective-permute-start.28 = (bf16[128,1024]{1,0:T(8,128)(2,1)S(1)}, bf16[128,1024]{1,0:T(8,128)(2,1)S(1)}, u32[]{:S(2)}, u32[]{:S(2)}) collective-permute-start(bf16[128,1024]{1,0:T(8,128)(2,1)S(1)} %shard_map.274), channel_id=1, source_target_pairs={{0,2},{1,3},{2,0},{3,1},{4,6},{5,7},{6,4},{7,5},{8,10},{9,11},{10,... | collective-permute-start | bytes 786440 | tf_op jit(solution)/shard_map/ppermute | solution.py:331
  171.3 5.7 %collective-permute-start.31 = (bf16[128,768]{1,0:T(8,128)(2,1)S(1)}, bf16[128,768]{1,0:T(8,128)(2,1)S(1)}, u32[]{:S(2)}, u32[]{:S(2)}) collective-permute-start(bf16[128,768]{1,0:T(8,128)(2,1)S(1)} %shard_map.278), channel_id=1, source_target_pairs={{0,8},{4,20},{8,0},{12,28},{16,24},{20,4},{24,16},{28,12},{1,9},{5... | collective-permute-start | bytes 589832 | tf_op jit(solution)/shard_map/ppermute | solution.py:331
  171.5 5.4 %collective-permute-start.33 = (bf16[128,768]{1,0:T(8,128)(2,1)S(1)}, bf16[128,768]{1,0:T(8,128)(2,1)S(1)}, u32[]{:S(2)}, u32[]{:S(2)}) collective-permute-start(bf16[128,768]{1,0:T(8,128)(2,1)S(1)} %collective-permute-done.32), channel_id=1, source_target_pairs={{0,4},{4,0},{8,12},{12,8},{16,20},{20,16},{24,28},{28,24},{1,5},{5... | collective-permute-start | bytes 589832 | tf_op jit(solution)/shard_map/ppermute | solution.py:331
  175.0 4.9 %copy-start.12 = (f32[32]{0:T(128)S(1)}, f32[32]{0:T(128)}, u32[]{:S(2)}) copy-start(f32[32]{0:T(128)} %get-tuple-element.168) | copy-start | bytes 388
